TPU v7x, 32 devices: a whole 2x2x4 slice. The times are simulated.
32 devices in a mesh: head: 2 (over x), ctx: 16 (over z, y, core).
Axes of the slice: x: 2, y: 2, z: 4, core: 2. Of those that a mesh axis runs over, the one named last changes fastest.
Arguments:
- queries: bfloat16 [8192, 8192], P(('ctx', 'head')), may hold values from -6 to 6
- unrotated_keys: bfloat16 [8192, 1024], P(('ctx', 'head')), may hold values from -6 to 6
- value_rows: bfloat16 [8192, 1024], P(('ctx', 'head')), may hold values from -6 to 6
- outputs: bfloat16 [8192, 8192], P(('ctx', 'head')), may hold values from -6 to 6
- output_gradient: bfloat16 [8192, 8192], P(('ctx', 'head')), may hold values from -6 to 6
- saved_logsumexp: float32 [64, 8192], P(None, ('ctx', 'head')), may hold values from 4 to 6
- ancestors: int32 [16, 1], replicated, may hold values from -1 to 14, as said below
- placement: int32 [16], replicated, may hold values from 0 to 15, as said below
- positions: int32 [8192], P(('ctx', 'head')), may hold values from 0 to 8191, as said below
Outputs:
- grad_queries: bfloat16 [8192, 8192], P(('ctx', 'head'))
- grad_keys: bfloat16 [8192, 1024], P(('ctx', 'head'))
- grad_values: bfloat16 [8192, 1024], P(('ctx', 'head'))
Inputs may be any that keep to these rules, and one draw needn't show every extreme that they name: Each logical block b > 0 has one parent among blocks max(0, b - 4) to b - 1; entry k of ancestors[b] is b's (k + 1)-th ancestor, -1 above the root block 0; block 15 has parent 16 - 2. `placement`: A permutation of the 16 logical blocks. `positions`: A token's position is 512 times the number of its logical block plus its offset in its block.
All inputs are finite; a program needn't handle non-finite values.
Results may differ from a plain program's by a relative error of at most 0.023.
Values may be sent and summed in bfloat16 or wider, within the bound.
No kernel may reach another device: no remote copies, remote signals or barrier semaphores. Data moves between devices by JAX's collectives and lax.ppermute only.
A program may use at most 256 MiB of HBM per device.

v0:
```python
import functools
import math

import jax
import jax.numpy as jnp
from jax import lax
from jax.experimental import pallas as pl
from jax.experimental.pallas import tpu as pltpu
from jax.sharding import PartitionSpec as P


HEAD_SIZE = 128
TREE_BLOCK = 512
LOG2E = math.log2(math.e)
LN2 = math.log(2.0)
SCALE = 1.0 / math.sqrt(HEAD_SIZE)
rope_base = 500000.0
VMEM_LIMIT = 60 * 1024 * 1024
NT = (((1,), (1,)), ((), ()))
NN = (((1,), (0,)), ((), ()))
TN = (((0,), (0,)), ((), ()))


def rope_tables(positions):
    half_dim = HEAD_SIZE // 2
    freq_index = jnp.arange(half_dim, dtype=jnp.float32)
    inverse = rope_base ** (-(2.0 * freq_index / HEAD_SIZE))
    angles = positions.astype(jnp.float32)[:, None] * inverse[None, :]
    c, s = jnp.cos(angles), jnp.sin(angles)
    return jnp.concatenate([c, c], -1), jnp.concatenate([-s, s], -1)


def dot(a, b, dims):
    return lax.dot_general(a, b, dims, preferred_element_type=jnp.float32)


def turn(x, c, s):
    return x * c + pltpu.roll(x, HEAD_SIZE // 2, 1) * s


def turn_back(x, c, s):
    return x * c - pltpu.roll(x, HEAD_SIZE // 2, 1) * s


def params(n=1):
    return pltpu.CompilerParams(
        dimension_semantics=("arbitrary",) * n, vmem_limit_bytes=VMEM_LIMIT
    )


def pack_kernel(sizes, k_ref, v_ref, c_ref, s_ref, *o_refs):
    c, s = c_ref[...], s_ref[...]
    g = 0
    for size, o_ref in zip(sizes, o_refs):
        for i in range(size):
            a, b = g * HEAD_SIZE, 2 * i * HEAD_SIZE
            x = k_ref[:, a : a + HEAD_SIZE].astype(jnp.float32)
            o_ref[:, b : b + HEAD_SIZE] = turn(x, c, s).astype(jnp.bfloat16)
            o_ref[:, b + HEAD_SIZE : b + 2 * HEAD_SIZE] = v_ref[:, a : a + HEAD_SIZE]
            g += 1


def pack(sizes, keys, values, c, s):
    rows = keys.shape[0]
    return pl.pallas_call(
        functools.partial(pack_kernel, sizes),
        out_shape=[
            jax.ShapeDtypeStruct((rows, 2 * size * HEAD_SIZE), jnp.bfloat16) for size in sizes
        ],
        compiler_params=params(0),
        name="pack",
    )(keys, values, c, s)


def pick_kernel(source_ref, x_ref, o_ref):
    for d in range(x_ref.shape[0]):
        o_ref[d] = x_ref[source_ref[d]]


def pick(source, x):
    return pl.pallas_call(
        pick_kernel,
        out_shape=jax.ShapeDtypeStruct(x.shape, x.dtype),
        in_specs=[
            pl.BlockSpec(memory_space=pltpu.SMEM),
            pl.BlockSpec(memory_space=pltpu.VMEM),
        ],
        out_specs=pl.BlockSpec(memory_space=pltpu.VMEM),
        compiler_params=params(0),
        name="pick",
    )(source, x)


def merge_kernel(source_ref, present_ref, x_ref, o_ref, acc_ref):
    acc_ref[...] = jnp.zeros_like(acc_ref)
    for d in range(x_ref.shape[0]):

        @pl.when(present_ref[d] != 0)
        def _():
            acc_ref[source_ref[d]] += x_ref[d].astype(jnp.float32)

    o_ref[...] = acc_ref[...].astype(o_ref.dtype)


def merge(source, present, x):
    return pl.pallas_call(
        merge_kernel,
        out_shape=jax.ShapeDtypeStruct(x.shape, x.dtype),
        in_specs=[
            pl.BlockSpec(memory_space=pltpu.SMEM),
            pl.BlockSpec(memory_space=pltpu.SMEM),
            pl.BlockSpec(memory_space=pltpu.VMEM),
        ],
        out_specs=pl.BlockSpec(memory_space=pltpu.VMEM),
        scratch_shapes=[pltpu.VMEM(x.shape, jnp.float32)],
        compiler_params=params(0),
        name="merge",
    )(source, present, x)


def fronts(rq, do, lse, delta, k, v, mask=None):
    prob = jnp.exp2(dot(k, rq, NT) - lse)
    if mask is not None:
        prob = jnp.where(mask, prob, 0.0)
    grad_score = prob * (dot(v, do, NT) - delta)
    return prob.astype(jnp.bfloat16), grad_score.astype(jnp.bfloat16)


def stacked(ref, group):
    return jnp.concatenate([ref[:, cols_of(h)] for h in range(group)], 0)


def heads_of(width, kv_count):
    return width // HEAD_SIZE // kv_count


def cols_of(h):
    return slice(h * HEAD_SIZE, (h + 1) * HEAD_SIZE)


def diagonal_kernel(group, q_ref, do_ref, out_ref, lse_ref, c_ref, s_ref, kv_ref, rq_ref, delta_ref, dq_ref, dkv_ref, p_ref, ds_ref):
    rows = q_ref.shape[0]
    c, s = c_ref[...] * (SCALE * LOG2E), s_ref[...] * (SCALE * LOG2E)
    key_at = lax.broadcasted_iota(jnp.int32, (rows, rows), 0)
    query_at = lax.broadcasted_iota(jnp.int32, (rows, rows), 1)
    causal = key_at <= query_at
    k = kv_ref[:, :HEAD_SIZE]
    v = kv_ref[:, HEAD_SIZE:]
    for h in range(group):
        cols, lanes = cols_of(h), slice(h * rows, (h + 1) * rows)
        do = do_ref[:, cols]
        rq = turn(q_ref[:, cols].astype(jnp.float32), c, s).astype(jnp.bfloat16)
        rq_ref[:, cols] = rq
        product = do.astype(jnp.float32) * out_ref[:, cols].astype(jnp.float32)
        delta = jnp.sum(product.T, axis=0, keepdims=True)
        delta_ref[h : h + 1, :] = delta
        p_ref[:, lanes], ds_ref[:, lanes] = fronts(
            rq, do, lse_ref[h : h + 1, :] * LOG2E, delta, k, v, causal
        )
    dkv_ref[:, :HEAD_SIZE] = dot(ds_ref[...], stacked(rq_ref, group), NN) * LN2
    dkv_ref[:, HEAD_SIZE:] = dot(p_ref[...], stacked(do_ref, group), NN)
    for h in range(group):
        dq_ref[:, cols_of(h)] = dot(ds_ref[:, h * rows : (h + 1) * rows], k, TN)


def diagonal(first, count, kv_count, q, do, out, lse, c, s, kv):
    rows, width = q.shape
    group = heads_of(width, kv_count)
    wide = group * HEAD_SIZE
    big = pl.BlockSpec((rows, wide), lambda g: (0, g + first))
    row = pl.BlockSpec((group, rows), lambda g: (g + first, 0))
    table = pl.BlockSpec((rows, HEAD_SIZE), lambda g: (0, 0))
    pair = pl.BlockSpec((rows, 2 * HEAD_SIZE), lambda g: (0, g))
    part = pl.BlockSpec((rows, wide), lambda g: (0, g))
    part_row = pl.BlockSpec((group, rows), lambda g: (g, 0))
    return pl.pallas_call(
        functools.partial(diagonal_kernel, group),
        out_shape=[
            jax.ShapeDtypeStruct((rows, count * wide), jnp.bfloat16),
            jax.ShapeDtypeStruct((count * group, rows), jnp.float32),
            jax.ShapeDtypeStruct((rows, count * wide), jnp.float32),
            jax.ShapeDtypeStruct((rows, count * 2 * HEAD_SIZE), jnp.float32),
        ],
        grid=(count,),
        in_specs=[big, big, big, row, table, table, pair],
        out_specs=[part, part_row, part, pair],
        scratch_shapes=[pltpu.VMEM((rows, group * rows), jnp.bfloat16)] * 2,
        compiler_params=params(),
        cost_estimate=pl.CostEstimate(
            flops=20 * count * group * rows * rows * HEAD_SIZE,
            bytes_accessed=rows * count * wide * 12,
            transcendentals=0,
        ),
        name="diagonal",
    )(q, do, out, lse, c, s, kv)


def cross_kernel(group, joint, final, flag_ref, rq_ref, do_ref, lse_ref, delta_ref, c_ref, s_ref, dq_in_ref, *refs):
    sets = len(joint)
    refs = list(refs)
    kv_refs = [refs.pop(0) for _ in range(sum(joint))]
    if final == 2:
        refs.pop(0)
    dq_ref = refs.pop(0)
    dkv_refs = [refs.pop(0) for _ in range(sum(joint))]
    p_ref, ds_ref, k_ref, v_ref = refs[:4]
    total_ref = refs[4] if final else dq_ref
    rows = rq_ref.shape[0]
    c, s = c_ref[...] * SCALE, s_ref[...] * SCALE

    def put(cols, total):
        if final and sets == 1:
            dq_ref[:, cols] = turn_back(total, c, s).astype(jnp.bfloat16)
        else:
            total_ref[:, cols] = total

    def run(members, fresh):
        here = slice(0, len(members) * rows)
        for n, m in enumerate(members):
            k_ref[n * rows : (n + 1) * rows] = kv_refs[m][:, :HEAD_SIZE]
            v_ref[n * rows : (n + 1) * rows] = kv_refs[m][:, HEAD_SIZE:]
        k = k_ref[here]
        for h in range(group):
            lanes = slice(h * rows, (h + 1) * rows)
            p_ref[here, lanes], ds_ref[here, lanes] = fronts(
                rq_ref[:, cols_of(h)],
                do_ref[:, cols_of(h)],
                lse_ref[h : h + 1, :] * LOG2E,
                delta_ref[h : h + 1, :],
                k,
                v_ref[here],
            )
        gk = dot(ds_ref[here], stacked(rq_ref, group), NN) * LN2
        gv = dot(p_ref[here], stacked(do_ref, group), NN)
        for n, m in enumerate(members):
            own = slice(n * rows, (n + 1) * rows)
            dkv_refs[m][:, :HEAD_SIZE] = gk[own].astype(jnp.bfloat16)
            dkv_refs[m][:, HEAD_SIZE:] = gv[own].astype(jnp.bfloat16)
        for h in range(group):
            cols = cols_of(h)
            before = dq_in_ref[:, cols] if fresh else total_ref[:, cols]
            put(cols, before + dot(ds_ref[here, h * rows : (h + 1) * rows], k, TN))

    def skip(members, fresh):
        if fresh:
            for h in range(group):
                put(cols_of(h), dq_in_ref[:, cols_of(h)])
        for m in members:
            dkv_refs[m][...] = jnp.zeros_like(dkv_refs[m])

    start = 0
    for i, size in enumerate(joint):
        members = tuple(range(start, start + size))
        start += size
        pl.when(flag_ref[i] != 0)(functools.partial(run, members, i == 0))
        pl.when(flag_ref[i] == 0)(functools.partial(skip, members, i == 0))
    if final and sets > 1:
        for h in range(group):
            cols = cols_of(h)
            dq_ref[:, cols] = turn_back(total_ref[:, cols], c, s).astype(jnp.bfloat16)


def cross(first, count, kv_count, flags, joint, rq, do, lse, delta, c, s, dq, kvs, whole=None, final=False):
    rows, width = do.shape
    group = heads_of(width, kv_count)
    wide = group * HEAD_SIZE
    most = max(joint)
    big = pl.BlockSpec((rows, wide), lambda g, i: (0, g + first))
    row = pl.BlockSpec((group, rows), lambda g, i: (g + first, 0))
    table = pl.BlockSpec((rows, HEAD_SIZE), lambda g, i: (0, 0))
    pair = pl.BlockSpec((rows, 2 * HEAD_SIZE), lambda g, i: (0, g))
    part = pl.BlockSpec((rows, wide), lambda g, i: (0, g))
    part_row = pl.BlockSpec((group, rows), lambda g, i: (g, 0))
    args = [flags, rq, do, lse, delta, c, s, dq, *kvs]
    in_specs = [part, big, row, part_row, table, table, part] + [pair] * len(kvs)
    mode = 0
    aliases = {}
    if final:
        mode = 1
        if whole is not None:
            mode = 2
            aliases = {len(args): 0}
            args.append(whole)
            in_specs.append(pl.BlockSpec(memory_space=pl.ANY))
    dq_shape = (
        jax.ShapeDtypeStruct((rows, width), jnp.bfloat16)
        if final
        else jax.ShapeDtypeStruct(dq.shape, jnp.float32)
    )
    return pl.pallas_call(
        functools.partial(cross_kernel, group, joint, mode),
        out_shape=[dq_shape] + [jax.ShapeDtypeStruct(kvs[0].shape, jnp.bfloat16)] * len(kvs),
        grid_spec=pltpu.PrefetchScalarGridSpec(
            num_scalar_prefetch=1,
            grid=(count,),
            in_specs=in_specs,
            out_specs=[big if final else part] + [pair] * len(kvs),
            scratch_shapes=[pltpu.VMEM((most * rows, group * rows), jnp.bfloat16)] * 2
            + [pltpu.VMEM((most * rows, HEAD_SIZE), jnp.bfloat16)] * 2
            + ([pltpu.VMEM((rows, wide), jnp.float32)] if final else []),
        ),
        input_output_aliases=aliases,
        compiler_params=params(),
        cost_estimate=pl.CostEstimate(
            flops=20 * count * group * rows * rows * HEAD_SIZE * len(kvs),
            bytes_accessed=rows * count * wide * 12,
            transcendentals=0,
        ),
        name="cross",
    )(*args)


def finish_kernel(sizes, parts, c_ref, s_ref, *refs):
    refs = list(refs)
    dk_ref, dv_ref = refs[-2:]
    c, s = c_ref[...], s_ref[...]
    g = 0
    for size in sizes:
        in_refs = [refs.pop(0) for _ in range(parts)]
        for i in range(size):
            a, b = g * HEAD_SIZE, 2 * i * HEAD_SIZE
            total = in_refs[0][:, b : b + 2 * HEAD_SIZE]
            for ref in in_refs[1:]:
                total = total + ref[:, b : b + 2 * HEAD_SIZE].astype(jnp.float32)
            gk = total[:, :HEAD_SIZE]
            dk_ref[:, a : a + HEAD_SIZE] = turn_back(gk, c, s).astype(jnp.bfloat16)
            dv_ref[:, a : a + HEAD_SIZE] = total[:, HEAD_SIZE:].astype(jnp.bfloat16)
            g += 1


def finish(sizes, chunks, c, s):
    rows = chunks[0][0].shape[0]
    width = sum(sizes) * HEAD_SIZE
    return pl.pallas_call(
        functools.partial(finish_kernel, sizes, len(chunks[0])),
        out_shape=[jax.ShapeDtypeStruct((rows, width), jnp.bfloat16)] * 2,
        compiler_params=params(0),
        name="finish",
    )(c, s, *[x for chunk in chunks for x in chunk])


def body(
    queries,
    unrotated_keys,
    value_rows,
    outputs,
    output_gradient,
    saved_logsumexp,
    ancestors,
    placement,
    positions,
):
    hops = lax.axis_size("head")
    places = lax.axis_size("ctx")
    here = lax.axis_index("ctx")
    me = lax.axis_index("head")
    rows = queries.shape[0]
    assert rows * hops == TREE_BLOCK and placement.shape[0] == places
    c, s = rope_tables(positions)

    match = ancestors[placement][:, :1] == placement[None, :]
    source = jnp.argmax(match, axis=1).astype(jnp.int32)
    present = jnp.any(match, axis=1).astype(jnp.int32)

    kv_count = unrotated_keys.shape[1] // HEAD_SIZE
    sizes = split(kv_count)
    chunks = range(len(sizes))
    firsts = [sum(sizes[:g]) for g in chunks]

    def exchange(x):
        width = x.shape[-1]
        return lax.all_to_all(
            x.reshape(places, rows // places, width), "ctx", 0, 0, tiled=True
        )

    def shift(x, n, wrap):
        route = [(i, (i + n) % hops) for i in range(hops) if wrap or 0 <= i + n < hops]
        return lax.ppermute(x, "head", route)

    kv = pack(sizes, unrotated_keys, value_rows, c, s)
    own_flags = jnp.stack([(me >= n).astype(jnp.int32) for n in range(1, hops)])
    parent_flag = present[here][None]
    own_sets, parent_sets = (1,) * (hops - 1), (hops,)

    grad_queries = None
    own_dkv, children, fetched = [], [], []
    for g in chunks:
        send = kv[g]
        if g:
            send, fetched[g - 1] = lax.optimization_barrier((send, fetched[g - 1]))
        middle = exchange(send)
        picked = pick(source, middle)
        fetched.append(exchange(picked))
    for g in chunks:
        own_kv = [shift(kv[g], n, False) for n in range(1, hops)]
        rq, delta, dq, local = diagonal(
            firsts[g], sizes[g], kv_count, queries, output_gradient, outputs,
            saved_logsumexp, c, s, kv[g],
        )
        near = fetched[g].reshape(rows, -1)
        parent_kv = [near] + [shift(near, n, True) for n in range(1, hops)]
        dq, *own_part = cross(
            firsts[g], sizes[g], kv_count, own_flags, own_sets, rq, output_gradient,
            saved_logsumexp, delta, c, s, dq, own_kv,
        )
        back = [shift(own_part[n - 1], -n, False) for n in range(1, hops)]
        own_dkv.append([local] + back)
        grad_queries, *part = cross(
            firsts[g], sizes[g], kv_count, parent_flag, parent_sets, rq, output_gradient,
            saved_logsumexp, delta, c, s, dq, parent_kv, grad_queries, True,
        )
        far_part = [shift(part[n], -n, True) for n in range(1, hops)]
        total = part[0].astype(jnp.float32)
        for x in far_part:
            total = total + x.astype(jnp.float32)
        send = total.astype(jnp.bfloat16)
        if g:
            send, children[g - 1] = lax.optimization_barrier((send, children[g - 1]))
        else:
            send, fetched[-1] = lax.optimization_barrier((send, fetched[-1]))
        up = exchange(send)
        merged = merge(source, present, up)
        children.append(exchange(merged))
    grad_keys, grad_values = finish(
        sizes, [own_dkv[g] + [children[g].reshape(rows, -1)] for g in chunks], c, s
    )
    return (grad_queries, grad_keys, grad_values)


def split(kv_count):
    return (kv_count // 2, kv_count - kv_count // 2)


def solution(mesh):
    return jax.shard_map(
        body,
        mesh=mesh,
        in_specs=(
            P(("ctx", "head"), None),
            P(("ctx", "head"), None),
            P(("ctx", "head"), None),
            P(("ctx", "head"), None),
            P(("ctx", "head"), None),
            P(None, ("ctx", "head")),
            P(),
            P(),
            P(("ctx", "head")),
        ),
        out_specs=(P(("ctx", "head"), None), P(("ctx", "head"), None), P(("ctx", "head"), None)),
        check_vma=False,
    )
```

profile of v0, /device:TPU:0, one launch (start us, length us, event | category | flops | bytes accessed | tf_op | source)
XLA Modules:
  0.0 243.1 jit_solution(122398038665574463)
XLA Ops:
  2.7 2.5 %pack.1 = (bf16[256,1024]{1,0:T(8,128)(2,1)}, bf16[256,1024]{1,0:T(8,128)(2,1)}) custom-call(bf16[256,1024]{1,0:T(8,128)(2,1)} %k_ref.1, bf16[256,1024]{1,0:T(8,128)(2,1)} %v_ref.1, f32[256,128]{1,0:T(8,128)} %get-tuple-element.64.c_ref, f32[256,128]{1,0:T(8,128)} %get-tuple-element.65.s_ref), custom_call_target="tpu_custom_call" | custom-call | tf_op jit(solution)/shard_map/pack/pallas_call | solution.py:65
  5.3 7.4 %all-to-all-start = ((bf16[16,16,1024]{2,1,0:T(8,128)(2,1)}), bf16[16,16,1024]{2,1,0:T(8,128)(2,1)S(1)}, u32[]{:S(2)}, u32[]{:S(2)}) async-start(bf16[16,16,1024]{2,1,0:T(8,128)(2,1)} %bitcast.17), calls=%async_computation | async-start | bytes 1048576 | tf_op jit(solution)/shard_map/all_to_all | solution.py:372
  15.4 11.6 %all-to-all-done.x_ref = bf16[16,16,1024]{2,1,0:T(8,128)(2,1)S(1)} async-done(((bf16[16,16,1024]{2,1,0:T(8,128)(2,1)}), bf16[16,16,1024]{2,1,0:T(8,128)(2,1)S(1)}, u32[]{:S(2)}, u32[]{:S(2)}) %all-to-all-start) | async-done | bytes 524320 | tf_op jit(solution)/shard_map/all_to_all | solution.py:372
  27.7 1.9 pick.2
  29.6 4.2 %all-to-all-start.1 = ((bf16[16,16,1024]{2,1,0:T(8,128)(2,1)}), bf16[16,16,1024]{2,1,0:T(8,128)(2,1)S(1)}, u32[]{:S(2)}, u32[]{:S(2)}) async-start(bf16[16,16,1024]{2,1,0:T(8,128)(2,1)} %pick.2), calls=%async_computation.1 | async-start | bytes 1048576 | tf_op jit(solution)/shard_map/all_to_all | solution.py:372
  33.8 3.4 %collective-permute-start.1 = (bf16[256,1024]{1,0:T(8,128)(2,1)}, bf16[256,1024]{1,0:T(8,128)(2,1)S(1)}, u32[]{:S(2)}, u32[]{:S(2)}) collective-permute-start(bf16[256,1024]{1,0:T(8,128)(2,1)} %get-tuple-element.37.kv_ref), channel_id=1, source_target_pairs={{0,16},{1,17},{2,18},{3,19},{4,20},{5,21},{6,22},{7,23},{8,24},{9,... | collective-permute-start | bytes 1572872 | tf_op jit(solution)/shard_map/ppermute | solution.py:378
  37.2 10.8 %all-to-all-done.1 = bf16[16,16,1024]{2,1,0:T(8,128)(2,1)S(1)} async-done(((bf16[16,16,1024]{2,1,0:T(8,128)(2,1)}), bf16[16,16,1024]{2,1,0:T(8,128)(2,1)S(1)}, u32[]{:S(2)}, u32[]{:S(2)}) %all-to-all-start.1) | async-done | bytes 524320 | tf_op jit(solution)/shard_map/all_to_all | solution.py:372
  48.1 4.2 %all-to-all-start.2 = ((bf16[16,16,1024]{2,1,0:T(8,128)(2,1)}), bf16[16,16,1024]{2,1,0:T(8,128)(2,1)S(1)}, u32[]{:S(2)}, u32[]{:S(2)}) async-start(bf16[16,16,1024]{2,1,0:T(8,128)(2,1)} %bitcast.14), calls=%async_computation.2 | async-start | bytes 1048576 | tf_op jit(solution)/shard_map/all_to_all | solution.py:372
  52.2 10.7 %diagonal.3 = (bf16[256,4096]{1,0:T(8,128)(2,1)}, f32[32,256]{1,0:T(8,128)}, f32[256,4096]{1,0:T(8,128)}, f32[256,1024]{1,0:T(8,128)}) custom-call(bf16[256,8192]{1,0:T(8,128)(2,1)} %q_ref.3, bf16[256,8192]{1,0:T(8,128)(2,1)} %do_ref.11, bf16[256,8192]{1,0:T(8,128)(2,1)} %out_ref.3, f32[64,256]{1,0:T(8,128)} %lse_ref.11, ...), custom_call_target="tpu_custom_call" | custom-call | flops 5368709120 | bytes 12582912 | tf_op jit(solution)/shard_map/diagonal/pallas_call | solution.py:176
  66.1 6.6 %cross.5 = (f32[256,4096]{1,0:T(8,128)}, bf16[256,1024]{1,0:T(8,128)(2,1)}) custom-call(s32[1]{0:T(128)} %bitcast.1.flag_ref, bf16[256,4096]{1,0:T(8,128)(2,1)} %get-tuple-element.38.rq_ref, bf16[256,8192]{1,0:T(8,128)(2,1)} %do_ref.11, f32[64,256]{1,0:T(8,128)} %lse_ref.11, f32[32,256]{1,0:T(8,128)} %get-tuple-element.39.delta_ref, ...), custom_call_target="tpu_custom_call" | custom-call | flops 5368709120 | bytes 12582912 | tf_op jit(solution)/shard_map/cross/pallas_call | solution.py:290
  73.5 1.9 pick.3
  75.4 6.0 %all-to-all-start.3 = ((bf16[16,16,1024]{2,1,0:T(8,128)(2,1)}), bf16[16,16,1024]{2,1,0:T(8,128)(2,1)S(1)}, u32[]{:S(2)}, u32[]{:S(2)}) async-start(bf16[16,16,1024]{2,1,0:T(8,128)(2,1)} %pick.3), calls=%async_computation.3 | async-start | bytes 1048576 | tf_op jit(solution)/shard_map/all_to_all | solution.py:372
  82.3 15.6 %cross.6 = (bf16[256,8192]{1,0:T(8,128)(2,1)}, bf16[256,1024]{1,0:T(8,128)(2,1)}, bf16[256,1024]{1,0:T(8,128)(2,1)}) custom-call(s32[1]{0:T(128)} %dynamic_slice.3.flag_ref, bf16[256,4096]{1,0:T(8,128)(2,1)} %get-tuple-element.38.rq_ref, bf16[256,8192]{1,0:T(8,128)(2,1)} %do_ref.11, f32[64,256]{1,0:T(8,128)} %lse_ref.11, ...), custom_call_target="tpu_custom_call" | custom-call | flops 10737418240 | bytes 12582912 | tf_op jit(solution)/shard_map/cross/pallas_call | solution.py:290
  97.9 3.9 %collective-permute-start.3 = (bf16[256,1024]{1,0:T(8,128)(2,1)}, bf16[256,1024]{1,0:T(8,128)(2,1)S(1)}, u32[]{:S(2)}, u32[]{:S(2)}) collective-permute-start(bf16[256,1024]{1,0:T(8,128)(2,1)} %get-tuple-element.45), channel_id=1, source_target_pairs={{0,16},{16,0},{1,17},{17,1},{2,18},{18,2},{3,19},{19,3},{4,20},{20... | collective-permute-start | bytes 1572872 | tf_op jit(solution)/shard_map/ppermute | solution.py:378
  101.8 2.0 collective-permute-start
  103.8 10.7 %collective-permute-done.3 = bf16[256,1024]{1,0:T(8,128)(2,1)S(1)} collective-permute-done((bf16[256,1024]{1,0:T(8,128)(2,1)}, bf16[256,1024]{1,0:T(8,128)(2,1)S(1)}, u32[]{:S(2)}, u32[]{:S(2)}) %collective-permute-start.3) | collective-permute-done | bytes 524320 | tf_op jit(solution)/shard_map/ppermute | solution.py:378
  114.5 2.0 add_convert_fusion.1
  116.5 2.3 collective-permute-start.4
  118.9 6.0 %all-to-all-start.4 = ((bf16[16,16,1024]{2,1,0:T(8,128)(2,1)}), bf16[16,16,1024]{2,1,0:T(8,128)(2,1)S(1)}, u32[]{:S(2)}, u32[]{:S(2)}) async-start(bf16[16,16,1024]{2,1,0:T(8,128)(2,1)} %bitcast.6), calls=%async_computation.4 | async-start | bytes 1048576 | tf_op jit(solution)/shard_map/all_to_all | solution.py:372
  124.9 10.7 %diagonal.2 = (bf16[256,4096]{1,0:T(8,128)(2,1)}, f32[32,256]{1,0:T(8,128)}, f32[256,4096]{1,0:T(8,128)}, f32[256,1024]{1,0:T(8,128)}) custom-call(bf16[256,8192]{1,0:T(8,128)(2,1)} %q_ref.3, bf16[256,8192]{1,0:T(8,128)(2,1)} %do_ref.11, bf16[256,8192]{1,0:T(8,128)(2,1)} %out_ref.3, f32[64,256]{1,0:T(8,128)} %lse_ref.11, ...), custom_call_target="tpu_custom_call" | custom-call | flops 5368709120 | bytes 12582912 | tf_op jit(solution)/shard_map/diagonal/pallas_call | solution.py:176
  136.3 6.4 %cross.4 = (f32[256,4096]{1,0:T(8,128)}, bf16[256,1024]{1,0:T(8,128)(2,1)}) custom-call(s32[1]{0:T(128)} %bitcast.1.flag_ref, bf16[256,4096]{1,0:T(8,128)(2,1)} %get-tuple-element.33.rq_ref, bf16[256,8192]{1,0:T(8,128)(2,1)} %do_ref.11, f32[64,256]{1,0:T(8,128)} %lse_ref.11, f32[32,256]{1,0:T(8,128)} %get-tuple-element.34.delta_ref, ...), custom_call_target="tpu_custom_call" | custom-call | flops 5368709120 | bytes 12582912 | tf_op jit(solution)/shard_map/cross/pallas_call | solution.py:290
  143.6 2.2 merge.2
  145.8 6.0 %all-to-all-start.5 = ((bf16[16,16,1024]{2,1,0:T(8,128)(2,1)}), bf16[16,16,1024]{2,1,0:T(8,128)(2,1)S(1)}, u32[]{:S(2)}, u32[]{:S(2)}) async-start(bf16[16,16,1024]{2,1,0:T(8,128)(2,1)} %merge.2), calls=%async_computation.5 | async-start | bytes 1048576 | tf_op jit(solution)/shard_map/all_to_all | solution.py:372
  152.6 15.8 %cross.7 = (bf16[256,8192]{1,0:T(8,128)(2,1)}, bf16[256,1024]{1,0:T(8,128)(2,1)}, bf16[256,1024]{1,0:T(8,128)(2,1)}) custom-call(s32[1]{0:T(128)} %dynamic_slice.3.flag_ref, bf16[256,4096]{1,0:T(8,128)(2,1)} %get-tuple-element.33.rq_ref, bf16[256,8192]{1,0:T(8,128)(2,1)} %do_ref.11, f32[64,256]{1,0:T(8,128)} %lse_ref.11, ...), custom_call_target="tpu_custom_call", output_to_operand_aliasing={{0}: (10, {})} | custom-call | flops 10737418240 | bytes 12582912 | tf_op jit(solution)/shard_map/cross/pallas_call | solution.py:290
  168.4 3.4 %collective-permute-start.6 = (bf16[256,1024]{1,0:T(8,128)(2,1)}, bf16[256,1024]{1,0:T(8,128)(2,1)S(1)}, u32[]{:S(2)}, u32[]{:S(2)}) collective-permute-start(bf16[256,1024]{1,0:T(8,128)(2,1)} %get-tuple-element.53), channel_id=1, source_target_pairs={{0,16},{16,0},{1,17},{17,1},{2,18},{18,2},{3,19},{19,3},{4,20},{20... | collective-permute-start | bytes 1572872 | tf_op jit(solution)/shard_map/ppermute | solution.py:378
  171.8 12.7 %collective-permute-done.6 = bf16[256,1024]{1,0:T(8,128)(2,1)S(1)} collective-permute-done((bf16[256,1024]{1,0:T(8,128)(2,1)}, bf16[256,1024]{1,0:T(8,128)(2,1)S(1)}, u32[]{:S(2)}, u32[]{:S(2)}) %collective-permute-start.6) | collective-permute-done | bytes 524320 | tf_op jit(solution)/shard_map/ppermute | solution.py:378
  185.8 19.0 %all_to_all.40.x_ref = bf16[16,16,1024]{2,1,0:T(8,128)(2,1)} all-to-all(bf16[16,16,1024]{2,1,0:T(8,128)(2,1)S(1)} %bitcast.13), channel_id=1, replica_groups=mesh['head'=2,'ctx'=16] {'ctx'}, dimensions={0} | all-to-all | bytes 1048576 | tf_op jit(solution)/shard_map/all_to_all | solution.py:372
  204.8 2.2 merge.3
  207.0 4.2 %all-to-all-start.7 = ((bf16[16,16,1024]{2,1,0:T(8,128)(2,1)}), bf16[16,16,1024]{2,1,0:T(8,128)(2,1)S(1)}, u32[]{:S(2)}, u32[]{:S(2)}) async-start(bf16[16,16,1024]{2,1,0:T(8,128)(2,1)} %merge.3), calls=%async_computation.7 | async-start | bytes 1048576 | tf_op jit(solution)/shard_map/all_to_all | solution.py:372
  213.8 14.1 %collective-permute-done.5.refs_1_ = bf16[256,1024]{1,0:T(8,128)(2,1)S(1)} collective-permute-done((bf16[256,1024]{1,0:T(8,128)(2,1)S(1)}, bf16[256,1024]{1,0:T(8,128)(2,1)S(1)}, u32[]{:S(2)}, u32[]{:S(2)}) %collective-permute-start.5) | collective-permute-done | bytes 524320 | tf_op jit(solution)/shard_map/ppermute | solution.py:378
  227.8 10.7 %collective-permute-done.7.refs_4_ = bf16[256,1024]{1,0:T(8,128)(2,1)S(1)} collective-permute-done((bf16[256,1024]{1,0:T(8,128)(2,1)S(1)}, bf16[256,1024]{1,0:T(8,128)(2,1)S(1)}, u32[]{:S(2)}, u32[]{:S(2)}) %collective-permute-start.7) | collective-permute-done | bytes 524320 | tf_op jit(solution)/shard_map/ppermute | solution.py:378
  239.5 3.7 %finish.1 = (bf16[256,1024]{1,0:T(8,128)(2,1)}, bf16[256,1024]{1,0:T(8,128)(2,1)}) custom-call(f32[256,128]{1,0:T(8,128)} %get-tuple-element.64.c_ref, f32[256,128]{1,0:T(8,128)} %get-tuple-element.65.s_ref, f32[256,1024]{1,0:T(8,128)} %get-tuple-element.50.refs_0_, bf16[256,1024]{1,0:T(8,128)(2,1)} %copy-done.6, bf16[256,1024]{1,0:T(8,128)(2,1)} %bitcast.11, ...), custom_call_target="tpu_custom_call" | custom-call | tf_op jit(solution)/shard_map/finish/pallas_call | solution.py:334
  (62 shorter events, 17.5 us)
Async XLA Ops:
  0.6 12.7 %copy-start = (s32[16,1]{0,1:T(1,128)S(1)}, s32[16,1]{0,1:T(1,128)}, u32[]{:S(2)}) copy-start(s32[16,1]{0,1:T(1,128)} %param.15) | copy-start | bytes 196
  5.3 21.7 %all-to-all-start = ((bf16[16,16,1024]{2,1,0:T(8,128)(2,1)}), bf16[16,16,1024]{2,1,0:T(8,128)(2,1)S(1)}, u32[]{:S(2)}, u32[]{:S(2)}) async-start(bf16[16,16,1024]{2,1,0:T(8,128)(2,1)} %bitcast.17), calls=%async_computation | async-start | bytes 1048576 | tf_op jit(solution)/shard_map/all_to_all | solution.py:372
  29.6 18.4 %all-to-all-start.1 = ((bf16[16,16,1024]{2,1,0:T(8,128)(2,1)}), bf16[16,16,1024]{2,1,0:T(8,128)(2,1)S(1)}, u32[]{:S(2)}, u32[]{:S(2)}) async-start(bf16[16,16,1024]{2,1,0:T(8,128)(2,1)} %pick.2), calls=%async_computation.1 | async-start | bytes 1048576 | tf_op jit(solution)/shard_map/all_to_all | solution.py:372
  33.8 31.5 %collective-permute-start.1 = (bf16[256,1024]{1,0:T(8,128)(2,1)}, bf16[256,1024]{1,0:T(8,128)(2,1)S(1)}, u32[]{:S(2)}, u32[]{:S(2)}) collective-permute-start(bf16[256,1024]{1,0:T(8,128)(2,1)} %get-tuple-element.37.kv_ref), channel_id=1, source_target_pairs={{0,16},{1,17},{2,18},{3,19},{4,20},{5,21},{6,22},{7,23},{8,24},{9,... | collective-permute-start | bytes 1572872 | tf_op jit(solution)/shard_map/ppermute | solution.py:378
  48.1 14.9 %copy-start.9 = (bf16[16,16,1024]{2,1,0:T(8,128)(2,1)}, bf16[16,16,1024]{2,1,0:T(8,128)(2,1)S(1)}, u32[]{:S(2)}) copy-start(bf16[16,16,1024]{2,1,0:T(8,128)(2,1)S(1)} %all-to-all-done.1) | copy-start | bytes 1572868
  48.1 24.7 %all-to-all-start.2 = ((bf16[16,16,1024]{2,1,0:T(8,128)(2,1)}), bf16[16,16,1024]{2,1,0:T(8,128)(2,1)S(1)}, u32[]{:S(2)}, u32[]{:S(2)}) async-start(bf16[16,16,1024]{2,1,0:T(8,128)(2,1)} %bitcast.14), calls=%async_computation.2 | async-start | bytes 1048576 | tf_op jit(solution)/shard_map/all_to_all | solution.py:372
  52.2 12.3 %copy-start.12 = (s32[16]{0:T(128)S(1)}, s32[16]{0:T(128)}, u32[]{:S(2)}) copy-start(s32[16]{0:T(128)} %param.16) | copy-start | bytes 196
  63.0 18.5 %collective-permute-start.2 = (bf16[256,1024]{1,0:T(8,128)(2,1)S(1)}, bf16[256,1024]{1,0:T(8,128)(2,1)S(1)}, u32[]{:S(2)}, u32[]{:S(2)}) collective-permute-start(bf16[256,1024]{1,0:T(8,128)(2,1)S(1)} %bitcast.15), channel_id=1, source_target_pairs={{0,16},{16,0},{1,17},{17,1},{2,18},{18,2},{3,19},{19,3},{4,20},{20... | collective-permute-start | bytes 1572872 | tf_op jit(solution)/shard_map/ppermute | solution.py:378
  64.7 8.0 %copy-start.11 = (s32[16]{0:T(128)}, s32[16]{0:T(128)S(1)}, u32[]{:S(2)}) copy-start(s32[16]{0:T(128)S(1)} %convert_element_type.25.present_ref) | copy-start | bytes 196
  65.3 0.8 copy-start.16
  72.7 0.8 copy-start.4
  75.4 41.1 %all-to-all-start.3 = ((bf16[16,16,1024]{2,1,0:T(8,128)(2,1)}), bf16[16,16,1024]{2,1,0:T(8,128)(2,1)S(1)}, u32[]{:S(2)}, u32[]{:S(2)}) async-start(bf16[16,16,1024]{2,1,0:T(8,128)(2,1)} %pick.3), calls=%async_computation.3 | async-start | bytes 1048576 | tf_op jit(solution)/shard_map/all_to_all | solution.py:372
  81.5 0.8 copy-start.15
  82.3 19.6 %copy-start.8 = (bf16[256,1024]{1,0:T(8,128)(2,1)S(1)}, bf16[256,1024]{1,0:T(8,128)(2,1)}, u32[]{:S(2)}) copy-start(bf16[256,1024]{1,0:T(8,128)(2,1)} %get-tuple-element.46.kv_ref) | copy-start | bytes 1572868
  97.9 16.6 %collective-permute-start.3 = (bf16[256,1024]{1,0:T(8,128)(2,1)}, bf16[256,1024]{1,0:T(8,128)(2,1)S(1)}, u32[]{:S(2)}, u32[]{:S(2)}) collective-permute-start(bf16[256,1024]{1,0:T(8,128)(2,1)} %get-tuple-element.45), channel_id=1, source_target_pairs={{0,16},{16,0},{1,17},{17,1},{2,18},{18,2},{3,19},{19,3},{4,20},{20... | collective-permute-start | bytes 1572872 | tf_op jit(solution)/shard_map/ppermute | solution.py:378
  101.8 33.7 %collective-permute-start = (bf16[256,1024]{1,0:T(8,128)(2,1)S(1)}, bf16[256,1024]{1,0:T(8,128)(2,1)S(1)}, u32[]{:S(2)}, u32[]{:S(2)}) collective-permute-start(bf16[256,1024]{1,0:T(8,128)(2,1)S(1)} %copy-done.8), channel_id=1, source_target_pairs={{0,16},{1,17},{2,18},{3,19},{4,20},{5,21},{6,22},{7,23},{8,24},{9,... | collective-permute-start | bytes 1572872 | tf_op jit(solution)/shard_map/ppermute | solution.py:378
  116.5 19.0 %copy-start.10 = (bf16[16,16,1024]{2,1,0:T(8,128)(2,1)}, bf16[16,16,1024]{2,1,0:T(8,128)(2,1)S(1)}, u32[]{:S(2)}) copy-start(bf16[16,16,1024]{2,1,0:T(8,128)(2,1)S(1)} %all-to-all-done.3) | copy-start | bytes 1572868
  116.5 35.2 %collective-permute-start.4 = (bf16[256,1024]{1,0:T(8,128)(2,1)S(1)}, bf16[256,1024]{1,0:T(8,128)(2,1)S(1)}, u32[]{:S(2)}, u32[]{:S(2)}) collective-permute-start(bf16[256,1024]{1,0:T(8,128)(2,1)S(1)} %bitcast.18), channel_id=1, source_target_pairs={{0,16},{16,0},{1,17},{17,1},{2,18},{18,2},{3,19},{19,3},{4,20},{20... | collective-permute-start | bytes 1572872 | tf_op jit(solution)/shard_map/ppermute | solution.py:378
  118.9 23.9 %all-to-all-start.4 = ((bf16[16,16,1024]{2,1,0:T(8,128)(2,1)}), bf16[16,16,1024]{2,1,0:T(8,128)(2,1)S(1)}, u32[]{:S(2)}, u32[]{:S(2)}) async-start(bf16[16,16,1024]{2,1,0:T(8,128)(2,1)} %bitcast.6), calls=%async_computation.4 | async-start | bytes 1048576 | tf_op jit(solution)/shard_map/all_to_all | solution.py:372
  135.5 0.8 copy-start.18
  142.8 0.8 copy-start.3
  145.8 40.0 %all-to-all-start.5 = ((bf16[16,16,1024]{2,1,0:T(8,128)(2,1)}), bf16[16,16,1024]{2,1,0:T(8,128)(2,1)S(1)}, u32[]{:S(2)}, u32[]{:S(2)}) async-start(bf16[16,16,1024]{2,1,0:T(8,128)(2,1)} %merge.2), calls=%async_computation.5 | async-start | bytes 1048576 | tf_op jit(solution)/shard_map/all_to_all | solution.py:372
  151.8 0.8 copy-start.17
  168.4 42.8 %copy-start.13 = (bf16[256,1024]{1,0:T(8,128)(2,1)S(1)}, bf16[256,1024]{1,0:T(8,128)(2,1)}, u32[]{:S(2)}) copy-start(bf16[256,1024]{1,0:T(8,128)(2,1)} %get-tuple-element.51) | copy-start | bytes 1572868
  168.4 44.1 %copy-start.14 = (bf16[256,1024]{1,0:T(8,128)(2,1)S(1)}, bf16[256,1024]{1,0:T(8,128)(2,1)}, u32[]{:S(2)}) copy-start(bf16[256,1024]{1,0:T(8,128)(2,1)} %get-tuple-element.57) | copy-start | bytes 1572868
  168.4 16.1 %collective-permute-start.6 = (bf16[256,1024]{1,0:T(8,128)(2,1)}, bf16[256,1024]{1,0:T(8,128)(2,1)S(1)}, u32[]{:S(2)}, u32[]{:S(2)}) collective-permute-start(bf16[256,1024]{1,0:T(8,128)(2,1)} %get-tuple-element.53), channel_id=1, source_target_pairs={{0,16},{16,0},{1,17},{17,1},{2,18},{18,2},{3,19},{19,3},{4,20},{20... | collective-permute-start | bytes 1572872 | tf_op jit(solution)/shard_map/ppermute | solution.py:378
  185.8 52.7 %copy-start.1 = (bf16[16,16,1024]{2,1,0:T(8,128)(2,1)}, bf16[16,16,1024]{2,1,0:T(8,128)(2,1)S(1)}, u32[]{:S(2)}) copy-start(bf16[16,16,1024]{2,1,0:T(8,128)(2,1)S(1)} %all-to-all-done.5) | copy-start | bytes 1572868
  207.0 31.6 %all-to-all-start.7 = ((bf16[16,16,1024]{2,1,0:T(8,128)(2,1)}), bf16[16,16,1024]{2,1,0:T(8,128)(2,1)S(1)}, u32[]{:S(2)}, u32[]{:S(2)}) async-start(bf16[16,16,1024]{2,1,0:T(8,128)(2,1)} %merge.3), calls=%async_computation.7 | async-start | bytes 1048576 | tf_op jit(solution)/shard_map/all_to_all | solution.py:372
  211.1 16.7 %collective-permute-start.5 = (bf16[256,1024]{1,0:T(8,128)(2,1)S(1)}, bf16[256,1024]{1,0:T(8,128)(2,1)S(1)}, u32[]{:S(2)}, u32[]{:S(2)}) collective-permute-start(bf16[256,1024]{1,0:T(8,128)(2,1)S(1)} %copy-done.13), channel_id=1, source_target_pairs={{16,0},{17,1},{18,2},{19,3},{20,4},{21,5},{22,6},{23,7},{24,8},{25... | collective-permute-start | bytes 1572872 | tf_op jit(solution)/shard_map/ppermute | solution.py:378
  212.5 26.1 %collective-permute-start.7 = (bf16[256,1024]{1,0:T(8,128)(2,1)S(1)}, bf16[256,1024]{1,0:T(8,128)(2,1)S(1)}, u32[]{:S(2)}, u32[]{:S(2)}) collective-permute-start(bf16[256,1024]{1,0:T(8,128)(2,1)S(1)} %copy-done.14), channel_id=1, source_target_pairs={{16,0},{17,1},{18,2},{19,3},{20,4},{21,5},{22,6},{23,7},{24,8},{25... | collective-permute-start | bytes 1572872 | tf_op jit(solution)/shard_map/ppermute | solution.py:378
  227.8 10.7 %copy-start.6 = (bf16[256,1024]{1,0:T(8,128)(2,1)}, bf16[256,1024]{1,0:T(8,128)(2,1)S(1)}, u32[]{:S(2)}) copy-start(bf16[256,1024]{1,0:T(8,128)(2,1)S(1)} %collective-permute-done.5.refs_1_) | copy-start | bytes 1572868
  238.5 1.0 copy-start.2
  (2 other events, 1.6 us)
where the time goes:
time: 245 us; the launch traced here: 243 us
  Pallas kernels  80.1 us (33%)
  waiting for transfers between devices  70.6 us (29%)
  starting transfers between devices  57.1 us (23%)
  blocking collectives  19 us (8%)
  local copies, waits for them, and re-layouts  7.77 us (3%)
  other arithmetic  7.58 us (3%)
    ppermute x8, waiting for transfers between devices, shift(): return lax.ppermute(x, 'head', route)  48.2 us
    pallas_call x4, Pallas kernels, cross(): pl.pallas_call(functools.partial(cross_kernel, group, joint, mode), out_s...  44.4 us
    all_to_all x7, starting transfers between devices, exchange(): lax.all_to_all(x.reshape(places, rows // places, width), 'ctx', 0, 0, til...  37.9 us
    all_to_all x7, waiting for transfers between devices, exchange(): lax.all_to_all(x.reshape(places, rows // places, width), 'ctx', 0, 0, til...  22.4 us
    pallas_call x2, Pallas kernels, diagonal(): pl.pallas_call(functools.partial(diagonal_kernel, group), out_shape=[jax....  21.4 us
    ppermute x8, starting transfers between devices, shift(): return lax.ppermute(x, 'head', route)  19.2 us
    all_to_all x1, blocking collectives, exchange(): lax.all_to_all(x.reshape(places, rows // places, width), 'ctx', 0, 0, til...  19 us
    unnamed x38, local copies, waits for them, and re-layouts  6.52 us
  transfers between devices with their start and end apart: 15, of which 6 were waited for; matrix products, arithmetic and copies ran while one was open for 3% of the time, Pallas kernels for 29%

commit v1 on v0

--- a/solution.py
+++ b/solution.py
@@ -48,25 +48,20 @@
     )
 
 
-def pack_kernel(sizes, k_ref, v_ref, c_ref, s_ref, *o_refs):
+def pack_kernel(k_ref, v_ref, c_ref, s_ref, o_ref):
     c, s = c_ref[...], s_ref[...]
-    g = 0
-    for size, o_ref in zip(sizes, o_refs):
-        for i in range(size):
-            a, b = g * HEAD_SIZE, 2 * i * HEAD_SIZE
-            x = k_ref[:, a : a + HEAD_SIZE].astype(jnp.float32)
-            o_ref[:, b : b + HEAD_SIZE] = turn(x, c, s).astype(jnp.bfloat16)
-            o_ref[:, b + HEAD_SIZE : b + 2 * HEAD_SIZE] = v_ref[:, a : a + HEAD_SIZE]
-            g += 1
-
-
-def pack(sizes, keys, values, c, s):
-    rows = keys.shape[0]
-    return pl.pallas_call(
-        functools.partial(pack_kernel, sizes),
-        out_shape=[
-            jax.ShapeDtypeStruct((rows, 2 * size * HEAD_SIZE), jnp.bfloat16) for size in sizes
-        ],
+    for g in range(k_ref.shape[1] // HEAD_SIZE):
+        a, b = g * HEAD_SIZE, 2 * g * HEAD_SIZE
+        x = k_ref[:, a : a + HEAD_SIZE].astype(jnp.float32)
+        o_ref[:, b : b + HEAD_SIZE] = turn(x, c, s).astype(jnp.bfloat16)
+        o_ref[:, b + HEAD_SIZE : b + 2 * HEAD_SIZE] = v_ref[:, a : a + HEAD_SIZE]
+
+
+def pack(keys, values, c, s):
+    rows, width = keys.shape
+    return pl.pallas_call(
+        pack_kernel,
+        out_shape=jax.ShapeDtypeStruct((rows, 2 * width), jnp.bfloat16),
         compiler_params=params(0),
         name="pack",
     )(keys, values, c, s)
@@ -91,31 +86,34 @@
     )(source, x)
 
 
-def merge_kernel(source_ref, present_ref, x_ref, o_ref, acc_ref):
+def merge_kernel(source_ref, present_ref, *refs):
+    *x_refs, o_ref, acc_ref = refs
     acc_ref[...] = jnp.zeros_like(acc_ref)
-    for d in range(x_ref.shape[0]):
+    for d in range(o_ref.shape[0]):
 
         @pl.when(present_ref[d] != 0)
         def _():
-            acc_ref[source_ref[d]] += x_ref[d].astype(jnp.float32)
+            at = 0
+            for x_ref in x_refs:
+                width = x_ref.shape[2]
+                acc_ref[source_ref[d], :, at : at + width] += x_ref[d].astype(jnp.float32)
+                at += width
 
     o_ref[...] = acc_ref[...].astype(o_ref.dtype)
 
 
-def merge(source, present, x):
+def merge(source, present, xs):
+    shape = xs[0].shape[:2] + (sum(x.shape[2] for x in xs),)
     return pl.pallas_call(
         merge_kernel,
-        out_shape=jax.ShapeDtypeStruct(x.shape, x.dtype),
-        in_specs=[
-            pl.BlockSpec(memory_space=pltpu.SMEM),
-            pl.BlockSpec(memory_space=pltpu.SMEM),
-            pl.BlockSpec(memory_space=pltpu.VMEM),
-        ],
+        out_shape=jax.ShapeDtypeStruct(shape, xs[0].dtype),
+        in_specs=[pl.BlockSpec(memory_space=pltpu.SMEM)] * 2
+        + [pl.BlockSpec(memory_space=pltpu.VMEM)] * len(xs),
         out_specs=pl.BlockSpec(memory_space=pltpu.VMEM),
-        scratch_shapes=[pltpu.VMEM(x.shape, jnp.float32)],
+        scratch_shapes=[pltpu.VMEM(shape, jnp.float32)],
         compiler_params=params(0),
         name="merge",
-    )(source, present, x)
+    )(source, present, *xs)
 
 
 def fronts(rq, do, lse, delta, k, v, mask=None):
@@ -163,8 +161,10 @@
         dq_ref[:, cols_of(h)] = dot(ds_ref[:, h * rows : (h + 1) * rows], k, TN)
 
 
-def diagonal(first, count, kv_count, q, do, out, lse, c, s, kv):
+def diagonal(q, do, out, lse, c, s, kv):
     rows, width = q.shape
+    kv_count = count = kv.shape[1] // (2 * HEAD_SIZE)
+    first = 0
     group = heads_of(width, kv_count)
     wide = group * HEAD_SIZE
     big = pl.BlockSpec((rows, wide), lambda g: (0, g + first))
@@ -260,8 +260,9 @@
             dq_ref[:, cols] = turn_back(total_ref[:, cols], c, s).astype(jnp.bfloat16)
 
 
-def cross(first, count, kv_count, flags, joint, rq, do, lse, delta, c, s, dq, kvs, whole=None, final=False):
+def cross(first, count, flags, joint, rq, do, lse, delta, c, s, dq, kvs, whole=None, final=False):
     rows, width = do.shape
+    kv_count = kvs[0].shape[1] // (2 * HEAD_SIZE)
     group = heads_of(width, kv_count)
     wide = group * HEAD_SIZE
     most = max(joint)
@@ -269,10 +270,10 @@
     row = pl.BlockSpec((group, rows), lambda g, i: (g + first, 0))
     table = pl.BlockSpec((rows, HEAD_SIZE), lambda g, i: (0, 0))
     pair = pl.BlockSpec((rows, 2 * HEAD_SIZE), lambda g, i: (0, g))
-    part = pl.BlockSpec((rows, wide), lambda g, i: (0, g))
-    part_row = pl.BlockSpec((group, rows), lambda g, i: (g, 0))
+    shifted = pl.BlockSpec((rows, 2 * HEAD_SIZE), lambda g, i: (0, g + first))
     args = [flags, rq, do, lse, delta, c, s, dq, *kvs]
-    in_specs = [part, big, row, part_row, table, table, part] + [pair] * len(kvs)
+    in_specs = [big, big, row, row, table, table, big]
+    in_specs += [shifted if x.shape == kvs[0].shape else pair for x in kvs]
     mode = 0
     aliases = {}
     if final:
@@ -289,12 +290,13 @@
     )
     return pl.pallas_call(
         functools.partial(cross_kernel, group, joint, mode),
-        out_shape=[dq_shape] + [jax.ShapeDtypeStruct(kvs[0].shape, jnp.bfloat16)] * len(kvs),
+        out_shape=[dq_shape]
+        + [jax.ShapeDtypeStruct((rows, count * 2 * HEAD_SIZE), jnp.bfloat16)] * len(kvs),
         grid_spec=pltpu.PrefetchScalarGridSpec(
             num_scalar_prefetch=1,
             grid=(count,),
             in_specs=in_specs,
-            out_specs=[big if final else part] + [pair] * len(kvs),
+            out_specs=[big] + [pair] * len(kvs),
             scratch_shapes=[pltpu.VMEM((most * rows, group * rows), jnp.bfloat16)] * 2
             + [pltpu.VMEM((most * rows, HEAD_SIZE), jnp.bfloat16)] * 2
             + ([pltpu.VMEM((rows, wide), jnp.float32)] if final else []),
@@ -310,33 +312,28 @@
     )(*args)
 
 
-def finish_kernel(sizes, parts, c_ref, s_ref, *refs):
-    refs = list(refs)
-    dk_ref, dv_ref = refs[-2:]
+def finish_kernel(parts, own_ref, c_ref, s_ref, *refs):
+    in_refs = refs[:parts]
+    dk_ref, dv_ref = refs[parts:]
     c, s = c_ref[...], s_ref[...]
-    g = 0
-    for size in sizes:
-        in_refs = [refs.pop(0) for _ in range(parts)]
-        for i in range(size):
-            a, b = g * HEAD_SIZE, 2 * i * HEAD_SIZE
-            total = in_refs[0][:, b : b + 2 * HEAD_SIZE]
-            for ref in in_refs[1:]:
-                total = total + ref[:, b : b + 2 * HEAD_SIZE].astype(jnp.float32)
-            gk = total[:, :HEAD_SIZE]
-            dk_ref[:, a : a + HEAD_SIZE] = turn_back(gk, c, s).astype(jnp.bfloat16)
-            dv_ref[:, a : a + HEAD_SIZE] = total[:, HEAD_SIZE:].astype(jnp.bfloat16)
-            g += 1
-
-
-def finish(sizes, chunks, c, s):
-    rows = chunks[0][0].shape[0]
-    width = sum(sizes) * HEAD_SIZE
-    return pl.pallas_call(
-        functools.partial(finish_kernel, sizes, len(chunks[0])),
-        out_shape=[jax.ShapeDtypeStruct((rows, width), jnp.bfloat16)] * 2,
+    for g in range(dk_ref.shape[1] // HEAD_SIZE):
+        a, b = g * HEAD_SIZE, 2 * g * HEAD_SIZE
+        total = own_ref[:, b : b + 2 * HEAD_SIZE]
+        for ref in in_refs:
+            total = total + ref[:, b : b + 2 * HEAD_SIZE].astype(jnp.float32)
+        gk = total[:, :HEAD_SIZE]
+        dk_ref[:, a : a + HEAD_SIZE] = turn_back(gk, c, s).astype(jnp.bfloat16)
+        dv_ref[:, a : a + HEAD_SIZE] = total[:, HEAD_SIZE:].astype(jnp.bfloat16)
+
+
+def finish(local, parts, c, s):
+    rows, width = local.shape
+    return pl.pallas_call(
+        functools.partial(finish_kernel, len(parts)),
+        out_shape=[jax.ShapeDtypeStruct((rows, width // 2), jnp.bfloat16)] * 2,
         compiler_params=params(0),
         name="finish",
-    )(c, s, *[x for chunk in chunks for x in chunk])
+    )(local, c, s, *parts)
 
 
 def body(
@@ -362,8 +359,7 @@
     source = jnp.argmax(match, axis=1).astype(jnp.int32)
     present = jnp.any(match, axis=1).astype(jnp.int32)
 
-    kv_count = unrotated_keys.shape[1] // HEAD_SIZE
-    sizes = split(kv_count)
+    sizes = split(unrotated_keys.shape[1] // HEAD_SIZE)
     chunks = range(len(sizes))
     firsts = [sum(sizes[:g]) for g in chunks]
 
@@ -377,36 +373,31 @@
         route = [(i, (i + n) % hops) for i in range(hops) if wrap or 0 <= i + n < hops]
         return lax.ppermute(x, "head", route)
 
-    kv = pack(sizes, unrotated_keys, value_rows, c, s)
+    kv = pack(unrotated_keys, value_rows, c, s)
     own_flags = jnp.stack([(me >= n).astype(jnp.int32) for n in range(1, hops)])
     parent_flag = present[here][None]
     own_sets, parent_sets = (1,) * (hops - 1), (hops,)
 
+    middle = exchange(kv)
+    own_kv = [shift(kv, n, False) for n in range(1, hops)]
+    rq, delta, dq, local = diagonal(
+        queries, output_gradient, outputs, saved_logsumexp, c, s, kv
+    )
+    picked = pick(source, middle)
+    near = exchange(picked).reshape(rows, -1)
+    dq, *own_part = cross(
+        0, sum(sizes), own_flags, own_sets, rq, output_gradient,
+        saved_logsumexp, delta, c, s, dq, own_kv,
+    )
+    back = [shift(own_part[n - 1], -n, False) for n in range(1, hops)]
     grad_queries = None
-    own_dkv, children, fetched = [], [], []
+    ups = []
     for g in chunks:
-        send = kv[g]
-        if g:
-            send, fetched[g - 1] = lax.optimization_barrier((send, fetched[g - 1]))
-        middle = exchange(send)
-        picked = pick(source, middle)
-        fetched.append(exchange(picked))
-    for g in chunks:
-        own_kv = [shift(kv[g], n, False) for n in range(1, hops)]
-        rq, delta, dq, local = diagonal(
-            firsts[g], sizes[g], kv_count, queries, output_gradient, outputs,
-            saved_logsumexp, c, s, kv[g],
-        )
-        near = fetched[g].reshape(rows, -1)
-        parent_kv = [near] + [shift(near, n, True) for n in range(1, hops)]
-        dq, *own_part = cross(
-            firsts[g], sizes[g], kv_count, own_flags, own_sets, rq, output_gradient,
-            saved_logsumexp, delta, c, s, dq, own_kv,
-        )
-        back = [shift(own_part[n - 1], -n, False) for n in range(1, hops)]
-        own_dkv.append([local] + back)
+        at = 2 * HEAD_SIZE * firsts[g]
+        piece = near[:, at : at + 2 * HEAD_SIZE * sizes[g]]
+        parent_kv = [near] + [shift(piece, n, True) for n in range(1, hops)]
         grad_queries, *part = cross(
-            firsts[g], sizes[g], kv_count, parent_flag, parent_sets, rq, output_gradient,
+            firsts[g], sizes[g], parent_flag, parent_sets, rq, output_gradient,
             saved_logsumexp, delta, c, s, dq, parent_kv, grad_queries, True,
         )
         far_part = [shift(part[n], -n, True) for n in range(1, hops)]
@@ -415,20 +406,18 @@
             total = total + x.astype(jnp.float32)
         send = total.astype(jnp.bfloat16)
         if g:
-            send, children[g - 1] = lax.optimization_barrier((send, children[g - 1]))
-        else:
-            send, fetched[-1] = lax.optimization_barrier((send, fetched[-1]))
-        up = exchange(send)
-        merged = merge(source, present, up)
-        children.append(exchange(merged))
-    grad_keys, grad_values = finish(
-        sizes, [own_dkv[g] + [children[g].reshape(rows, -1)] for g in chunks], c, s
-    )
+            send, ups[-1] = lax.optimization_barrier((send, ups[-1]))
+        ups.append(exchange(send))
+    merged = merge(source, present, ups)
+    children = exchange(merged).reshape(rows, -1)
+    grad_keys, grad_values = finish(local, back + [children], c, s)
     return (grad_queries, grad_keys, grad_values)
 
 
 def split(kv_count):
-    return (kv_count // 2, kv_count - kv_count // 2)
+    first = kv_count // 4
+    second = (kv_count - first) // 2
+    return (first, second, kv_count - first - second)
 
 
 def solution(mesh):

time: 245 us -> 222 us (0.906)
  starting transfers between devices: 57.1 us -> 43.7 us
  Pallas kernels: 80.1 us -> 76.9 us
    all_to_all x7 -> x5, starting transfers between devices: 37.9 us -> 27.4 us  [exchange(): lax.all_to_all(x.reshape(places, rows // places, width), 'ctx', 0, 0, til...]
    ppermute x8, waiting for transfers between devices: 48.2 us -> 41.1 us  [shift(): return lax.ppermute(x, 'head', route)]
    all_to_all x7 -> x5, waiting for transfers between devices: 22.4 us -> 28.1 us  [exchange(): lax.all_to_all(x.reshape(places, rows // places, width), 'ctx', 0, 0, til...]
    ppermute x8, starting transfers between devices: 19.2 us -> 16.2 us  [shift(): return lax.ppermute(x, 'head', route)]
    pallas_call x2 -> x1, Pallas kernels: 21.4 us -> 18.7 us  [diagonal(): pl.pallas_call(functools.partial(diagonal_kernel, group), out_shape=[jax....]
    unnamed x38 -> x30, local copies, waits for them, and re-layouts: 6.52 us -> 4.77 us
    pallas_call x4 -> x3, Pallas kernels: 10.5 us -> 9.06 us  [the longest x1 3.7 us: finish(): pl.pallas_call(functools.partial(finish_kernel, len(parts)), out_shape=[j...]
  transfers between devices with their start and end apart: 15 -> 13, of which waited for: 6 -> 6; matrix products, arithmetic and copies ran while one was open for 3% -> 3% of each run, Pallas kernels for 29% -> 30%
where the time goes in v1:
time: 222 us; the launch traced here: 221 us
  Pallas kernels  76.9 us (35%)
  waiting for transfers between devices  69.2 us (31%)
  starting transfers between devices  43.7 us (20%)
  blocking collectives  17 us (8%)
  other arithmetic  6.84 us (3%)
  local copies, waits for them, and re-layouts  6.16 us (3%)
    pallas_call x4, Pallas kernels, cross(): pl.pallas_call(functools.partial(cross_kernel, group, joint, mode), out_s...  46.8 us
    ppermute x8, waiting for transfers between devices, shift(): return lax.ppermute(x, 'head', route)  41.1 us
    all_to_all x5, waiting for transfers between devices, exchange(): lax.all_to_all(x.reshape(places, rows // places, width), 'ctx', 0, 0, til...  28.1 us
    all_to_all x5, starting transfers between devices, exchange(): lax.all_to_all(x.reshape(places, rows // places, width), 'ctx', 0, 0, til...  27.4 us
    pallas_call x1, Pallas kernels, diagonal(): pl.pallas_call(functools.partial(diagonal_kernel, group), out_shape=[jax....  18.7 us
    all_to_all x1, blocking collectives, exchange(): lax.all_to_all(x.reshape(places, rows // places, width), 'ctx', 0, 0, til...  17 us
    ppermute x8, starting transfers between devices, shift(): return lax.ppermute(x, 'head', route)  16.2 us
    unnamed x30, local copies, waits for them, and re-layouts  4.77 us
  transfers between devices with their start and end apart: 13, of which 6 were waited for; matrix products, arithmetic and copies ran while one was open for 3% of the time, Pallas kernels for 30%

profile of v1, /device:TPU:0, one launch (start us, length us, event | category | flops | bytes accessed | tf_op | source)
XLA Modules:
  0.0 220.6 jit_solution(6825405371373986170)
XLA Ops:
  1.9 0.9 pad_maximum_fusion
  2.7 2.6 %pack.1.kv_ref = bf16[256,2048]{1,0:T(8,128)(2,1)} custom-call(bf16[256,1024]{1,0:T(8,128)(2,1)} %k_ref.1, bf16[256,1024]{1,0:T(8,128)(2,1)} %v_ref.1, f32[256,128]{1,0:T(8,128)} %get-tuple-element.52.c_ref, f32[256,128]{1,0:T(8,128)} %get-tuple-element.53.s_ref), custom_call_target="tpu_custom_call" | custom-call | tf_op jit(solution)/shard_map/pack/pallas_call | solution.py:62
  5.4 7.5 %all-to-all-start = ((bf16[16,16,2048]{2,1,0:T(8,128)(2,1)}), bf16[16,16,2048]{2,1,0:T(8,128)(2,1)S(1)}, u32[]{:S(2)}, u32[]{:S(2)}) async-start(bf16[16,16,2048]{2,1,0:T(8,128)(2,1)} %bitcast.15), calls=%async_computation | async-start | bytes 2097152 | tf_op jit(solution)/shard_map/all_to_all | solution.py:368
  14.4 21.4 %all-to-all-done.x_ref = bf16[16,16,2048]{2,1,0:T(8,128)(2,1)S(1)} async-done(((bf16[16,16,2048]{2,1,0:T(8,128)(2,1)}), bf16[16,16,2048]{2,1,0:T(8,128)(2,1)S(1)}, u32[]{:S(2)}, u32[]{:S(2)}) %all-to-all-start) | async-done | bytes 1048608 | tf_op jit(solution)/shard_map/all_to_all | solution.py:368
  35.8 1.0 copy-done.2
  36.8 2.3 %pick.1 = bf16[16,16,2048]{2,1,0:T(8,128)(2,1)} custom-call(s32[16]{0:T(128)} %get-tuple-element.29.source_ref, bf16[16,16,2048]{2,1,0:T(8,128)(2,1)} %copy-done.2), custom_call_target="tpu_custom_call" | custom-call | tf_op jit(solution)/shard_map/pick/pallas_call | solution.py:76
  39.1 6.8 %all-to-all-start.1 = ((bf16[16,16,2048]{2,1,0:T(8,128)(2,1)}), bf16[16,16,2048]{2,1,0:T(8,128)(2,1)S(1)}, u32[]{:S(2)}, u32[]{:S(2)}) async-start(bf16[16,16,2048]{2,1,0:T(8,128)(2,1)} %pick.1), calls=%async_computation.1 | async-start | bytes 2097152 | tf_op jit(solution)/shard_map/all_to_all | solution.py:368
  45.9 3.5 %collective-permute-start = (bf16[256,2048]{1,0:T(8,128)(2,1)S(1)}, bf16[256,2048]{1,0:T(8,128)(2,1)S(1)}, u32[]{:S(2)}, u32[]{:S(2)}) collective-permute-start(bf16[256,2048]{1,0:T(8,128)(2,1)S(1)} %copy-done.4), channel_id=1, source_target_pairs={{0,16},{1,17},{2,18},{3,19},{4,20},{5,21},{6,22},{7,23},{8,24},{9,... | collective-permute-start | bytes 3145736 | tf_op jit(solution)/shard_map/ppermute | solution.py:374
  50.2 18.7 %diagonal.1 = (bf16[256,8192]{1,0:T(8,128)(2,1)}, f32[64,256]{1,0:T(8,128)}, f32[256,8192]{1,0:T(8,128)}, f32[256,2048]{1,0:T(8,128)}) custom-call(bf16[256,8192]{1,0:T(8,128)(2,1)} %q_ref.1, bf16[256,8192]{1,0:T(8,128)(2,1)} %do_ref.9, bf16[256,8192]{1,0:T(8,128)(2,1)} %out_ref.1, f32[64,256]{1,0:T(8,128)} %lse_ref.9, f32[256,128]{1,0:T(8,128)} %get-tuple-element.52.c_ref, ...), custom_call_target="tpu_custom_call" | custom-call | flops 10737418240 | bytes 25165824 | tf_op jit(solution)/shard_map/diagonal/pallas_call | solution.py:176
  69.0 1.4 collective-permute-start.3
  70.3 2.5 %collective-permute-done.refs_0_ = bf16[256,2048]{1,0:T(8,128)(2,1)S(1)} collective-permute-done((bf16[256,2048]{1,0:T(8,128)(2,1)S(1)}, bf16[256,2048]{1,0:T(8,128)(2,1)S(1)}, u32[]{:S(2)}, u32[]{:S(2)}) %collective-permute-start) | collective-permute-done | bytes 1048608 | tf_op jit(solution)/shard_map/ppermute | solution.py:374
  72.8 1.0 copy-done.12
  73.8 11.8 %cross.4 = (f32[256,8192]{1,0:T(8,128)}, bf16[256,2048]{1,0:T(8,128)(2,1)}) custom-call(s32[1]{0:T(128)} %bitcast.1.flag_ref, bf16[256,8192]{1,0:T(8,128)(2,1)} %get-tuple-element.25.rq_ref, bf16[256,8192]{1,0:T(8,128)(2,1)} %do_ref.9, f32[64,256]{1,0:T(8,128)} %lse_ref.9, f32[64,256]{1,0:T(8,128)} %get-tuple-element.26.delta_ref, ...), custom_call_target="tpu_custom_call" | custom-call | flops 10737418240 | bytes 25165824 | tf_op jit(solution)/shard_map/cross/pallas_call | solution.py:291
  85.7 7.8 %collective-permute-start.2 = (bf16[256,768]{1,0:T(8,128)(2,1)S(1)}, bf16[256,768]{1,0:T(8,128)(2,1)S(1)}, u32[]{:S(2)}, u32[]{:S(2)}) collective-permute-start(bf16[256,768]{1,0:T(8,128)(2,1)S(1)} %get-tuple-element.47), channel_id=1, source_target_pairs={{0,16},{16,0},{1,17},{17,1},{2,18},{18,2},{3,19},{19,3},{4,20},{20... | collective-permute-start | bytes 1179656 | tf_op jit(solution)/shard_map/ppermute | solution.py:374
  93.5 9.7 %cross.5 = (bf16[256,8192]{1,0:T(8,128)(2,1)}, bf16[256,512]{1,0:T(8,128)(2,1)}, bf16[256,512]{1,0:T(8,128)(2,1)}) custom-call(s32[1]{0:T(128)} %dynamic_slice.3.flag_ref, bf16[256,8192]{1,0:T(8,128)(2,1)} %get-tuple-element.25.rq_ref, bf16[256,8192]{1,0:T(8,128)(2,1)} %do_ref.9, f32[64,256]{1,0:T(8,128)} %lse_ref.9, f32[64,256]{1,0:T(8,128)} %get-tuple-element.26.delta_ref, ...), custom_call_target="tpu_custom_call" | custom-call | flops 5368709120 | bytes 6291456 | tf_op jit(solution)/shard_map/cross/pallas_call | solution.py:291
  104.0 12.7 %cross.6 = (bf16[256,8192]{1,0:T(8,128)(2,1)}, bf16[256,768]{1,0:T(8,128)(2,1)}, bf16[256,768]{1,0:T(8,128)(2,1)}) custom-call(s32[1]{0:T(128)} %dynamic_slice.3.flag_ref, bf16[256,8192]{1,0:T(8,128)(2,1)} %get-tuple-element.25.rq_ref, bf16[256,8192]{1,0:T(8,128)(2,1)} %do_ref.9, f32[64,256]{1,0:T(8,128)} %lse_ref.9, ...), custom_call_target="tpu_custom_call", output_to_operand_aliasing={{0}: (10, {})} | custom-call | flops 8053063680 | bytes 9437184 | tf_op jit(solution)/shard_map/cross/pallas_call | solution.py:291
  116.7 2.0 collective-permute-start.5
  119.5 5.7 %all-to-all-start.2 = ((bf16[16,16,512]{2,1,0:T(8,128)(2,1)}), bf16[16,16,512]{2,1,0:T(8,128)(2,1)S(1)}, u32[]{:S(2)}, u32[]{:S(2)}) async-start(bf16[16,16,512]{2,1,0:T(8,128)(2,1)} %bitcast.4), calls=%async_computation.2 | async-start | bytes 524288 | tf_op jit(solution)/shard_map/all_to_all | solution.py:368
  125.3 1.3 collective-permute-done.5
  126.7 1.9 add_convert_fusion.1
  128.6 6.7 %all-to-all-done.2.refs_0_ = bf16[16,16,512]{2,1,0:T(8,128)(2,1)S(1)} async-done(((bf16[16,16,512]{2,1,0:T(8,128)(2,1)}), bf16[16,16,512]{2,1,0:T(8,128)(2,1)S(1)}, u32[]{:S(2)}, u32[]{:S(2)}) %all-to-all-start.2) | async-done | bytes 262176 | tf_op jit(solution)/shard_map/all_to_all | solution.py:368
  135.2 3.7 %all-to-all-start.3 = ((bf16[16,16,768]{2,1,0:T(8,128)(2,1)}), bf16[16,16,768]{2,1,0:T(8,128)(2,1)S(1)}, u32[]{:S(2)}, u32[]{:S(2)}) async-start(bf16[16,16,768]{2,1,0:T(8,128)(2,1)} %bitcast.5), calls=%async_computation.3 | async-start | bytes 786432 | tf_op jit(solution)/shard_map/all_to_all | solution.py:368
  139.7 12.6 %cross.7 = (bf16[256,8192]{1,0:T(8,128)(2,1)}, bf16[256,768]{1,0:T(8,128)(2,1)}, bf16[256,768]{1,0:T(8,128)(2,1)}) custom-call(s32[1]{0:T(128)} %dynamic_slice.3.flag_ref, bf16[256,8192]{1,0:T(8,128)(2,1)} %get-tuple-element.25.rq_ref, bf16[256,8192]{1,0:T(8,128)(2,1)} %do_ref.9, f32[64,256]{1,0:T(8,128)} %lse_ref.9, ...), custom_call_target="tpu_custom_call", output_to_operand_aliasing={{0}: (10, {})} | custom-call | flops 8053063680 | bytes 9437184 | tf_op jit(solution)/shard_map/cross/pallas_call | solution.py:291
  152.5 11.3 %collective-permute-done.7 = bf16[256,768]{1,0:T(8,128)(2,1)S(1)} collective-permute-done((bf16[256,768]{1,0:T(8,128)(2,1)}, bf16[256,768]{1,0:T(8,128)(2,1)S(1)}, u32[]{:S(2)}, u32[]{:S(2)}) %collective-permute-start.7) | collective-permute-done | bytes 393248 | tf_op jit(solution)/shard_map/ppermute | solution.py:374
  163.8 1.1 add_convert_fusion
  164.9 17.0 %all_to_all.30.refs_2_ = bf16[16,16,768]{2,1,0:T(8,128)(2,1)} all-to-all(bf16[16,16,768]{2,1,0:T(8,128)(2,1)S(1)} %bitcast.16), channel_id=1, replica_groups=mesh['head'=2,'ctx'=16] {'ctx'}, dimensions={0} | all-to-all | bytes 786432 | tf_op jit(solution)/shard_map/all_to_all | solution.py:368
  181.9 2.7 %merge.1 = bf16[16,16,2048]{2,1,0:T(8,128)(2,1)} custom-call(s32[16]{0:T(128)} %get-tuple-element.29.source_ref, s32[16]{0:T(128)} %copy-done.10, bf16[16,16,512]{2,1,0:T(8,128)(2,1)} %copy-done.7, bf16[16,16,768]{2,1,0:T(8,128)(2,1)} %copy-done.5, bf16[16,16,768]{2,1,0:T(8,128)(2,1)} %all_to_all.30.refs_2_), custom_call_target="tpu_custom_call" | custom-call | tf_op jit(solution)/shard_map/merge/pallas_call | solution.py:107
  184.6 3.7 %all-to-all-start.5 = ((bf16[16,16,2048]{2,1,0:T(8,128)(2,1)}), bf16[16,16,2048]{2,1,0:T(8,128)(2,1)S(1)}, u32[]{:S(2)}, u32[]{:S(2)}) async-start(bf16[16,16,2048]{2,1,0:T(8,128)(2,1)} %merge.1), calls=%async_computation.5 | async-start | bytes 2097152 | tf_op jit(solution)/shard_map/all_to_all | solution.py:368
  188.3 1.3 collective-permute-start.4
  189.6 25.9 %collective-permute-done.4.refs_0_ = bf16[256,2048]{1,0:T(8,128)(2,1)S(1)} collective-permute-done((bf16[256,2048]{1,0:T(8,128)(2,1)S(1)}, bf16[256,2048]{1,0:T(8,128)(2,1)S(1)}, u32[]{:S(2)}, u32[]{:S(2)}) %collective-permute-start.4) | collective-permute-done | bytes 1048608 | tf_op jit(solution)/shard_map/ppermute | solution.py:374
  215.5 1.0 copy-done.6
  216.9 3.7 %finish.1 = (bf16[256,1024]{1,0:T(8,128)(2,1)}, bf16[256,1024]{1,0:T(8,128)(2,1)}) custom-call(f32[256,2048]{1,0:T(8,128)} %get-tuple-element.33.own_ref, f32[256,128]{1,0:T(8,128)} %get-tuple-element.52.c_ref, f32[256,128]{1,0:T(8,128)} %get-tuple-element.53.s_ref, bf16[256,2048]{1,0:T(8,128)(2,1)} %copy-done.6, bf16[256,2048]{1,0:T(8,128)(2,1)} %bitcast.9), custom_call_target="tpu_custom_call" | custom-call | tf_op jit(solution)/shard_map/finish/pallas_call | solution.py:331
  (50 shorter events, 6.5 us)
Async XLA Ops:
  0.6 12.3 %copy-start = (s32[16,1]{0,1:T(1,128)S(1)}, s32[16,1]{0,1:T(1,128)}, u32[]{:S(2)}) copy-start(s32[16,1]{0,1:T(1,128)} %param.15) | copy-start | bytes 196
  0.6 12.3 %copy-start.9 = (s32[16]{0:T(128)S(1)}, s32[16]{0:T(128)}, u32[]{:S(2)}) copy-start(s32[16]{0:T(128)} %param.16) | copy-start | bytes 196
  5.4 40.5 %copy-start.4 = (bf16[256,2048]{1,0:T(8,128)(2,1)S(1)}, bf16[256,2048]{1,0:T(8,128)(2,1)}, u32[]{:S(2)}) copy-start(bf16[256,2048]{1,0:T(8,128)(2,1)} %pack.1.kv_ref) | copy-start | bytes 3145732
  5.4 30.4 %all-to-all-start = ((bf16[16,16,2048]{2,1,0:T(8,128)(2,1)}), bf16[16,16,2048]{2,1,0:T(8,128)(2,1)S(1)}, u32[]{:S(2)}, u32[]{:S(2)}) async-start(bf16[16,16,2048]{2,1,0:T(8,128)(2,1)} %bitcast.15), calls=%async_computation | async-start | bytes 2097152 | tf_op jit(solution)/shard_map/all_to_all | solution.py:368
  35.8 1.0 copy-start.2
  39.1 29.8 %all-to-all-start.1 = ((bf16[16,16,2048]{2,1,0:T(8,128)(2,1)}), bf16[16,16,2048]{2,1,0:T(8,128)(2,1)S(1)}, u32[]{:S(2)}, u32[]{:S(2)}) async-start(bf16[16,16,2048]{2,1,0:T(8,128)(2,1)} %pick.1), calls=%async_computation.1 | async-start | bytes 2097152 | tf_op jit(solution)/shard_map/all_to_all | solution.py:368
  45.9 26.9 %collective-permute-start = (bf16[256,2048]{1,0:T(8,128)(2,1)S(1)}, bf16[256,2048]{1,0:T(8,128)(2,1)S(1)}, u32[]{:S(2)}, u32[]{:S(2)}) collective-permute-start(bf16[256,2048]{1,0:T(8,128)(2,1)S(1)} %copy-done.4), channel_id=1, source_target_pairs={{0,16},{1,17},{2,18},{3,19},{4,20},{5,21},{6,22},{7,23},{8,24},{9,... | collective-permute-start | bytes 3145736 | tf_op jit(solution)/shard_map/ppermute | solution.py:374
  49.5 19.4 %copy-start.10 = (s32[16]{0:T(128)}, s32[16]{0:T(128)S(1)}, u32[]{:S(2)}) copy-start(s32[16]{0:T(128)S(1)} %convert_element_type.34.present_ref) | copy-start | bytes 196
  68.9 16.7 %copy-start.3 = (bf16[16,16,2048]{2,1,0:T(8,128)(2,1)}, bf16[16,16,2048]{2,1,0:T(8,128)(2,1)S(1)}, u32[]{:S(2)}) copy-start(bf16[16,16,2048]{2,1,0:T(8,128)(2,1)S(1)} %all-to-all-done.1) | copy-start | bytes 3145732
  69.0 24.6 %collective-permute-start.3 = (bf16[256,512]{1,0:T(8,128)(2,1)S(1)}, bf16[256,512]{1,0:T(8,128)(2,1)}, u32[]{:S(2)}, u32[]{:S(2)}) collective-permute-start(bf16[256,512]{1,0:T(8,128)(2,1)S(1)} %slice.16), channel_id=1, source_target_pairs={{0,16},{16,0},{1,17},{17,1},{2,18},{18,2},{3,19},{19,3},{4,20},{20... | collective-permute-start | bytes 786440 | tf_op jit(solution)/shard_map/ppermute | solution.py:374
  72.8 1.0 copy-start.12
  85.7 17.6 %collective-permute-start.2 = (bf16[256,768]{1,0:T(8,128)(2,1)S(1)}, bf16[256,768]{1,0:T(8,128)(2,1)S(1)}, u32[]{:S(2)}, u32[]{:S(2)}) collective-permute-start(bf16[256,768]{1,0:T(8,128)(2,1)S(1)} %get-tuple-element.47), channel_id=1, source_target_pairs={{0,16},{16,0},{1,17},{17,1},{2,18},{18,2},{3,19},{19,3},{4,20},{20... | collective-permute-start | bytes 1179656 | tf_op jit(solution)/shard_map/ppermute | solution.py:374
  103.2 15.5 %collective-permute-start.6 = (bf16[256,512]{1,0:T(8,128)(2,1)}, bf16[256,512]{1,0:T(8,128)(2,1)S(1)}, u32[]{:S(2)}, u32[]{:S(2)}) collective-permute-start(bf16[256,512]{1,0:T(8,128)(2,1)} %get-tuple-element.38), channel_id=1, source_target_pairs={{0,16},{16,0},{1,17},{17,1},{2,18},{18,2},{3,19},{19,3},{4,20},{20... | collective-permute-start | bytes 786440 | tf_op jit(solution)/shard_map/ppermute | solution.py:374
  103.3 0.7 copy-start.14
  104.0 14.7 %copy-start.8 = (bf16[256,512]{1,0:T(8,128)(2,1)S(1)}, bf16[256,512]{1,0:T(8,128)(2,1)}, u32[]{:S(2)}) copy-start(bf16[256,512]{1,0:T(8,128)(2,1)} %get-tuple-element.37) | copy-start | bytes 786436
  116.7 10.0 %collective-permute-start.5 = (bf16[256,768]{1,0:T(8,128)(2,1)}, bf16[256,768]{1,0:T(8,128)(2,1)S(1)}, u32[]{:S(2)}, u32[]{:S(2)}) collective-permute-start(bf16[256,768]{1,0:T(8,128)(2,1)} %get-tuple-element.36), channel_id=1, source_target_pairs={{0,16},{16,0},{1,17},{17,1},{2,18},{18,2},{3,19},{19,3},{4,20},{20... | collective-permute-start | bytes 1179656 | tf_op jit(solution)/shard_map/ppermute | solution.py:374
  119.5 15.7 %all-to-all-start.2 = ((bf16[16,16,512]{2,1,0:T(8,128)(2,1)}), bf16[16,16,512]{2,1,0:T(8,128)(2,1)S(1)}, u32[]{:S(2)}, u32[]{:S(2)}) async-start(bf16[16,16,512]{2,1,0:T(8,128)(2,1)} %bitcast.4), calls=%async_computation.2 | async-start | bytes 524288 | tf_op jit(solution)/shard_map/all_to_all | solution.py:368
  125.2 13.8 %collective-permute-start.1 = (bf16[256,768]{1,0:T(8,128)(2,1)S(1)}, bf16[256,768]{1,0:T(8,128)(2,1)S(1)}, u32[]{:S(2)}, u32[]{:S(2)}) collective-permute-start(bf16[256,768]{1,0:T(8,128)(2,1)S(1)} %get-tuple-element.48), channel_id=1, source_target_pairs={{0,16},{16,0},{1,17},{17,1},{2,18},{18,2},{3,19},{19,3},{4,20},{20... | collective-permute-start | bytes 1179656 | tf_op jit(solution)/shard_map/ppermute | solution.py:374
  135.2 17.1 %copy-start.7 = (bf16[16,16,512]{2,1,0:T(8,128)(2,1)}, bf16[16,16,512]{2,1,0:T(8,128)(2,1)S(1)}, u32[]{:S(2)}) copy-start(bf16[16,16,512]{2,1,0:T(8,128)(2,1)S(1)} %all-to-all-done.2.refs_0_) | copy-start | bytes 786436
  135.2 29.7 %all-to-all-start.3 = ((bf16[16,16,768]{2,1,0:T(8,128)(2,1)}), bf16[16,16,768]{2,1,0:T(8,128)(2,1)S(1)}, u32[]{:S(2)}, u32[]{:S(2)}) async-start(bf16[16,16,768]{2,1,0:T(8,128)(2,1)} %bitcast.5), calls=%async_computation.3 | async-start | bytes 786432 | tf_op jit(solution)/shard_map/all_to_all | solution.py:368
  139.0 0.7 copy-start.13
  152.4 35.9 %copy-start.11 = (bf16[256,2048]{1,0:T(8,128)(2,1)S(1)}, bf16[256,2048]{1,0:T(8,128)(2,1)}, u32[]{:S(2)}) copy-start(bf16[256,2048]{1,0:T(8,128)(2,1)} %get-tuple-element.34) | copy-start | bytes 3145732
  152.4 11.4 %collective-permute-start.7 = (bf16[256,768]{1,0:T(8,128)(2,1)}, bf16[256,768]{1,0:T(8,128)(2,1)S(1)}, u32[]{:S(2)}, u32[]{:S(2)}) collective-permute-start(bf16[256,768]{1,0:T(8,128)(2,1)} %get-tuple-element.41), channel_id=1, source_target_pairs={{0,16},{16,0},{1,17},{17,1},{2,18},{18,2},{3,19},{19,3},{4,20},{20... | collective-permute-start | bytes 1179656 | tf_op jit(solution)/shard_map/ppermute | solution.py:374
  164.9 17.0 %copy-start.5 = (bf16[16,16,768]{2,1,0:T(8,128)(2,1)}, bf16[16,16,768]{2,1,0:T(8,128)(2,1)S(1)}, u32[]{:S(2)}) copy-start(bf16[16,16,768]{2,1,0:T(8,128)(2,1)S(1)} %all-to-all-done.3.refs_1_) | copy-start | bytes 1179652
  184.6 30.9 %all-to-all-start.5 = ((bf16[16,16,2048]{2,1,0:T(8,128)(2,1)}), bf16[16,16,2048]{2,1,0:T(8,128)(2,1)S(1)}, u32[]{:S(2)}, u32[]{:S(2)}) async-start(bf16[16,16,2048]{2,1,0:T(8,128)(2,1)} %merge.1), calls=%async_computation.5 | async-start | bytes 2097152 | tf_op jit(solution)/shard_map/all_to_all | solution.py:368
  188.3 27.2 %collective-permute-start.4 = (bf16[256,2048]{1,0:T(8,128)(2,1)S(1)}, bf16[256,2048]{1,0:T(8,128)(2,1)S(1)}, u32[]{:S(2)}, u32[]{:S(2)}) collective-permute-start(bf16[256,2048]{1,0:T(8,128)(2,1)S(1)} %copy-done.11), channel_id=1, source_target_pairs={{16,0},{17,1},{18,2},{19,3},{20,4},{21,5},{22,6},{23,7},{24,8},{25... | collective-permute-start | bytes 3145736 | tf_op jit(solution)/shard_map/ppermute | solution.py:374
  215.5 1.0 copy-start.6
  215.5 1.3 copy-start.1

commit v2 on v1

--- a/solution.py
+++ b/solution.py
@@ -15,7 +15,7 @@
 LN2 = math.log(2.0)
 SCALE = 1.0 / math.sqrt(HEAD_SIZE)
 rope_base = 500000.0
-VMEM_LIMIT = 60 * 1024 * 1024
+MIB = 1024 * 1024
 NT = (((1,), (1,)), ((), ()))
 NN = (((1,), (0,)), ((), ()))
 TN = (((0,), (0,)), ((), ()))
@@ -42,51 +42,70 @@
     return x * c - pltpu.roll(x, HEAD_SIZE // 2, 1) * s
 
 
-def params(n=1):
+def params(n, mib):
     return pltpu.CompilerParams(
-        dimension_semantics=("arbitrary",) * n, vmem_limit_bytes=VMEM_LIMIT
+        dimension_semantics=("arbitrary",) * n, vmem_limit_bytes=mib * MIB
     )
 
 
-def pack_kernel(k_ref, v_ref, c_ref, s_ref, o_ref):
-    c, s = c_ref[...], s_ref[...]
+def pair_kernel(k_ref, v_ref, o_ref):
     for g in range(k_ref.shape[1] // HEAD_SIZE):
         a, b = g * HEAD_SIZE, 2 * g * HEAD_SIZE
-        x = k_ref[:, a : a + HEAD_SIZE].astype(jnp.float32)
-        o_ref[:, b : b + HEAD_SIZE] = turn(x, c, s).astype(jnp.bfloat16)
+        o_ref[:, b : b + HEAD_SIZE] = k_ref[:, a : a + HEAD_SIZE]
         o_ref[:, b + HEAD_SIZE : b + 2 * HEAD_SIZE] = v_ref[:, a : a + HEAD_SIZE]
 
 
-def pack(keys, values, c, s):
+def turn_keys_kernel(x_ref, c_ref, s_ref, o_ref):
+    c, s = c_ref[...], s_ref[...]
+    for b in range(0, x_ref.shape[1], 2 * HEAD_SIZE):
+        k, v = slice(b, b + HEAD_SIZE), slice(b + HEAD_SIZE, b + 2 * HEAD_SIZE)
+        o_ref[:, k] = turn(x_ref[:, k].astype(jnp.float32), c, s).astype(jnp.bfloat16)
+        o_ref[:, v] = x_ref[:, v]
+
+
+def pair(keys, values):
     rows, width = keys.shape
     return pl.pallas_call(
-        pack_kernel,
+        pair_kernel,
         out_shape=jax.ShapeDtypeStruct((rows, 2 * width), jnp.bfloat16),
-        compiler_params=params(0),
-        name="pack",
-    )(keys, values, c, s)
-
-
-def pick_kernel(source_ref, x_ref, o_ref):
+        compiler_params=params(0, 6),
+        name="pair",
+    )(keys, values)
+
+
+def turn_keys(x, c, s):
+    return pl.pallas_call(
+        turn_keys_kernel,
+        out_shape=jax.ShapeDtypeStruct(x.shape, x.dtype),
+        compiler_params=params(0, 6),
+        name="turn_keys",
+    )(x, c, s)
+
+
+def pick_kernel(source_ref, x_ref, c_ref, s_ref, o_ref):
     for d in range(x_ref.shape[0]):
-        o_ref[d] = x_ref[source_ref[d]]
-
-
-def pick(source, x):
+        at = source_ref[d]
+        c, s = c_ref[at], s_ref[at]
+        for b in range(0, x_ref.shape[2], 2 * HEAD_SIZE):
+            k, v = slice(b, b + HEAD_SIZE), slice(b + HEAD_SIZE, b + 2 * HEAD_SIZE)
+            x = x_ref[at, :, k].astype(jnp.float32)
+            o_ref[d, :, k] = turn(x, c, s).astype(jnp.bfloat16)
+            o_ref[d, :, v] = x_ref[at, :, v]
+
+
+def pick(source, x, c, s):
     return pl.pallas_call(
         pick_kernel,
         out_shape=jax.ShapeDtypeStruct(x.shape, x.dtype),
-        in_specs=[
-            pl.BlockSpec(memory_space=pltpu.SMEM),
-            pl.BlockSpec(memory_space=pltpu.VMEM),
-        ],
+        in_specs=[pl.BlockSpec(memory_space=pltpu.SMEM)]
+        + [pl.BlockSpec(memory_space=pltpu.VMEM)] * 3,
         out_specs=pl.BlockSpec(memory_space=pltpu.VMEM),
-        compiler_params=params(0),
+        compiler_params=params(0, 8),
         name="pick",
-    )(source, x)
-
-
-def merge_kernel(source_ref, present_ref, *refs):
+    )(source, x, c, s)
+
+
+def merge_kernel(source_ref, present_ref, c_ref, s_ref, *refs):
     *x_refs, o_ref, acc_ref = refs
     acc_ref[...] = jnp.zeros_like(acc_ref)
     for d in range(o_ref.shape[0]):
@@ -99,21 +118,26 @@
                 acc_ref[source_ref[d], :, at : at + width] += x_ref[d].astype(jnp.float32)
                 at += width
 
-    o_ref[...] = acc_ref[...].astype(o_ref.dtype)
-
-
-def merge(source, present, xs):
+    for d in range(o_ref.shape[0]):
+        c, s = c_ref[d], s_ref[d]
+        for b in range(0, o_ref.shape[2], 2 * HEAD_SIZE):
+            k, v = slice(b, b + HEAD_SIZE), slice(b + HEAD_SIZE, b + 2 * HEAD_SIZE)
+            o_ref[d, :, k] = turn_back(acc_ref[d, :, k], c, s).astype(o_ref.dtype)
+            o_ref[d, :, v] = acc_ref[d, :, v].astype(o_ref.dtype)
+
+
+def merge(source, present, c, s, xs):
     shape = xs[0].shape[:2] + (sum(x.shape[2] for x in xs),)
     return pl.pallas_call(
         merge_kernel,
         out_shape=jax.ShapeDtypeStruct(shape, xs[0].dtype),
         in_specs=[pl.BlockSpec(memory_space=pltpu.SMEM)] * 2
-        + [pl.BlockSpec(memory_space=pltpu.VMEM)] * len(xs),
+        + [pl.BlockSpec(memory_space=pltpu.VMEM)] * (2 + len(xs)),
         out_specs=pl.BlockSpec(memory_space=pltpu.VMEM),
         scratch_shapes=[pltpu.VMEM(shape, jnp.float32)],
-        compiler_params=params(0),
+        compiler_params=params(0, 10),
         name="merge",
-    )(source, present, *xs)
+    )(source, present, c, s, *xs)
 
 
 def fronts(rq, do, lse, delta, k, v, mask=None):
@@ -185,7 +209,7 @@
         in_specs=[big, big, big, row, table, table, pair],
         out_specs=[part, part_row, part, pair],
         scratch_shapes=[pltpu.VMEM((rows, group * rows), jnp.bfloat16)] * 2,
-        compiler_params=params(),
+        compiler_params=params(1, 24),
         cost_estimate=pl.CostEstimate(
             flops=20 * count * group * rows * rows * HEAD_SIZE,
             bytes_accessed=rows * count * wide * 12,
@@ -260,9 +284,8 @@
             dq_ref[:, cols] = turn_back(total_ref[:, cols], c, s).astype(jnp.bfloat16)
 
 
-def cross(first, count, flags, joint, rq, do, lse, delta, c, s, dq, kvs, whole=None, final=False):
+def cross(kv_count, first, count, flags, joint, rq, do, lse, delta, c, s, dq, kvs, whole=None, final=False):
     rows, width = do.shape
-    kv_count = kvs[0].shape[1] // (2 * HEAD_SIZE)
     group = heads_of(width, kv_count)
     wide = group * HEAD_SIZE
     most = max(joint)
@@ -273,7 +296,8 @@
     shifted = pl.BlockSpec((rows, 2 * HEAD_SIZE), lambda g, i: (0, g + first))
     args = [flags, rq, do, lse, delta, c, s, dq, *kvs]
     in_specs = [big, big, row, row, table, table, big]
-    in_specs += [shifted if x.shape == kvs[0].shape else pair for x in kvs]
+    chunk_width = count * 2 * HEAD_SIZE
+    in_specs += [pair if x.shape[1] == chunk_width else shifted for x in kvs]
     mode = 0
     aliases = {}
     if final:
@@ -302,7 +326,7 @@
             + ([pltpu.VMEM((rows, wide), jnp.float32)] if final else []),
         ),
         input_output_aliases=aliases,
-        compiler_params=params(),
+        compiler_params=params(1, 24),
         cost_estimate=pl.CostEstimate(
             flops=20 * count * group * rows * rows * HEAD_SIZE * len(kvs),
             bytes_accessed=rows * count * wide * 12,
@@ -312,28 +336,45 @@
     )(*args)
 
 
-def finish_kernel(parts, own_ref, c_ref, s_ref, *refs):
-    in_refs = refs[:parts]
-    dk_ref, dv_ref = refs[parts:]
+def settle_kernel(own_ref, c_ref, s_ref, *refs):
+    *in_refs, o_ref = refs
     c, s = c_ref[...], s_ref[...]
+    for b in range(0, o_ref.shape[1], 2 * HEAD_SIZE):
+        k, v = slice(b, b + HEAD_SIZE), slice(b + HEAD_SIZE, b + 2 * HEAD_SIZE)
+        gk, gv = own_ref[:, k], own_ref[:, v]
+        for ref in in_refs:
+            gk = gk + ref[:, k].astype(jnp.float32)
+            gv = gv + ref[:, v].astype(jnp.float32)
+        o_ref[:, k] = turn_back(gk, c, s)
+        o_ref[:, v] = gv
+
+
+def settle(local, parts, c, s):
+    return pl.pallas_call(
+        settle_kernel,
+        out_shape=jax.ShapeDtypeStruct(local.shape, jnp.float32),
+        compiler_params=params(0, 12),
+        name="settle",
+    )(local, c, s, *parts)
+
+
+def finish_kernel(own_ref, children_ref, dk_ref, dv_ref):
     for g in range(dk_ref.shape[1] // HEAD_SIZE):
         a, b = g * HEAD_SIZE, 2 * g * HEAD_SIZE
         total = own_ref[:, b : b + 2 * HEAD_SIZE]
-        for ref in in_refs:
-            total = total + ref[:, b : b + 2 * HEAD_SIZE].astype(jnp.float32)
-        gk = total[:, :HEAD_SIZE]
-        dk_ref[:, a : a + HEAD_SIZE] = turn_back(gk, c, s).astype(jnp.bfloat16)
+        total = total + children_ref[:, b : b + 2 * HEAD_SIZE].astype(jnp.float32)
+        dk_ref[:, a : a + HEAD_SIZE] = total[:, :HEAD_SIZE].astype(jnp.bfloat16)
         dv_ref[:, a : a + HEAD_SIZE] = total[:, HEAD_SIZE:].astype(jnp.bfloat16)
 
 
-def finish(local, parts, c, s):
-    rows, width = local.shape
-    return pl.pallas_call(
-        functools.partial(finish_kernel, len(parts)),
+def finish(base, children):
+    rows, width = base.shape
+    return pl.pallas_call(
+        finish_kernel,
         out_shape=[jax.ShapeDtypeStruct((rows, width // 2), jnp.bfloat16)] * 2,
-        compiler_params=params(0),
+        compiler_params=params(0, 8),
         name="finish",
-    )(local, c, s, *parts)
+    )(base, children)
 
 
 def body(
@@ -359,7 +400,8 @@
     source = jnp.argmax(match, axis=1).astype(jnp.int32)
     present = jnp.any(match, axis=1).astype(jnp.int32)
 
-    sizes = split(unrotated_keys.shape[1] // HEAD_SIZE)
+    kv_count = unrotated_keys.shape[1] // HEAD_SIZE
+    sizes = split(kv_count)
     chunks = range(len(sizes))
     firsts = [sum(sizes[:g]) for g in chunks]
 
@@ -373,51 +415,70 @@
         route = [(i, (i + n) % hops) for i in range(hops) if wrap or 0 <= i + n < hops]
         return lax.ppermute(x, "head", route)
 
-    kv = pack(unrotated_keys, value_rows, c, s)
+    raw = pair(unrotated_keys, value_rows)
     own_flags = jnp.stack([(me >= n).astype(jnp.int32) for n in range(1, hops)])
     parent_flag = present[here][None]
-    own_sets, parent_sets = (1,) * (hops - 1), (hops,)
-
-    middle = exchange(kv)
+
+    piece_rows = rows // places
+    offset = me * rows + here * piece_rows + jnp.arange(piece_rows, dtype=jnp.int32)
+    middle_at = (TREE_BLOCK * placement[:, None] + offset[None, :]).reshape(-1)
+    middle_c, middle_s = [
+        t.reshape(places, piece_rows, HEAD_SIZE) for t in rope_tables(middle_at)
+    ]
+
+    middle = exchange(raw)
+    kv = turn_keys(raw, c, s)
     own_kv = [shift(kv, n, False) for n in range(1, hops)]
     rq, delta, dq, local = diagonal(
         queries, output_gradient, outputs, saved_logsumexp, c, s, kv
     )
-    picked = pick(source, middle)
+    picked = pick(source, middle, middle_c, middle_s)
     near = exchange(picked).reshape(rows, -1)
     dq, *own_part = cross(
-        0, sum(sizes), own_flags, own_sets, rq, output_gradient,
+        kv_count, 0, kv_count, own_flags, (1,) * (hops - 1), rq, output_gradient,
         saved_logsumexp, delta, c, s, dq, own_kv,
     )
     back = [shift(own_part[n - 1], -n, False) for n in range(1, hops)]
+    base = settle(local, back, c, s)
+
+    far = []
+    for g in chunks:
+        at = 2 * HEAD_SIZE * firsts[g]
+        piece = near[:, at : at + 2 * HEAD_SIZE * sizes[g]]
+        far.append([shift(piece, n, True) for n in range(1, hops)])
+
+    def tiles(g, dq, kvs, whole, final):
+        return cross(
+            kv_count, firsts[g], sizes[g], parent_flag, (len(kvs),), rq, output_gradient,
+            saved_logsumexp, delta, c, s, dq, kvs, whole, final,
+        )
+
     grad_queries = None
     ups = []
     for g in chunks:
-        at = 2 * HEAD_SIZE * firsts[g]
-        piece = near[:, at : at + 2 * HEAD_SIZE * sizes[g]]
-        parent_kv = [near] + [shift(piece, n, True) for n in range(1, hops)]
-        grad_queries, *part = cross(
-            firsts[g], sizes[g], parent_flag, parent_sets, rq, output_gradient,
-            saved_logsumexp, delta, c, s, dq, parent_kv, grad_queries, True,
-        )
-        far_part = [shift(part[n], -n, True) for n in range(1, hops)]
-        total = part[0].astype(jnp.float32)
-        for x in far_part:
+        part = dq
+        if g == 0:
+            part, near_part = tiles(g, part, [near], None, False)
+        part, *far_part = tiles(g, part, far[g], grad_queries, g == 0)
+        if g:
+            part, near_part = tiles(g, part, [near], grad_queries, True)
+        grad_queries = part
+        joined = [shift(x, -n - 1, True) for n, x in enumerate(far_part)]
+        total = near_part.astype(jnp.float32)
+        for x in joined:
             total = total + x.astype(jnp.float32)
         send = total.astype(jnp.bfloat16)
         if g:
             send, ups[-1] = lax.optimization_barrier((send, ups[-1]))
         ups.append(exchange(send))
-    merged = merge(source, present, ups)
+    merged = merge(source, present, middle_c, middle_s, ups)
     children = exchange(merged).reshape(rows, -1)
-    grad_keys, grad_values = finish(local, back + [children], c, s)
+    grad_keys, grad_values = finish(base, children)
     return (grad_queries, grad_keys, grad_values)
 
 
 def split(kv_count):
-    first = kv_count // 4
-    second = (kv_count - first) // 2
-    return (first, second, kv_count - first - second)
+    return (kv_count // 2, kv_count - kv_count // 2)
 
 
 def solution(mesh):

time: 222 us -> 237 us (1.068)
  local copies, waits for them, and re-layouts: 6.16 us -> 36.5 us
  Pallas kernels: 76.9 us -> 67.3 us
  other arithmetic: 6.84 us -> 3.58 us
  waiting for transfers between devices: 69.2 us -> 66.2 us
    unnamed x30 -> x60, local copies, waits for them, and re-layouts: 4.77 us -> 34.3 us
    pallas_call x4 -> x5, Pallas kernels: 46.8 us -> 39.2 us  [cross(): pl.pallas_call(functools.partial(cross_kernel, group, joint, mode), out_s...]
    all_to_all x5 -> x4, waiting for transfers between devices: 28.1 us -> 20.6 us  [exchange(): lax.all_to_all(x.reshape(places, rows // places, width), 'ctx', 0, 0, til...]
    ppermute x8 -> x6, waiting for transfers between devices: 41.1 us -> 45.5 us  [shift(): return lax.ppermute(x, 'head', route)]
    all_to_all x5 -> x4, starting transfers between devices: 27.4 us -> 23.6 us  [exchange(): lax.all_to_all(x.reshape(places, rows // places, width), 'ctx', 0, 0, til...]
    ppermute x8 -> x6, starting transfers between devices: 16.2 us -> 19.1 us  [shift(): return lax.ppermute(x, 'head', route)]
    convert_element_type x3 -> x2, other arithmetic: 3.79 us -> 1.18 us  [body(): send = total.astype(jnp.bfloat16)]
    pallas_call x2 -> x4, Pallas kernels: 6.31 us -> 5.65 us  [the longest x1 2.67 us: turn_keys(): pl.pallas_call(turn_keys_kernel, out_shape=jax.ShapeDtypeStruct(x.shape,...]
  transfers between devices with their start and end apart: 13 -> 10, of which waited for: 6 -> 5; matrix products, arithmetic and copies ran while one was open for 3% -> 2% of each run, Pallas kernels for 30% -> 22%
where the time goes in v2:
time: 237 us; the launch traced here: 236 us
  Pallas kernels  67.3 us (28%)
  waiting for transfers between devices  66.2 us (28%)
  starting transfers between devices  42.7 us (18%)
  local copies, waits for them, and re-layouts  36.5 us (15%)
  blocking collectives  18.6 us (8%)
  other arithmetic  3.58 us (2%)
    ppermute x6, waiting for transfers between devices, shift(): return lax.ppermute(x, 'head', route)  45.5 us
    pallas_call x5, Pallas kernels, cross(): pl.pallas_call(functools.partial(cross_kernel, group, joint, mode), out_s...  39.2 us
    unnamed x60, local copies, waits for them, and re-layouts  34.3 us
    all_to_all x4, starting transfers between devices, exchange(): lax.all_to_all(x.reshape(places, rows // places, width), 'ctx', 0, 0, til...  23.6 us
    all_to_all x4, waiting for transfers between devices, exchange(): lax.all_to_all(x.reshape(places, rows // places, width), 'ctx', 0, 0, til...  20.6 us
    ppermute x6, starting transfers between devices, shift(): return lax.ppermute(x, 'head', route)  19.1 us
    all_to_all x1, blocking collectives, exchange(): lax.all_to_all(x.reshape(places, rows // places, width), 'ctx', 0, 0, til...  18.6 us
    pallas_call x1, Pallas kernels, diagonal(): pl.pallas_call(functools.partial(diagonal_kernel, group), out_shape=[jax....  18.2 us
  transfers between devices with their start and end apart: 10, of which 5 were waited for; matrix products, arithmetic and copies ran while one was open for 2% of the time, Pallas kernels for 22%

profile of v2, /device:TPU:0, one launch (start us, length us, event | category | flops | bytes accessed | tf_op | source)
XLA Modules:
  0.0 235.9 jit_solution(4387856063048653158)
XLA Ops:
  3.9 7.5 %all-to-all-start = ((bf16[16,16,2048]{2,1,0:T(8,128)(2,1)}), bf16[16,16,2048]{2,1,0:T(8,128)(2,1)S(1)}, u32[]{:S(2)}, u32[]{:S(2)}) async-start(bf16[16,16,2048]{2,1,0:T(8,128)(2,1)} %bitcast.2), calls=%async_computation | async-start | bytes 2097152 | tf_op jit(solution)/shard_map/all_to_all | solution.py:410
  13.7 20.6 %all-to-all-done.x_ref = bf16[16,16,2048]{2,1,0:T(8,128)(2,1)S(1)} async-done(((bf16[16,16,2048]{2,1,0:T(8,128)(2,1)}), bf16[16,16,2048]{2,1,0:T(8,128)(2,1)S(1)}, u32[]{:S(2)}, u32[]{:S(2)}) %all-to-all-start) | async-done | bytes 1048608 | tf_op jit(solution)/shard_map/all_to_all | solution.py:410
  34.4 1.9 pick.1
  36.2 6.8 %all-to-all-start.1 = ((bf16[16,16,2048]{2,1,0:T(8,128)(2,1)}), bf16[16,16,2048]{2,1,0:T(8,128)(2,1)S(1)}, u32[]{:S(2)}, u32[]{:S(2)}) async-start(bf16[16,16,2048]{2,1,0:T(8,128)(2,1)} %pick.1), calls=%async_computation.1 | async-start | bytes 2097152 | tf_op jit(solution)/shard_map/all_to_all | solution.py:410
  43.7 2.7 %turn_keys.1.kv_ref = bf16[256,2048]{1,0:T(8,128)(2,1)} custom-call(bf16[256,2048]{1,0:T(8,128)(2,1)} %pair.1.x_ref, f32[256,128]{1,0:T(8,128)S(1)} %get-tuple-element.51.c_ref, f32[256,128]{1,0:T(8,128)S(1)} %get-tuple-element.52.s_ref), custom_call_target="tpu_custom_call" | custom-call | tf_op jit(solution)/shard_map/turn_keys/pallas_call | solution.py:77
  46.4 4.4 %collective-permute-start = (bf16[256,2048]{1,0:T(8,128)(2,1)}, bf16[256,2048]{1,0:T(8,128)(2,1)}, u32[]{:S(2)}, u32[]{:S(2)}) collective-permute-start(bf16[256,2048]{1,0:T(8,128)(2,1)} %turn_keys.1.kv_ref), channel_id=1, source_target_pairs={{0,16},{1,17},{2,18},{3,19},{4,20},{5,21},{6,22},{7,23},{8,24},{9,... | collective-permute-start | bytes 3145736 | tf_op jit(solution)/shard_map/ppermute | solution.py:416
  51.6 2.2 copy-done.2
  54.6 2.2 copy-done.20
  56.8 2.2 copy-done.21
  59.0 18.2 %diagonal.1 = (bf16[256,8192]{1,0:T(8,128)(2,1)S(1)}, f32[64,256]{1,0:T(8,128)S(1)}, f32[256,8192]{1,0:T(8,128)S(1)}, f32[256,2048]{1,0:T(8,128)S(1)}) custom-call(bf16[256,8192]{1,0:T(8,128)(2,1)S(1)} %copy-done.20, bf16[256,8192]{1,0:T(8,128)(2,1)S(1)} %copy-done.2, bf16[256,8192]{1,0:T(8,128)(2,1)S(1)} %copy-done.21, f32[64,256]{1,0:T(8,128)S(1)} %copy-done.14, ...), custom_call_target="tpu_custom_call" | custom-call | flops 10737418240 | bytes 25165824 | tf_op jit(solution)/shard_map/diagonal/pallas_call | solution.py:200
  77.2 2.0 copy-done.5
  79.9 3.3 %copy-done.26 = f32[256,8192]{1,0:T(8,128)} copy-done((f32[256,8192]{1,0:T(8,128)}, f32[256,8192]{1,0:T(8,128)S(1)}, u32[]{:S(2)}) %copy-start.26) | copy-done | bytes 8388632
  84.1 2.2 copy-done.3
  86.3 2.2 copy-done.6
  90.2 3.4 %copy-done.27 = f32[256,8192]{1,0:T(8,128)S(1)} copy-done((f32[256,8192]{1,0:T(8,128)S(1)}, f32[256,8192]{1,0:T(8,128)}, u32[]{:S(2)}) %copy-start.27) | copy-done | bytes 8388632
  93.6 5.6 %cross.5 = (f32[256,8192]{1,0:T(8,128)S(1)}, bf16[256,2048]{1,0:T(8,128)(2,1)S(1)}) custom-call(s32[1]{0:T(128)} %bitcast.1.flag_ref, bf16[256,8192]{1,0:T(8,128)(2,1)S(1)} %copy-done.6, bf16[256,8192]{1,0:T(8,128)(2,1)S(1)} %copy-done.3, f32[64,256]{1,0:T(8,128)S(1)} %copy-done.15, f32[64,256]{1,0:T(8,128)S(1)} %copy-done.18, ...), custom_call_target="tpu_custom_call" | custom-call | flops 10737418240 | bytes 25165824 | tf_op jit(solution)/shard_map/cross/pallas_call | solution.py:315
  99.2 7.9 %cross.7 = (f32[256,8192]{1,0:T(8,128)S(1)}, bf16[256,1024]{1,0:T(8,128)(2,1)S(1)}) custom-call(s32[1]{0:T(128)} %dynamic_slice.3.flag_ref, bf16[256,8192]{1,0:T(8,128)(2,1)S(1)} %copy-done.6, bf16[256,8192]{1,0:T(8,128)(2,1)S(1)} %copy-done.3, f32[64,256]{1,0:T(8,128)S(1)} %copy-done.15, f32[64,256]{1,0:T(8,128)S(1)} %copy-done.18, ...), custom_call_target="tpu_custom_call" | custom-call | flops 5368709120 | bytes 12582912 | tf_op jit(solution)/shard_map/cross/pallas_call | solution.py:315
  107.2 8.9 %cross.8 = (bf16[256,8192]{1,0:T(8,128)(2,1)}, bf16[256,1024]{1,0:T(8,128)(2,1)S(1)}) custom-call(s32[1]{0:T(128)} %dynamic_slice.3.flag_ref, bf16[256,8192]{1,0:T(8,128)(2,1)S(1)} %copy-done.6, bf16[256,8192]{1,0:T(8,128)(2,1)S(1)} %copy-done.3, f32[64,256]{1,0:T(8,128)S(1)} %copy-done.15, f32[64,256]{1,0:T(8,128)S(1)} %copy-done.18, ...), custom_call_target="tpu_custom_call" | custom-call | flops 5368709120 | bytes 12582912 | tf_op jit(solution)/shard_map/cross/pallas_call | solution.py:315
  116.1 11.6 %collective-permute-start.5 = (bf16[256,1024]{1,0:T(8,128)(2,1)S(1)}, bf16[256,1024]{1,0:T(8,128)(2,1)S(1)}, u32[]{:S(2)}, u32[]{:S(2)}) collective-permute-start(bf16[256,1024]{1,0:T(8,128)(2,1)S(1)} %get-tuple-element.36), channel_id=1, source_target_pairs={{0,16},{16,0},{1,17},{17,1},{2,18},{18,2},{3,19},{19,3},{4,20},{20... | collective-permute-start | bytes 1572872 | tf_op jit(solution)/shard_map/ppermute | solution.py:416
  127.7 12.7 %collective-permute-done.5 = bf16[256,1024]{1,0:T(8,128)(2,1)S(1)} collective-permute-done((bf16[256,1024]{1,0:T(8,128)(2,1)S(1)}, bf16[256,1024]{1,0:T(8,128)(2,1)S(1)}, u32[]{:S(2)}, u32[]{:S(2)}) %collective-permute-start.5) | collective-permute-done | bytes 524320 | tf_op jit(solution)/shard_map/ppermute | solution.py:416
  141.4 5.1 %all-to-all-start.2 = ((bf16[16,16,1024]{2,1,0:T(8,128)(2,1)}), bf16[16,16,1024]{2,1,0:T(8,128)(2,1)S(1)}, u32[]{:S(2)}, u32[]{:S(2)}) async-start(bf16[16,16,1024]{2,1,0:T(8,128)(2,1)} %bitcast.4), calls=%async_computation.2 | async-start | bytes 1048576 | tf_op jit(solution)/shard_map/all_to_all | solution.py:410
  146.6 4.3 %collective-permute-done.1.refs_0_ = bf16[256,1024]{1,0:T(8,128)(2,1)S(1)} collective-permute-done((bf16[256,1024]{1,0:T(8,128)(2,1)}, bf16[256,1024]{1,0:T(8,128)(2,1)S(1)}, u32[]{:S(2)}, u32[]{:S(2)}) %collective-permute-start.1) | collective-permute-done | bytes 524320 | tf_op jit(solution)/shard_map/ppermute | solution.py:416
  150.8 2.2 copy-done.4
  153.0 2.2 copy-done.7
  155.2 3.4 %copy-done.25 = f32[256,8192]{1,0:T(8,128)S(1)} copy-done((f32[256,8192]{1,0:T(8,128)S(1)}, f32[256,8192]{1,0:T(8,128)}, u32[]{:S(2)}) %copy-start.25) | copy-done | bytes 8388632
  158.6 8.0 %cross.6 = (f32[256,8192]{1,0:T(8,128)S(1)}, bf16[256,1024]{1,0:T(8,128)(2,1)S(1)}) custom-call(s32[1]{0:T(128)} %dynamic_slice.3.flag_ref, bf16[256,8192]{1,0:T(8,128)(2,1)S(1)} %copy-done.7, bf16[256,8192]{1,0:T(8,128)(2,1)S(1)} %copy-done.4, f32[64,256]{1,0:T(8,128)S(1)} %copy-done.16, f32[64,256]{1,0:T(8,128)S(1)} %copy-done.19, ...), custom_call_target="tpu_custom_call" | custom-call | flops 5368709120 | bytes 12582912 | tf_op jit(solution)/shard_map/cross/pallas_call | solution.py:315
  168.4 8.9 %cross.9 = (bf16[256,8192]{1,0:T(8,128)(2,1)}, bf16[256,1024]{1,0:T(8,128)(2,1)S(1)}) custom-call(s32[1]{0:T(128)} %dynamic_slice.3.flag_ref, bf16[256,8192]{1,0:T(8,128)(2,1)S(1)} %copy-done.7, bf16[256,8192]{1,0:T(8,128)(2,1)S(1)} %copy-done.4, f32[64,256]{1,0:T(8,128)S(1)} %copy-done.16, ...), custom_call_target="tpu_custom_call", output_to_operand_aliasing={{0}: (9, {})} | custom-call | flops 5368709120 | bytes 12582912 | tf_op jit(solution)/shard_map/cross/pallas_call | solution.py:315
  177.3 2.4 %collective-permute-done.4 = bf16[256,1024]{1,0:T(8,128)(2,1)S(1)} collective-permute-done((bf16[256,1024]{1,0:T(8,128)(2,1)S(1)}, bf16[256,1024]{1,0:T(8,128)(2,1)S(1)}, u32[]{:S(2)}, u32[]{:S(2)}) %collective-permute-start.4) | collective-permute-done | bytes 524320 | tf_op jit(solution)/shard_map/ppermute | solution.py:416
  179.9 18.6 %all_to_all.25.refs_1_ = bf16[16,16,1024]{2,1,0:T(8,128)(2,1)S(1)} all-to-all(bf16[16,16,1024]{2,1,0:T(8,128)(2,1)S(1)} %bitcast.12), channel_id=1, replica_groups=mesh['head'=2,'ctx'=16] {'ctx'}, dimensions={0} | all-to-all | bytes 1048576 | tf_op jit(solution)/shard_map/all_to_all | solution.py:410
  198.5 2.3 merge.1
  200.9 4.2 %all-to-all-start.4 = ((bf16[16,16,2048]{2,1,0:T(8,128)(2,1)}), bf16[16,16,2048]{2,1,0:T(8,128)(2,1)S(1)}, u32[]{:S(2)}, u32[]{:S(2)}) async-start(bf16[16,16,2048]{2,1,0:T(8,128)(2,1)} %merge.1), calls=%async_computation.4 | async-start | bytes 2097152 | tf_op jit(solution)/shard_map/all_to_all | solution.py:410
  206.3 26.1 %collective-permute-done.3.refs_0_ = bf16[256,2048]{1,0:T(8,128)(2,1)S(1)} collective-permute-done((bf16[256,2048]{1,0:T(8,128)(2,1)S(1)}, bf16[256,2048]{1,0:T(8,128)(2,1)S(1)}, u32[]{:S(2)}, u32[]{:S(2)}) %collective-permute-start.3) | collective-permute-done | bytes 1048608 | tf_op jit(solution)/shard_map/ppermute | solution.py:416
  (79 shorter events, 18.8 us)
Async XLA Ops:
  0.6 10.9 %copy-start = (s32[16,1]{0,1:T(1,128)S(1)}, s32[16,1]{0,1:T(1,128)}, u32[]{:S(2)}) copy-start(s32[16,1]{0,1:T(1,128)} %param.15) | copy-start | bytes 196
  2.7 8.7 %copy-start.28 = (s32[16]{0:T(128)S(1)}, s32[16]{0:T(128)}, u32[]{:S(2)}) copy-start(s32[16]{0:T(128)} %param.16) | copy-start | bytes 196
  3.9 39.1 %copy-start.29 = (s32[256]{0:T(256)S(1)}, s32[256]{0:T(256)}, u32[]{:S(2)}) copy-start(s32[256]{0:T(256)} %param.17) | copy-start | bytes 3076
  3.9 30.4 %all-to-all-start = ((bf16[16,16,2048]{2,1,0:T(8,128)(2,1)}), bf16[16,16,2048]{2,1,0:T(8,128)(2,1)S(1)}, u32[]{:S(2)}, u32[]{:S(2)}) async-start(bf16[16,16,2048]{2,1,0:T(8,128)(2,1)} %bitcast.2), calls=%async_computation | async-start | bytes 2097152 | tf_op jit(solution)/shard_map/all_to_all | solution.py:410
  12.9 38.0 %copy-start.10 = (f32[16,16,128]{2,1,0:T(8,128)}, f32[16,16,128]{2,1,0:T(8,128)S(1)}, u32[]{:S(2)}) copy-start(f32[16,16,128]{2,1,0:T(8,128)S(1)} %pad_maximum_fusion.2.c_ref) | copy-start | bytes 393220
  36.2 46.9 %all-to-all-start.1 = ((bf16[16,16,2048]{2,1,0:T(8,128)(2,1)}), bf16[16,16,2048]{2,1,0:T(8,128)(2,1)S(1)}, u32[]{:S(2)}, u32[]{:S(2)}) async-start(bf16[16,16,2048]{2,1,0:T(8,128)(2,1)} %pick.1), calls=%async_computation.1 | async-start | bytes 2097152 | tf_op jit(solution)/shard_map/all_to_all | solution.py:410
  46.4 37.8 %collective-permute-start = (bf16[256,2048]{1,0:T(8,128)(2,1)}, bf16[256,2048]{1,0:T(8,128)(2,1)}, u32[]{:S(2)}, u32[]{:S(2)}) collective-permute-start(bf16[256,2048]{1,0:T(8,128)(2,1)} %turn_keys.1.kv_ref), channel_id=1, source_target_pairs={{0,16},{1,17},{2,18},{3,19},{4,20},{5,21},{6,22},{7,23},{8,24},{9,... | collective-permute-start | bytes 3145736 | tf_op jit(solution)/shard_map/ppermute | solution.py:416
  51.6 2.2 copy-start.2
  54.6 2.2 copy-start.20
  56.8 2.2 copy-start.21
  79.9 3.3 %copy-start.26 = (f32[256,8192]{1,0:T(8,128)}, f32[256,8192]{1,0:T(8,128)S(1)}, u32[]{:S(2)}) copy-start(f32[256,8192]{1,0:T(8,128)S(1)} %get-tuple-element.24.dq_in_ref) | copy-start | bytes 25165828
  83.2 16.0 %copy-start.8 = (f32[256,2048]{1,0:T(8,128)}, f32[256,2048]{1,0:T(8,128)S(1)}, u32[]{:S(2)}) copy-start(f32[256,2048]{1,0:T(8,128)S(1)} %get-tuple-element.31.own_ref) | copy-start | bytes 6291460
  84.1 23.0 %collective-permute-start.2 = (bf16[256,1024]{1,0:T(8,128)(2,1)S(1)}, bf16[256,1024]{1,0:T(8,128)(2,1)S(1)}, u32[]{:S(2)}, u32[]{:S(2)}) collective-permute-start(bf16[256,1024]{1,0:T(8,128)(2,1)S(1)} %get-tuple-element.41), channel_id=1, source_target_pairs={{0,16},{16,0},{1,17},{17,1},{2,18},{18,2},{3,19},{19,3},{4,20},{20... | collective-permute-start | bytes 1572872 | tf_op jit(solution)/shard_map/ppermute | solution.py:416
  84.1 2.2 copy-start.3
  86.3 2.2 copy-start.6
  90.2 3.4 %copy-start.27 = (f32[256,8192]{1,0:T(8,128)S(1)}, f32[256,8192]{1,0:T(8,128)}, u32[]{:S(2)}) copy-start(f32[256,8192]{1,0:T(8,128)} %copy-done.26) | copy-start | bytes 25165828
  99.2 7.9 %copy-start.22 = (bf16[256,2048]{1,0:T(8,128)(2,1)}, bf16[256,2048]{1,0:T(8,128)(2,1)S(1)}, u32[]{:S(2)}) copy-start(bf16[256,2048]{1,0:T(8,128)(2,1)S(1)} %get-tuple-element.32) | copy-start | bytes 3145732
  99.2 7.9 %copy-start.24 = (f32[256,8192]{1,0:T(8,128)}, f32[256,8192]{1,0:T(8,128)S(1)}, u32[]{:S(2)}) copy-start(f32[256,8192]{1,0:T(8,128)S(1)} %get-tuple-element.25.dq_in_ref) | copy-start | bytes 25165828
  107.1 43.7 %copy-start.16 = (f32[64,256]{1,0:T(8,128)S(1)}, f32[64,256]{1,0:T(8,128)}, u32[]{:S(2)}) copy-start(f32[64,256]{1,0:T(8,128)} %lse_ref.11) | copy-start | bytes 196612
  107.2 43.7 %copy-start.19 = (f32[64,256]{1,0:T(8,128)S(1)}, f32[64,256]{1,0:T(8,128)}, u32[]{:S(2)}) copy-start(f32[64,256]{1,0:T(8,128)} %copy-done.17) | copy-start | bytes 196612
  116.1 24.4 %collective-permute-start.5 = (bf16[256,1024]{1,0:T(8,128)(2,1)S(1)}, bf16[256,1024]{1,0:T(8,128)(2,1)S(1)}, u32[]{:S(2)}, u32[]{:S(2)}) collective-permute-start(bf16[256,1024]{1,0:T(8,128)(2,1)S(1)} %get-tuple-element.36), channel_id=1, source_target_pairs={{0,16},{16,0},{1,17},{17,1},{2,18},{18,2},{3,19},{19,3},{4,20},{20... | collective-permute-start | bytes 1572872 | tf_op jit(solution)/shard_map/ppermute | solution.py:416
  127.7 23.2 %collective-permute-start.1 = (bf16[256,1024]{1,0:T(8,128)(2,1)}, bf16[256,1024]{1,0:T(8,128)(2,1)S(1)}, u32[]{:S(2)}, u32[]{:S(2)}) collective-permute-start(bf16[256,1024]{1,0:T(8,128)(2,1)} %get-tuple-element.42), channel_id=1, source_target_pairs={{0,16},{16,0},{1,17},{17,1},{2,18},{18,2},{3,19},{19,3},{4,20},{20... | collective-permute-start | bytes 1572872 | tf_op jit(solution)/shard_map/ppermute | solution.py:416
  141.4 38.5 %all-to-all-start.2 = ((bf16[16,16,1024]{2,1,0:T(8,128)(2,1)}), bf16[16,16,1024]{2,1,0:T(8,128)(2,1)S(1)}, u32[]{:S(2)}, u32[]{:S(2)}) async-start(bf16[16,16,1024]{2,1,0:T(8,128)(2,1)} %bitcast.4), calls=%async_computation.2 | async-start | bytes 1048576 | tf_op jit(solution)/shard_map/all_to_all | solution.py:410
  150.8 2.2 copy-start.4
  153.0 2.2 copy-start.7
  155.2 3.4 %copy-start.25 = (f32[256,8192]{1,0:T(8,128)S(1)}, f32[256,8192]{1,0:T(8,128)}, u32[]{:S(2)}) copy-start(f32[256,8192]{1,0:T(8,128)} %copy-done.24) | copy-start | bytes 25165828
  166.6 13.2 %collective-permute-start.4 = (bf16[256,1024]{1,0:T(8,128)(2,1)S(1)}, bf16[256,1024]{1,0:T(8,128)(2,1)S(1)}, u32[]{:S(2)}, u32[]{:S(2)}) collective-permute-start(bf16[256,1024]{1,0:T(8,128)(2,1)S(1)} %get-tuple-element.34), channel_id=1, source_target_pairs={{0,16},{16,0},{1,17},{17,1},{2,18},{18,2},{3,19},{19,3},{4,20},{20... | collective-permute-start | bytes 1572872 | tf_op jit(solution)/shard_map/ppermute | solution.py:416
  168.4 30.2 %copy-start.11 = (f32[16,16,128]{2,1,0:T(8,128)S(1)}, f32[16,16,128]{2,1,0:T(8,128)}, u32[]{:S(2)}) copy-start(f32[16,16,128]{2,1,0:T(8,128)} %copy-done.10) | copy-start | bytes 393220
  177.3 27.8 %copy-start.23 = (bf16[256,2048]{1,0:T(8,128)(2,1)S(1)}, bf16[256,2048]{1,0:T(8,128)(2,1)}, u32[]{:S(2)}) copy-start(bf16[256,2048]{1,0:T(8,128)(2,1)} %copy-done.22) | copy-start | bytes 3145732
  200.9 33.7 %all-to-all-start.4 = ((bf16[16,16,2048]{2,1,0:T(8,128)(2,1)}), bf16[16,16,2048]{2,1,0:T(8,128)(2,1)S(1)}, u32[]{:S(2)}, u32[]{:S(2)}) async-start(bf16[16,16,2048]{2,1,0:T(8,128)(2,1)} %merge.1), calls=%async_computation.4 | async-start | bytes 2097152 | tf_op jit(solution)/shard_map/all_to_all | solution.py:410
  205.0 27.4 %collective-permute-start.3 = (bf16[256,2048]{1,0:T(8,128)(2,1)S(1)}, bf16[256,2048]{1,0:T(8,128)(2,1)S(1)}, u32[]{:S(2)}, u32[]{:S(2)}) collective-permute-start(bf16[256,2048]{1,0:T(8,128)(2,1)S(1)} %copy-done.23), channel_id=1, source_target_pairs={{16,0},{17,1},{18,2},{19,3},{20,4},{21,5},{22,6},{23,7},{24,8},{25... | collective-permute-start | bytes 3145736 | tf_op jit(solution)/shard_map/ppermute | solution.py:416
  232.4 3.4 %copy-start.1 = (s32[16,1]{0,1:T(1,128)S(1)}, s32[16,1]{0,1:T(1,128)}, u32[]{:S(2)}) copy-start(s32[16,1]{0,1:T(1,128)} %param.15) | copy-start | bytes 196
  (8 other events, 8.9 us)

commit v3 on v2

--- a/solution.py
+++ b/solution.py
@@ -68,7 +68,7 @@
     return pl.pallas_call(
         pair_kernel,
         out_shape=jax.ShapeDtypeStruct((rows, 2 * width), jnp.bfloat16),
-        compiler_params=params(0, 6),
+        compiler_params=params(0, 60),
         name="pair",
     )(keys, values)
 
@@ -77,7 +77,7 @@
     return pl.pallas_call(
         turn_keys_kernel,
         out_shape=jax.ShapeDtypeStruct(x.shape, x.dtype),
-        compiler_params=params(0, 6),
+        compiler_params=params(0, 60),
         name="turn_keys",
     )(x, c, s)
 
@@ -209,7 +209,7 @@
         in_specs=[big, big, big, row, table, table, pair],
         out_specs=[part, part_row, part, pair],
         scratch_shapes=[pltpu.VMEM((rows, group * rows), jnp.bfloat16)] * 2,
-        compiler_params=params(1, 24),
+        compiler_params=params(1, 60),
         cost_estimate=pl.CostEstimate(
             flops=20 * count * group * rows * rows * HEAD_SIZE,
             bytes_accessed=rows * count * wide * 12,
@@ -326,7 +326,7 @@
             + ([pltpu.VMEM((rows, wide), jnp.float32)] if final else []),
         ),
         input_output_aliases=aliases,
-        compiler_params=params(1, 24),
+        compiler_params=params(1, 60),
         cost_estimate=pl.CostEstimate(
             flops=20 * count * group * rows * rows * HEAD_SIZE * len(kvs),
             bytes_accessed=rows * count * wide * 12,
@@ -353,7 +353,7 @@
     return pl.pallas_call(
         settle_kernel,
         out_shape=jax.ShapeDtypeStruct(local.shape, jnp.float32),
-        compiler_params=params(0, 12),
+        compiler_params=params(0, 60),
         name="settle",
     )(local, c, s, *parts)
 

time: 237 us -> 224 us (0.945)
  local copies, waits for them, and re-layouts: 36.5 us -> 6.52 us
  Pallas kernels: 67.3 us -> 86.4 us
  starting transfers between devices: 42.7 us -> 38 us
    unnamed x60 -> x24, local copies, waits for them, and re-layouts: 34.3 us -> 5.15 us
    pallas_call x5, Pallas kernels: 39.2 us -> 53.1 us  [cross(): pl.pallas_call(functools.partial(cross_kernel, group, joint, mode), out_s...]
    ppermute x6, starting transfers between devices: 19.1 us -> 14.4 us  [shift(): return lax.ppermute(x, 'head', route)]
    pallas_call x1, Pallas kernels: 0.54 us -> 3.87 us  [settle(): pl.pallas_call(settle_kernel, out_shape=jax.ShapeDtypeStruct(local.shape,...]
  transfers between devices with their start and end apart: 10 -> 10, of which waited for: 5 -> 6; matrix products, arithmetic and copies ran while one was open for 2% -> 3% of each run, Pallas kernels for 22% -> 31%
where the time goes in v3:
time: 224 us; the launch traced here: 223 us
  Pallas kernels  86.4 us (39%)
  waiting for transfers between devices  67.4 us (30%)
  starting transfers between devices  38 us (17%)
  blocking collectives  18.2 us (8%)
  local copies, waits for them, and re-layouts  6.52 us (3%)
  other arithmetic  5.43 us (2%)
    pallas_call x5, Pallas kernels, cross(): pl.pallas_call(functools.partial(cross_kernel, group, joint, mode), out_s...  53.1 us
    ppermute x6, waiting for transfers between devices, shift(): return lax.ppermute(x, 'head', route)  46.7 us
    all_to_all x4, starting transfers between devices, exchange(): lax.all_to_all(x.reshape(places, rows // places, width), 'ctx', 0, 0, til...  23.6 us
    all_to_all x4, waiting for transfers between devices, exchange(): lax.all_to_all(x.reshape(places, rows // places, width), 'ctx', 0, 0, til...  20.6 us
    pallas_call x1, Pallas kernels, diagonal(): pl.pallas_call(functools.partial(diagonal_kernel, group), out_shape=[jax....  18.8 us
    all_to_all x1, blocking collectives, exchange(): lax.all_to_all(x.reshape(places, rows // places, width), 'ctx', 0, 0, til...  18.2 us
    ppermute x6, starting transfers between devices, shift(): return lax.ppermute(x, 'head', route)  14.4 us
    unnamed x24, local copies, waits for them, and re-layouts  5.15 us
  transfers between devices with their start and end apart: 10, of which 6 were waited for; matrix products, arithmetic and copies ran while one was open for 3% of the time, Pallas kernels for 31%

profile of v3, /device:TPU:0, one launch (start us, length us, event | category | flops | bytes accessed | tf_op | source)
XLA Modules:
  0.0 222.8 jit_solution(15579444743402293603)
XLA Ops:
  0.7 2.4 %pair.1.x_ref = bf16[256,2048]{1,0:T(8,128)(2,1)} custom-call(bf16[256,1024]{1,0:T(8,128)(2,1)} %k_ref.1, bf16[256,1024]{1,0:T(8,128)(2,1)} %v_ref.1), custom_call_target="tpu_custom_call" | custom-call | tf_op jit(solution)/shard_map/pair/pallas_call | solution.py:68
  3.0 7.5 %all-to-all-start = ((bf16[16,16,2048]{2,1,0:T(8,128)(2,1)}), bf16[16,16,2048]{2,1,0:T(8,128)(2,1)S(1)}, u32[]{:S(2)}, u32[]{:S(2)}) async-start(bf16[16,16,2048]{2,1,0:T(8,128)(2,1)} %bitcast.12), calls=%async_computation | async-start | bytes 2097152 | tf_op jit(solution)/shard_map/all_to_all | solution.py:410
  12.9 20.6 %all-to-all-done.x_ref = bf16[16,16,2048]{2,1,0:T(8,128)(2,1)S(1)} async-done(((bf16[16,16,2048]{2,1,0:T(8,128)(2,1)}), bf16[16,16,2048]{2,1,0:T(8,128)(2,1)S(1)}, u32[]{:S(2)}, u32[]{:S(2)}) %all-to-all-start) | async-done | bytes 1048608 | tf_op jit(solution)/shard_map/all_to_all | solution.py:410
  33.5 1.9 pick.1
  35.4 6.8 %all-to-all-start.1 = ((bf16[16,16,2048]{2,1,0:T(8,128)(2,1)}), bf16[16,16,2048]{2,1,0:T(8,128)(2,1)S(1)}, u32[]{:S(2)}, u32[]{:S(2)}) async-start(bf16[16,16,2048]{2,1,0:T(8,128)(2,1)} %pick.1), calls=%async_computation.1 | async-start | bytes 2097152 | tf_op jit(solution)/shard_map/all_to_all | solution.py:410
  42.7 0.9 pad_maximum_fusion
  43.6 2.7 %turn_keys.1.kv_ref = bf16[256,2048]{1,0:T(8,128)(2,1)} custom-call(bf16[256,2048]{1,0:T(8,128)(2,1)} %pair.1.x_ref, f32[256,128]{1,0:T(8,128)} %get-tuple-element.51.c_ref, f32[256,128]{1,0:T(8,128)} %get-tuple-element.52.s_ref), custom_call_target="tpu_custom_call" | custom-call | tf_op jit(solution)/shard_map/turn_keys/pallas_call | solution.py:77
  46.3 3.4 %collective-permute-start = (bf16[256,2048]{1,0:T(8,128)(2,1)}, bf16[256,2048]{1,0:T(8,128)(2,1)S(1)}, u32[]{:S(2)}, u32[]{:S(2)}) collective-permute-start(bf16[256,2048]{1,0:T(8,128)(2,1)} %turn_keys.1.kv_ref), channel_id=1, source_target_pairs={{0,16},{1,17},{2,18},{3,19},{4,20},{5,21},{6,22},{7,23},{8,24},{9,... | collective-permute-start | bytes 3145736 | tf_op jit(solution)/shard_map/ppermute | solution.py:416
  50.6 18.8 %diagonal.1 = (bf16[256,8192]{1,0:T(8,128)(2,1)}, f32[64,256]{1,0:T(8,128)}, f32[256,8192]{1,0:T(8,128)}, f32[256,2048]{1,0:T(8,128)}) custom-call(bf16[256,8192]{1,0:T(8,128)(2,1)} %q_ref.1, bf16[256,8192]{1,0:T(8,128)(2,1)} %do_ref.11, bf16[256,8192]{1,0:T(8,128)(2,1)} %out_ref.1, f32[64,256]{1,0:T(8,128)} %lse_ref.11, ...), custom_call_target="tpu_custom_call" | custom-call | flops 10737418240 | bytes 25165824 | tf_op jit(solution)/shard_map/diagonal/pallas_call | solution.py:200
  69.5 4.0 %collective-permute-done.refs_0_ = bf16[256,2048]{1,0:T(8,128)(2,1)S(1)} collective-permute-done((bf16[256,2048]{1,0:T(8,128)(2,1)}, bf16[256,2048]{1,0:T(8,128)(2,1)S(1)}, u32[]{:S(2)}, u32[]{:S(2)}) %collective-permute-start) | collective-permute-done | bytes 1048608 | tf_op jit(solution)/shard_map/ppermute | solution.py:416
  73.5 1.0 copy-done.9
  74.5 11.8 %cross.5 = (f32[256,8192]{1,0:T(8,128)}, bf16[256,2048]{1,0:T(8,128)(2,1)}) custom-call(s32[1]{0:T(128)} %bitcast.1.flag_ref, bf16[256,8192]{1,0:T(8,128)(2,1)} %get-tuple-element.22.rq_ref, bf16[256,8192]{1,0:T(8,128)(2,1)} %do_ref.11, f32[64,256]{1,0:T(8,128)} %lse_ref.11, f32[64,256]{1,0:T(8,128)} %get-tuple-element.23.delta_ref, ...), custom_call_target="tpu_custom_call" | custom-call | flops 10737418240 | bytes 25165824 | tf_op jit(solution)/shard_map/cross/pallas_call | solution.py:315
  86.3 10.4 %cross.7 = (f32[256,8192]{1,0:T(8,128)}, bf16[256,1024]{1,0:T(8,128)(2,1)}) custom-call(s32[1]{0:T(128)} %dynamic_slice.3.flag_ref, bf16[256,8192]{1,0:T(8,128)(2,1)} %get-tuple-element.22.rq_ref, bf16[256,8192]{1,0:T(8,128)(2,1)} %do_ref.11, f32[64,256]{1,0:T(8,128)} %lse_ref.11, f32[64,256]{1,0:T(8,128)} %get-tuple-element.23.delta_ref, ...), custom_call_target="tpu_custom_call" | custom-call | flops 5368709120 | bytes 12582912 | tf_op jit(solution)/shard_map/cross/pallas_call | solution.py:315
  97.5 10.3 %cross.8 = (bf16[256,8192]{1,0:T(8,128)(2,1)}, bf16[256,1024]{1,0:T(8,128)(2,1)}) custom-call(s32[1]{0:T(128)} %dynamic_slice.3.flag_ref, bf16[256,8192]{1,0:T(8,128)(2,1)} %get-tuple-element.22.rq_ref, bf16[256,8192]{1,0:T(8,128)(2,1)} %do_ref.11, f32[64,256]{1,0:T(8,128)} %lse_ref.11, f32[64,256]{1,0:T(8,128)} %get-tuple-element.23.delta_ref, ...), custom_call_target="tpu_custom_call" | custom-call | flops 5368709120 | bytes 12582912 | tf_op jit(solution)/shard_map/cross/pallas_call | solution.py:315
  107.8 7.7 %collective-permute-start.5 = (bf16[256,1024]{1,0:T(8,128)(2,1)}, bf16[256,1024]{1,0:T(8,128)(2,1)S(1)}, u32[]{:S(2)}, u32[]{:S(2)}) collective-permute-start(bf16[256,1024]{1,0:T(8,128)(2,1)} %get-tuple-element.36), channel_id=1, source_target_pairs={{0,16},{16,0},{1,17},{17,1},{2,18},{18,2},{3,19},{19,3},{4,20},{20... | collective-permute-start | bytes 1572872 | tf_op jit(solution)/shard_map/ppermute | solution.py:416
  115.6 12.9 %collective-permute-done.5 = bf16[256,1024]{1,0:T(8,128)(2,1)S(1)} collective-permute-done((bf16[256,1024]{1,0:T(8,128)(2,1)}, bf16[256,1024]{1,0:T(8,128)(2,1)S(1)}, u32[]{:S(2)}, u32[]{:S(2)}) %collective-permute-start.5) | collective-permute-done | bytes 524320 | tf_op jit(solution)/shard_map/ppermute | solution.py:416
  128.5 1.1 add_convert_fusion
  129.6 5.1 %all-to-all-start.2 = ((bf16[16,16,1024]{2,1,0:T(8,128)(2,1)}), bf16[16,16,1024]{2,1,0:T(8,128)(2,1)S(1)}, u32[]{:S(2)}, u32[]{:S(2)}) async-start(bf16[16,16,1024]{2,1,0:T(8,128)(2,1)} %bitcast.4), calls=%async_computation.2 | async-start | bytes 1048576 | tf_op jit(solution)/shard_map/all_to_all | solution.py:410
  134.7 3.3 %collective-permute-done.1.refs_0_ = bf16[256,1024]{1,0:T(8,128)(2,1)S(1)} collective-permute-done((bf16[256,1024]{1,0:T(8,128)(2,1)S(1)}, bf16[256,1024]{1,0:T(8,128)(2,1)S(1)}, u32[]{:S(2)}, u32[]{:S(2)}) %collective-permute-start.1) | collective-permute-done | bytes 524320 | tf_op jit(solution)/shard_map/ppermute | solution.py:416
  138.8 10.4 %cross.6 = (f32[256,8192]{1,0:T(8,128)}, bf16[256,1024]{1,0:T(8,128)(2,1)}) custom-call(s32[1]{0:T(128)} %dynamic_slice.3.flag_ref, bf16[256,8192]{1,0:T(8,128)(2,1)} %get-tuple-element.22.rq_ref, bf16[256,8192]{1,0:T(8,128)(2,1)} %do_ref.11, f32[64,256]{1,0:T(8,128)} %lse_ref.11, f32[64,256]{1,0:T(8,128)} %get-tuple-element.23.delta_ref, ...), custom_call_target="tpu_custom_call" | custom-call | flops 5368709120 | bytes 12582912 | tf_op jit(solution)/shard_map/cross/pallas_call | solution.py:315
  149.2 1.8 collective-permute-start.4
  151.0 10.2 %cross.9 = (bf16[256,8192]{1,0:T(8,128)(2,1)}, bf16[256,1024]{1,0:T(8,128)(2,1)}) custom-call(s32[1]{0:T(128)} %dynamic_slice.3.flag_ref, bf16[256,8192]{1,0:T(8,128)(2,1)} %get-tuple-element.22.rq_ref, bf16[256,8192]{1,0:T(8,128)(2,1)} %do_ref.11, f32[64,256]{1,0:T(8,128)} %lse_ref.11, ...), custom_call_target="tpu_custom_call", output_to_operand_aliasing={{0}: (9, {})} | custom-call | flops 5368709120 | bytes 12582912 | tf_op jit(solution)/shard_map/cross/pallas_call | solution.py:315
  161.7 1.2 add_convert_fusion.1
  163.0 18.2 %all_to_all.25.refs_1_ = bf16[16,16,1024]{2,1,0:T(8,128)(2,1)S(1)} all-to-all(bf16[16,16,1024]{2,1,0:T(8,128)(2,1)S(1)} %bitcast.13), channel_id=1, replica_groups=mesh['head'=2,'ctx'=16] {'ctx'}, dimensions={0} | all-to-all | bytes 1048576 | tf_op jit(solution)/shard_map/all_to_all | solution.py:410
  181.2 2.3 %merge.1 = bf16[16,16,2048]{2,1,0:T(8,128)(2,1)} custom-call(s32[16]{0:T(128)S(1)} %get-tuple-element.26.source_ref, s32[16]{0:T(128)S(1)} %convert_element_type.32.present_ref, f32[16,16,128]{2,1,0:T(8,128)S(1)} %pad_maximum_fusion.2.c_ref, f32[16,16,128]{2,1,0:T(8,128)S(1)} %pad_maximum_fusion.3.s_ref, bf16[16,16,1024]{2,1,0:T(8,128)(2,1)S(1)} %all-to-all-done.2.refs_0_, ...), custom_call_target="tpu_custom_call" | custom-call | tf_op jit(solution)/shard_map/merge/pallas_call | solution.py:131
  183.5 4.2 %all-to-all-start.4 = ((bf16[16,16,2048]{2,1,0:T(8,128)(2,1)}), bf16[16,16,2048]{2,1,0:T(8,128)(2,1)S(1)}, u32[]{:S(2)}, u32[]{:S(2)}) async-start(bf16[16,16,2048]{2,1,0:T(8,128)(2,1)} %merge.1), calls=%async_computation.4 | async-start | bytes 2097152 | tf_op jit(solution)/shard_map/all_to_all | solution.py:410
  187.7 1.3 collective-permute-start.3
  189.0 26.1 %collective-permute-done.3.refs_0_ = bf16[256,2048]{1,0:T(8,128)(2,1)S(1)} collective-permute-done((bf16[256,2048]{1,0:T(8,128)(2,1)S(1)}, bf16[256,2048]{1,0:T(8,128)(2,1)S(1)}, u32[]{:S(2)}, u32[]{:S(2)}) %collective-permute-start.3) | collective-permute-done | bytes 1048608 | tf_op jit(solution)/shard_map/ppermute | solution.py:416
  215.1 1.0 copy-done.4
  216.0 3.9 %settle.1.own_ref = f32[256,2048]{1,0:T(8,128)} custom-call(f32[256,2048]{1,0:T(8,128)} %get-tuple-element.31.own_ref, f32[256,128]{1,0:T(8,128)} %get-tuple-element.51.c_ref, f32[256,128]{1,0:T(8,128)} %get-tuple-element.52.s_ref, bf16[256,2048]{1,0:T(8,128)(2,1)} %copy-done.4), custom_call_target="tpu_custom_call" | custom-call | tf_op jit(solution)/shard_map/settle/pallas_call | solution.py:353
  219.9 1.6 copy-done.2
  221.5 1.3 finish.1
  (43 shorter events, 5.9 us)
Async XLA Ops:
  0.6 10.0 %copy-start = (s32[16,1]{0,1:T(1,128)S(1)}, s32[16,1]{0,1:T(1,128)}, u32[]{:S(2)}) copy-start(s32[16,1]{0,1:T(1,128)} %param.15) | copy-start | bytes 196
  0.6 10.0 %copy-start.6 = (s32[16]{0:T(128)S(1)}, s32[16]{0:T(128)}, u32[]{:S(2)}) copy-start(s32[16]{0:T(128)} %param.16) | copy-start | bytes 196
  3.0 39.1 %copy-start.7 = (s32[256]{0:T(256)S(1)}, s32[256]{0:T(256)}, u32[]{:S(2)}) copy-start(s32[256]{0:T(256)} %param.17) | copy-start | bytes 3076
  3.0 30.4 %all-to-all-start = ((bf16[16,16,2048]{2,1,0:T(8,128)(2,1)}), bf16[16,16,2048]{2,1,0:T(8,128)(2,1)S(1)}, u32[]{:S(2)}, u32[]{:S(2)}) async-start(bf16[16,16,2048]{2,1,0:T(8,128)(2,1)} %bitcast.12), calls=%async_computation | async-start | bytes 2097152 | tf_op jit(solution)/shard_map/all_to_all | solution.py:410
  35.4 34.0 %all-to-all-start.1 = ((bf16[16,16,2048]{2,1,0:T(8,128)(2,1)}), bf16[16,16,2048]{2,1,0:T(8,128)(2,1)S(1)}, u32[]{:S(2)}, u32[]{:S(2)}) async-start(bf16[16,16,2048]{2,1,0:T(8,128)(2,1)} %pick.1), calls=%async_computation.1 | async-start | bytes 2097152 | tf_op jit(solution)/shard_map/all_to_all | solution.py:410
  46.3 27.2 %collective-permute-start = (bf16[256,2048]{1,0:T(8,128)(2,1)}, bf16[256,2048]{1,0:T(8,128)(2,1)S(1)}, u32[]{:S(2)}, u32[]{:S(2)}) collective-permute-start(bf16[256,2048]{1,0:T(8,128)(2,1)} %turn_keys.1.kv_ref), channel_id=1, source_target_pairs={{0,16},{1,17},{2,18},{3,19},{4,20},{5,21},{6,22},{7,23},{8,24},{9,... | collective-permute-start | bytes 3145736 | tf_op jit(solution)/shard_map/ppermute | solution.py:416
  69.4 17.0 %copy-start.3 = (bf16[16,16,2048]{2,1,0:T(8,128)(2,1)}, bf16[16,16,2048]{2,1,0:T(8,128)(2,1)S(1)}, u32[]{:S(2)}) copy-start(bf16[16,16,2048]{2,1,0:T(8,128)(2,1)S(1)} %all-to-all-done.1) | copy-start | bytes 3145732
  69.5 27.3 %collective-permute-start.2 = (bf16[256,1024]{1,0:T(8,128)(2,1)S(1)}, bf16[256,1024]{1,0:T(8,128)(2,1)S(1)}, u32[]{:S(2)}, u32[]{:S(2)}) collective-permute-start(bf16[256,1024]{1,0:T(8,128)(2,1)S(1)} %get-tuple-element.41), channel_id=1, source_target_pairs={{0,16},{16,0},{1,17},{17,1},{2,18},{18,2},{3,19},{19,3},{4,20},{20... | collective-permute-start | bytes 1572872 | tf_op jit(solution)/shard_map/ppermute | solution.py:416
  73.5 1.0 copy-start.9
  96.7 0.8 copy-start.11
  97.5 31.0 %copy-start.5 = (bf16[256,1024]{1,0:T(8,128)(2,1)S(1)}, bf16[256,1024]{1,0:T(8,128)(2,1)}, u32[]{:S(2)}) copy-start(bf16[256,1024]{1,0:T(8,128)(2,1)} %get-tuple-element.35) | copy-start | bytes 1572868
  107.8 20.6 %collective-permute-start.5 = (bf16[256,1024]{1,0:T(8,128)(2,1)}, bf16[256,1024]{1,0:T(8,128)(2,1)S(1)}, u32[]{:S(2)}, u32[]{:S(2)}) collective-permute-start(bf16[256,1024]{1,0:T(8,128)(2,1)} %get-tuple-element.36), channel_id=1, source_target_pairs={{0,16},{16,0},{1,17},{17,1},{2,18},{18,2},{3,19},{19,3},{4,20},{20... | collective-permute-start | bytes 1572872 | tf_op jit(solution)/shard_map/ppermute | solution.py:416
  115.5 22.5 %collective-permute-start.1 = (bf16[256,1024]{1,0:T(8,128)(2,1)S(1)}, bf16[256,1024]{1,0:T(8,128)(2,1)S(1)}, u32[]{:S(2)}, u32[]{:S(2)}) collective-permute-start(bf16[256,1024]{1,0:T(8,128)(2,1)S(1)} %get-tuple-element.42), channel_id=1, source_target_pairs={{0,16},{16,0},{1,17},{17,1},{2,18},{18,2},{3,19},{19,3},{4,20},{20... | collective-permute-start | bytes 1572872 | tf_op jit(solution)/shard_map/ppermute | solution.py:416
  129.6 33.4 %all-to-all-start.2 = ((bf16[16,16,1024]{2,1,0:T(8,128)(2,1)}), bf16[16,16,1024]{2,1,0:T(8,128)(2,1)S(1)}, u32[]{:S(2)}, u32[]{:S(2)}) async-start(bf16[16,16,1024]{2,1,0:T(8,128)(2,1)} %bitcast.4), calls=%async_computation.2 | async-start | bytes 1048576 | tf_op jit(solution)/shard_map/all_to_all | solution.py:410
  138.0 0.8 copy-start.10
  149.2 12.5 %collective-permute-start.4 = (bf16[256,1024]{1,0:T(8,128)(2,1)}, bf16[256,1024]{1,0:T(8,128)(2,1)S(1)}, u32[]{:S(2)}, u32[]{:S(2)}) collective-permute-start(bf16[256,1024]{1,0:T(8,128)(2,1)} %get-tuple-element.34), channel_id=1, source_target_pairs={{0,16},{16,0},{1,17},{17,1},{2,18},{18,2},{3,19},{19,3},{4,20},{20... | collective-permute-start | bytes 1572872 | tf_op jit(solution)/shard_map/ppermute | solution.py:416
  161.2 26.4 %copy-start.8 = (bf16[256,2048]{1,0:T(8,128)(2,1)S(1)}, bf16[256,2048]{1,0:T(8,128)(2,1)}, u32[]{:S(2)}) copy-start(bf16[256,2048]{1,0:T(8,128)(2,1)} %get-tuple-element.32) | copy-start | bytes 3145732
  183.5 36.4 %all-to-all-start.4 = ((bf16[16,16,2048]{2,1,0:T(8,128)(2,1)}), bf16[16,16,2048]{2,1,0:T(8,128)(2,1)S(1)}, u32[]{:S(2)}, u32[]{:S(2)}) async-start(bf16[16,16,2048]{2,1,0:T(8,128)(2,1)} %merge.1), calls=%async_computation.4 | async-start | bytes 2097152 | tf_op jit(solution)/shard_map/all_to_all | solution.py:410
  187.7 27.4 %collective-permute-start.3 = (bf16[256,2048]{1,0:T(8,128)(2,1)S(1)}, bf16[256,2048]{1,0:T(8,128)(2,1)S(1)}, u32[]{:S(2)}, u32[]{:S(2)}) collective-permute-start(bf16[256,2048]{1,0:T(8,128)(2,1)S(1)} %copy-done.8), channel_id=1, source_target_pairs={{16,0},{17,1},{18,2},{19,3},{20,4},{21,5},{22,6},{23,7},{24,8},{25... | collective-permute-start | bytes 3145736 | tf_op jit(solution)/shard_map/ppermute | solution.py:416
  215.1 1.0 copy-start.4
  215.1 7.7 %copy-start.1 = (s32[16,1]{0,1:T(1,128)S(1)}, s32[16,1]{0,1:T(1,128)}, u32[]{:S(2)}) copy-start(s32[16,1]{0,1:T(1,128)} %param.15) | copy-start | bytes 196
  219.9 1.6 copy-start.2

commit v4 on v3

v4 whole, which is shorter than its diff:
```python
import functools
import math

import jax
import jax.numpy as jnp
from jax import lax
from jax.experimental import pallas as pl
from jax.experimental.pallas import tpu as pltpu
from jax.sharding import PartitionSpec as P


HEAD_SIZE = 128
TREE_BLOCK = 512
LOG2E = math.log2(math.e)
LN2 = math.log(2.0)
SCALE = 1.0 / math.sqrt(HEAD_SIZE)
rope_base = 500000.0
MIB = 1024 * 1024
NT = (((1,), (1,)), ((), ()))
NN = (((1,), (0,)), ((), ()))
TN = (((0,), (0,)), ((), ()))


def rope_tables(positions):
    half_dim = HEAD_SIZE // 2
    freq_index = jnp.arange(half_dim, dtype=jnp.float32)
    inverse = rope_base ** (-(2.0 * freq_index / HEAD_SIZE))
    angles = positions.astype(jnp.float32)[:, None] * inverse[None, :]
    c, s = jnp.cos(angles), jnp.sin(angles)
    return jnp.concatenate([c, c], -1), jnp.concatenate([-s, s], -1)


def dot(a, b, dims):
    return lax.dot_general(a, b, dims, preferred_element_type=jnp.float32)


def turn(x, c, s):
    return x * c + pltpu.roll(x, HEAD_SIZE // 2, 1) * s


def turn_back(x, c, s):
    return x * c - pltpu.roll(x, HEAD_SIZE // 2, 1) * s


def params(n, mib):
    return pltpu.CompilerParams(
        dimension_semantics=("arbitrary",) * n, vmem_limit_bytes=mib * MIB
    )


def find_slots(place_ref, slot_ref):
    for b in range(place_ref.shape[0]):
        slot_ref[place_ref[b]] = b


def pick_kernel(place_ref, anc_ref, x_ref, c_ref, s_ref, *refs):
    *o_refs, slot_ref = refs
    find_slots(place_ref, slot_ref)
    half = x_ref.shape[2] // 2
    for d in range(x_ref.shape[0]):
        at = slot_ref[jnp.maximum(anc_ref[place_ref[d]], 0)]
        c, s = c_ref[at], s_ref[at]
        a = 0
        for o_ref in o_refs:
            for b in range(0, o_ref.shape[2], 2 * HEAD_SIZE):
                x = x_ref[at, :, a : a + HEAD_SIZE].astype(jnp.float32)
                o_ref[d, :, b : b + HEAD_SIZE] = turn(x, c, s).astype(jnp.bfloat16)
                o_ref[d, :, b + HEAD_SIZE : b + 2 * HEAD_SIZE] = x_ref[
                    at, :, half + a : half + a + HEAD_SIZE
                ]
                a += HEAD_SIZE


def pick(sizes, places, ancestors, x, c, s):
    return pl.pallas_call(
        pick_kernel,
        out_shape=[
            jax.ShapeDtypeStruct(x.shape[:2] + (size * 2 * HEAD_SIZE,), x.dtype) for size in sizes
        ],
        in_specs=[pl.BlockSpec(memory_space=pltpu.SMEM)] * 2
        + [pl.BlockSpec(memory_space=pltpu.VMEM)] * 3,
        out_specs=[pl.BlockSpec(memory_space=pltpu.VMEM)] * len(sizes),
        scratch_shapes=[pltpu.SMEM(places.shape, jnp.int32)],
        compiler_params=params(0, 8),
        name="pick",
    )(places, ancestors, x, c, s)


def merge_kernel(place_ref, anc_ref, c_ref, s_ref, *refs):
    *x_refs, o_ref, acc_ref, slot_ref = refs
    find_slots(place_ref, slot_ref)
    acc_ref[...] = jnp.zeros_like(acc_ref)
    for d in range(o_ref.shape[0]):

        above = anc_ref[place_ref[d]]

        @pl.when(above >= 0)
        def _():
            into, at = slot_ref[jnp.maximum(above, 0)], 0
            for x_ref in x_refs:
                width = x_ref.shape[2]
                acc_ref[into, :, at : at + width] += x_ref[d].astype(jnp.float32)
                at += width

    for d in range(o_ref.shape[0]):
        c, s = c_ref[d], s_ref[d]
        for b in range(0, o_ref.shape[2], 2 * HEAD_SIZE):
            k, v = slice(b, b + HEAD_SIZE), slice(b + HEAD_SIZE, b + 2 * HEAD_SIZE)
            o_ref[d, :, k] = turn_back(acc_ref[d, :, k], c, s).astype(o_ref.dtype)
            o_ref[d, :, v] = acc_ref[d, :, v].astype(o_ref.dtype)


def merge(places, ancestors, c, s, xs):
    shape = xs[0].shape[:2] + (sum(x.shape[2] for x in xs),)
    return pl.pallas_call(
        merge_kernel,
        out_shape=jax.ShapeDtypeStruct(shape, xs[0].dtype),
        in_specs=[pl.BlockSpec(memory_space=pltpu.SMEM)] * 2
        + [pl.BlockSpec(memory_space=pltpu.VMEM)] * (2 + len(xs)),
        out_specs=pl.BlockSpec(memory_space=pltpu.VMEM),
        scratch_shapes=[pltpu.VMEM(shape, jnp.float32), pltpu.SMEM(places.shape, jnp.int32)],
        compiler_params=params(0, 10),
        name="merge",
    )(places, ancestors, c, s, *xs)


def fronts(rq, do, lse, delta, k, v, mask=None):
    prob = jnp.exp2(dot(k, rq, NT) - lse)
    if mask is not None:
        prob = jnp.where(mask, prob, 0.0)
    grad_score = prob * (dot(v, do, NT) - delta)
    return prob.astype(jnp.bfloat16), grad_score.astype(jnp.bfloat16)


def stacked(ref, group):
    return jnp.concatenate([ref[:, cols_of(h)] for h in range(group)], 0)


def heads_of(width, kv_count):
    return width // HEAD_SIZE // kv_count


def cols_of(h):
    return slice(h * HEAD_SIZE, (h + 1) * HEAD_SIZE)


def diagonal_kernel(group, q_ref, do_ref, out_ref, lse_ref, c_ref, s_ref, raw_ref, v_ref, rq_ref, delta_ref, dq_ref, dkv_ref, p_ref, ds_ref):
    rows = q_ref.shape[0]
    c, s = c_ref[...] * (SCALE * LOG2E), s_ref[...] * (SCALE * LOG2E)
    key_at = lax.broadcasted_iota(jnp.int32, (rows, rows), 0)
    query_at = lax.broadcasted_iota(jnp.int32, (rows, rows), 1)
    causal = key_at <= query_at
    k = turn(raw_ref[...].astype(jnp.float32), c_ref[...], s_ref[...]).astype(jnp.bfloat16)
    v = v_ref[...]
    for h in range(group):
        cols, lanes = cols_of(h), slice(h * rows, (h + 1) * rows)
        do = do_ref[:, cols]
        rq = turn(q_ref[:, cols].astype(jnp.float32), c, s).astype(jnp.bfloat16)
        rq_ref[:, cols] = rq
        product = do.astype(jnp.float32) * out_ref[:, cols].astype(jnp.float32)
        delta = jnp.sum(product.T, axis=0, keepdims=True)
        delta_ref[h : h + 1, :] = delta
        p_ref[:, lanes], ds_ref[:, lanes] = fronts(
            rq, do, lse_ref[h : h + 1, :] * LOG2E, delta, k, v, causal
        )
    dkv_ref[:, :HEAD_SIZE] = dot(ds_ref[...], stacked(rq_ref, group), NN) * LN2
    dkv_ref[:, HEAD_SIZE:] = dot(p_ref[...], stacked(do_ref, group), NN)
    for h in range(group):
        gq = dot(ds_ref[:, h * rows : (h + 1) * rows], k, TN)
        dq_ref[:, cols_of(h)] = gq.astype(jnp.bfloat16)


def diagonal(q, do, out, lse, c, s, keys, values):
    rows, width = q.shape
    kv_count = count = keys.shape[1] // HEAD_SIZE
    first = 0
    group = heads_of(width, kv_count)
    wide = group * HEAD_SIZE
    big = pl.BlockSpec((rows, wide), lambda g: (0, g + first))
    row = pl.BlockSpec((group, rows), lambda g: (g + first, 0))
    table = pl.BlockSpec((rows, HEAD_SIZE), lambda g: (0, 0))
    pair = pl.BlockSpec((rows, 2 * HEAD_SIZE), lambda g: (0, g))
    one = pl.BlockSpec((rows, HEAD_SIZE), lambda g: (0, g))
    part = pl.BlockSpec((rows, wide), lambda g: (0, g))
    part_row = pl.BlockSpec((group, rows), lambda g: (g, 0))
    return pl.pallas_call(
        functools.partial(diagonal_kernel, group),
        out_shape=[
            jax.ShapeDtypeStruct((rows, count * wide), jnp.bfloat16),
            jax.ShapeDtypeStruct((count * group, rows), jnp.float32),
            jax.ShapeDtypeStruct((rows, count * wide), jnp.bfloat16),
            jax.ShapeDtypeStruct((rows, count * 2 * HEAD_SIZE), jnp.float32),
        ],
        grid=(count,),
        in_specs=[big, big, big, row, table, table, one, one],
        out_specs=[part, part_row, part, pair],
        scratch_shapes=[pltpu.VMEM((rows, group * rows), jnp.bfloat16)] * 2,
        compiler_params=params(1, 60),
        cost_estimate=pl.CostEstimate(
            flops=20 * count * group * rows * rows * HEAD_SIZE,
            bytes_accessed=rows * count * wide * 12,
            transcendentals=0,
        ),
        name="diagonal",
    )(q, do, out, lse, c, s, keys, values)


def cross_kernel(group, joint, final, ours, info_ref, place_ref, anc_ref, rq_ref, do_ref, lse_ref, delta_ref, c_ref, s_ref, dq_in_ref, *refs):
    sets = len(joint)
    refs = list(refs)
    kv_refs = [[refs.pop(0) for _ in range(4 if ours else 1)] for _ in range(sum(joint))]
    if final == 2:
        refs.pop(0)
    dq_ref = refs.pop(0)
    dkv_refs = [refs.pop(0) for _ in range(sum(joint))]
    p_ref, ds_ref, k_ref, v_ref = refs[:4]
    total_ref = refs[4] if sets > 1 else None
    rows = rq_ref.shape[0]
    c, s = c_ref[...] * SCALE, s_ref[...] * SCALE

    def put(cols, total):
        if final and sets == 1:
            dq_ref[:, cols] = turn_back(total, c, s).astype(jnp.bfloat16)
        elif sets == 1:
            dq_ref[:, cols] = total.astype(jnp.bfloat16)
        else:
            total_ref[:, cols] = total

    def run(members, fresh):
        here = slice(0, len(members) * rows)
        for n, m in enumerate(members):
            at = slice(n * rows, (n + 1) * rows)
            if ours:
                raw_ref, values_ref, kc_ref, ks_ref = kv_refs[m]
                raw = raw_ref[...].astype(jnp.float32)
                k_ref[at] = turn(raw, kc_ref[...], ks_ref[...]).astype(jnp.bfloat16)
                v_ref[at] = values_ref[...]
            else:
                k_ref[at] = kv_refs[m][0][:, :HEAD_SIZE]
                v_ref[at] = kv_refs[m][0][:, HEAD_SIZE:]
        k = k_ref[here]
        for h in range(group):
            lanes = slice(h * rows, (h + 1) * rows)
            p_ref[here, lanes], ds_ref[here, lanes] = fronts(
                rq_ref[:, cols_of(h)],
                do_ref[:, cols_of(h)],
                lse_ref[h : h + 1, :] * LOG2E,
                delta_ref[h : h + 1, :],
                k,
                v_ref[here],
            )
        gk = dot(ds_ref[here], stacked(rq_ref, group), NN) * LN2
        gv = dot(p_ref[here], stacked(do_ref, group), NN)
        for n, m in enumerate(members):
            own = slice(n * rows, (n + 1) * rows)
            dkv_refs[m][:, :HEAD_SIZE] = gk[own].astype(jnp.bfloat16)
            dkv_refs[m][:, HEAD_SIZE:] = gv[own].astype(jnp.bfloat16)
        for h in range(group):
            cols = cols_of(h)
            before = dq_in_ref[:, cols].astype(jnp.float32) if fresh else total_ref[:, cols]
            put(cols, before + dot(ds_ref[here, h * rows : (h + 1) * rows], k, TN))

    def skip(members, fresh):
        if fresh:
            for h in range(group):
                put(cols_of(h), dq_in_ref[:, cols_of(h)].astype(jnp.float32))
        for m in members:
            dkv_refs[m][...] = jnp.zeros_like(dkv_refs[m])

    start = 0
    for i, size in enumerate(joint):
        members = tuple(range(start, start + size))
        start += size
        if ours:
            counts = info_ref[0] > i
        else:
            counts = anc_ref[place_ref[info_ref[1]]] >= 0
        pl.when(counts)(functools.partial(run, members, i == 0))
        pl.when(jnp.logical_not(counts))(functools.partial(skip, members, i == 0))
    if sets > 1:
        for h in range(group):
            total = total_ref[:, cols_of(h)]
            if final:
                total = turn_back(total, c, s)
            dq_ref[:, cols_of(h)] = total.astype(jnp.bfloat16)


def cross(kv_count, first, count, tree, ours, joint, rq, do, lse, delta, c, s, dq, kvs, whole=None, final=False):
    rows, width = do.shape
    group = heads_of(width, kv_count)
    wide = group * HEAD_SIZE
    most = max(joint)
    big = pl.BlockSpec((rows, wide), lambda g, *_: (0, g + first))
    row = pl.BlockSpec((group, rows), lambda g, *_: (g + first, 0))
    table = pl.BlockSpec((rows, HEAD_SIZE), lambda g, *_: (0, 0))
    pair = pl.BlockSpec((rows, 2 * HEAD_SIZE), lambda g, *_: (0, g))
    args = [*tree, rq, do, lse, delta, c, s, dq]
    args += [x for x in kvs] if not ours else [y for x, kc, ks in kvs for y in (x, x, kc, ks)]
    in_specs = [big, big, row, row, table, table, big]
    if ours:
        keys_at = pl.BlockSpec((rows, HEAD_SIZE), lambda g, *_: (0, g + first))
        values_at = pl.BlockSpec((rows, HEAD_SIZE), lambda g, *_: (0, g + first + kv_count))
        in_specs += [keys_at, values_at, table, table] * len(kvs)
    else:
        in_specs += [pair] * len(kvs)
    mode = 0
    aliases = {}
    if final:
        mode = 1
        if whole is not None:
            mode = 2
            aliases = {len(args): 0}
            args.append(whole)
            in_specs.append(pl.BlockSpec(memory_space=pl.ANY))
    dq_shape = (
        jax.ShapeDtypeStruct((rows, width), jnp.bfloat16)
        if final
        else jax.ShapeDtypeStruct(dq.shape, jnp.bfloat16)
    )
    return pl.pallas_call(
        functools.partial(cross_kernel, group, joint, mode, ours),
        out_shape=[dq_shape]
        + [jax.ShapeDtypeStruct((rows, count * 2 * HEAD_SIZE), jnp.bfloat16)] * len(kvs),
        grid_spec=pltpu.PrefetchScalarGridSpec(
            num_scalar_prefetch=3,
            grid=(count,),
            in_specs=in_specs,
            out_specs=[big] + [pair] * len(kvs),
            scratch_shapes=[pltpu.VMEM((most * rows, group * rows), jnp.bfloat16)] * 2
            + [pltpu.VMEM((most * rows, HEAD_SIZE), jnp.bfloat16)] * 2
            + ([pltpu.VMEM((rows, wide), jnp.float32)] if len(joint) > 1 else []),
        ),
        input_output_aliases=aliases,
        compiler_params=params(1, 60),
        cost_estimate=pl.CostEstimate(
            flops=20 * count * group * rows * rows * HEAD_SIZE * len(kvs),
            bytes_accessed=rows * count * wide * 12,
            transcendentals=0,
        ),
        name="cross",
    )(*args)


def settle_kernel(counts, own_ref, c_ref, s_ref, *refs):
    *in_refs, o_ref = refs
    c, s = c_ref[...], s_ref[...]
    a = 0
    for count in counts:
        mine, in_refs = in_refs[:count], in_refs[count:]
        for b in range(0, mine[0].shape[1], 2 * HEAD_SIZE):
            total = own_ref[:, a : a + 2 * HEAD_SIZE]
            for ref in mine:
                total = total + ref[:, b : b + 2 * HEAD_SIZE].astype(jnp.float32)
            o_ref[:, a : a + HEAD_SIZE] = turn_back(total[:, :HEAD_SIZE], c, s)
            o_ref[:, a + HEAD_SIZE : a + 2 * HEAD_SIZE] = total[:, HEAD_SIZE:]
            a += 2 * HEAD_SIZE


def settle(local, chunks, c, s):
    return pl.pallas_call(
        functools.partial(settle_kernel, [len(x) for x in chunks]),
        out_shape=jax.ShapeDtypeStruct(local.shape, jnp.float32),
        compiler_params=params(0, 12),
        name="settle",
    )(local, c, s, *[x for chunk in chunks for x in chunk])


def finish_kernel(own_ref, children_ref, dk_ref, dv_ref):
    for g in range(dk_ref.shape[1] // HEAD_SIZE):
        a, b = g * HEAD_SIZE, 2 * g * HEAD_SIZE
        total = own_ref[:, b : b + 2 * HEAD_SIZE]
        total = total + children_ref[:, b : b + 2 * HEAD_SIZE].astype(jnp.float32)
        dk_ref[:, a : a + HEAD_SIZE] = total[:, :HEAD_SIZE].astype(jnp.bfloat16)
        dv_ref[:, a : a + HEAD_SIZE] = total[:, HEAD_SIZE:].astype(jnp.bfloat16)


def finish(base, children):
    rows, width = base.shape
    return pl.pallas_call(
        finish_kernel,
        out_shape=[jax.ShapeDtypeStruct((rows, width // 2), jnp.bfloat16)] * 2,
        compiler_params=params(0, 8),
        name="finish",
    )(base, children)


def body(
    queries,
    unrotated_keys,
    value_rows,
    outputs,
    output_gradient,
    saved_logsumexp,
    ancestors,
    placement,
    positions,
):
    hops = lax.axis_size("head")
    places = lax.axis_size("ctx")
    here = lax.axis_index("ctx")
    me = lax.axis_index("head")
    rows = queries.shape[0]
    assert rows * hops == TREE_BLOCK and placement.shape[0] == places
    assert ancestors.shape[1] == 1
    c, s = rope_tables(positions)

    parents = ancestors.reshape(-1)
    tree = (jnp.stack([me, here]).astype(jnp.int32), placement, parents)

    kv_count = unrotated_keys.shape[1] // HEAD_SIZE
    sizes = split(kv_count)
    chunks = range(len(sizes))
    firsts = [sum(sizes[:g]) for g in chunks]

    def exchange(x):
        width = x.shape[-1]
        return lax.all_to_all(
            x.reshape(places, rows // places, width), "ctx", 0, 0, tiled=True
        )

    def shift(x, n, wrap):
        route = [(i, (i + n) % hops) for i in range(hops) if wrap or 0 <= i + n < hops]
        return lax.ppermute(x, "head", route)

    raw = jnp.concatenate([unrotated_keys, value_rows], 1)

    piece_rows = rows // places
    offset = me * rows + here * piece_rows + jnp.arange(piece_rows, dtype=jnp.int32)
    middle_at = (TREE_BLOCK * placement[:, None] + offset[None, :]).reshape(-1)
    middle_c, middle_s = [
        t.reshape(places, piece_rows, HEAD_SIZE) for t in rope_tables(middle_at)
    ]

    middle = exchange(raw)
    own_kv = [(shift(raw, n, False), *rope_tables(positions - n * rows)) for n in range(1, hops)]
    rq, delta, dq, local = diagonal(
        queries, output_gradient, outputs, saved_logsumexp, c, s, unrotated_keys, value_rows
    )
    picked = pick(sizes, placement, parents, middle, middle_c, middle_s)
    near = []
    for g in chunks:
        send = picked[g]
        if g:
            send, near[-1] = lax.optimization_barrier((send, near[-1]))
        near.append(exchange(send))
    near = [x.reshape(rows, -1) for x in near]

    far = []
    for g in chunks:
        far.append([shift(near[g], n, True) for n in range(1, hops)])

    def tiles(g, dq, kvs, ours, joint, whole=None, final=False):
        return cross(
            kv_count, firsts[g], sizes[g], tree, ours, joint, rq, output_gradient,
            saved_logsumexp, delta, c, s, dq, kvs, whole, final,
        )

    grad_queries = None
    ups, backs = [], []
    for g in chunks:

        def peers(part, *rest):
            return tiles(g, part, own_kv, True, (1,) * (hops - 1), *rest)

        def parent(part, *rest):
            return tiles(g, part, [near[g]], False, (1,), *rest)

        def beyond(part, *rest):
            return tiles(g, part, far[g], False, (hops - 1,), *rest)

        if g == 0:
            part, *own_part = peers(dq)
            part, near_part = parent(part)
            grad_queries, *far_part = beyond(part, None, True)
        else:
            part, *far_part = beyond(dq)
            part, near_part = parent(part)
            grad_queries, *own_part = peers(part, grad_queries, True)
        backs.append([shift(x, -n - 1, False) for n, x in enumerate(own_part)])
        joined = [shift(x, -n - 1, True) for n, x in enumerate(far_part)]
        total = near_part.astype(jnp.float32)
        for x in joined:
            total = total + x.astype(jnp.float32)
        send = total.astype(jnp.bfloat16)
        if g:
            send, ups[-1] = lax.optimization_barrier((send, ups[-1]))
        ups.append(exchange(send))
    base = settle(local, backs, c, s)
    merged = merge(placement, parents, middle_c, middle_s, ups)
    children = exchange(merged).reshape(rows, -1)
    grad_keys, grad_values = finish(base, children)
    return (grad_queries, grad_keys, grad_values)


def split(kv_count):
    return (kv_count // 2, kv_count - kv_count // 2)


def solution(mesh):
    return jax.shard_map(
        body,
        mesh=mesh,
        in_specs=(
            P(("ctx", "head"), None),
            P(("ctx", "head"), None),
            P(("ctx", "head"), None),
            P(("ctx", "head"), None),
            P(("ctx", "head"), None),
            P(None, ("ctx", "head")),
            P(),
            P(),
            P(("ctx", "head")),
        ),
        out_specs=(P(("ctx", "head"), None), P(("ctx", "head"), None), P(("ctx", "head"), None)),
        check_vma=False,
    )
```

time: 224 us -> 211 us (0.942)
  waiting for transfers between devices: 67.4 us -> 53.3 us
  Pallas kernels: 86.4 us -> 76.8 us
  starting transfers between devices: 38 us -> 43.4 us
  local copies, waits for them, and re-layouts: 6.52 us -> 9.81 us
    pallas_call x9 -> x8, Pallas kernels: 64 us -> 54.6 us  [the longest x6 52.3 us: cross(): pl.pallas_call(functools.partial(cross_kernel, group, joint, mode, ours),...]
    ppermute x6 -> x7, waiting for transfers between devices: 46.7 us -> 38.1 us  [shift(): return lax.ppermute(x, 'head', route)]
    all_to_all x4 -> x5, starting transfers between devices: 23.6 us -> 29.5 us  [exchange(): lax.all_to_all(x.reshape(places, rows // places, width), 'ctx', 0, 0, til...]
    all_to_all x4 -> x5, waiting for transfers between devices: 20.6 us -> 15.2 us  [exchange(): lax.all_to_all(x.reshape(places, rows // places, width), 'ctx', 0, 0, til...]
    unnamed x24 -> x35, local copies, waits for them, and re-layouts: 5.15 us -> 7.94 us
    ppermute x6 -> x7, starting transfers between devices: 14.4 us -> 13.9 us  [shift(): return lax.ppermute(x, 'head', route)]
  transfers between devices with their start and end apart: 10 -> 12, of which waited for: 6 -> 6; matrix products, arithmetic and copies ran while one was open for 3% -> 3% of each run, Pallas kernels for 31% -> 35%
where the time goes in v4:
time: 211 us; the launch traced here: 209 us
  Pallas kernels  76.8 us (36%)
  waiting for transfers between devices  53.3 us (25%)
  starting transfers between devices  43.4 us (21%)
  blocking collectives  18.6 us (9%)
  local copies, waits for them, and re-layouts  9.81 us (5%)
  other arithmetic  6.37 us (3%)
    pallas_call x6, Pallas kernels, cross(): pl.pallas_call(functools.partial(cross_kernel, group, joint, mode, ours),...  52.3 us
    ppermute x7, waiting for transfers between devices, shift(): return lax.ppermute(x, 'head', route)  38.1 us
    all_to_all x5, starting transfers between devices, exchange(): lax.all_to_all(x.reshape(places, rows // places, width), 'ctx', 0, 0, til...  29.5 us
    all_to_all x1, blocking collectives, exchange(): lax.all_to_all(x.reshape(places, rows // places, width), 'ctx', 0, 0, til...  18.6 us
    pallas_call x1, Pallas kernels, diagonal(): pl.pallas_call(functools.partial(diagonal_kernel, group), out_shape=[jax....  18.5 us
    all_to_all x5, waiting for transfers between devices, exchange(): lax.all_to_all(x.reshape(places, rows // places, width), 'ctx', 0, 0, til...  15.2 us
    ppermute x7, starting transfers between devices, shift(): return lax.ppermute(x, 'head', route)  13.9 us
    unnamed x35, local copies, waits for them, and re-layouts  7.94 us
  transfers between devices with their start and end apart: 12, of which 6 were waited for; matrix products, arithmetic and copies ran while one was open for 3% of the time, Pallas kernels for 35%

profile of v4, /device:TPU:0, one launch (start us, length us, event | category | flops | bytes accessed | tf_op | source)
XLA Modules:
  0.0 209.2 jit_solution(16138721089070570036)
XLA Ops:
  0.7 1.9 constant_dynamic-update-slice_fusion.1
  2.5 1.9 constant_dynamic-update-slice_fusion
  4.4 7.4 %all-to-all-start = ((bf16[16,16,2048]{2,1,0:T(8,128)(2,1)}), bf16[16,16,2048]{2,1,0:T(8,128)(2,1)S(1)}, u32[]{:S(2)}, u32[]{:S(2)}) async-start(bf16[16,16,2048]{2,1,0:T(8,128)(2,1)} %bitcast.3), calls=%async_computation | async-start | bytes 2097152 | tf_op jit(solution)/shard_map/all_to_all | solution.py:417
  11.8 3.5 %collective-permute-start.1 = (bf16[256,2048]{1,0:T(8,128)(2,1)}, bf16[256,2048]{1,0:T(8,128)(2,1)S(1)}, u32[]{:S(2)}, u32[]{:S(2)}) collective-permute-start(bf16[256,2048]{1,0:T(8,128)(2,1)} %constant_dynamic-update-slice_fusion), channel_id=1, source_target_pairs={{0,16},{1,17},{2,18},{3,19},{4,20},{5,21},{6,22},{7,23},{8,24},{9,... | collective-permute-start | bytes 3145736 | tf_op jit(solution)/shard_map/ppermute | solution.py:423
  19.5 15.2 %all-to-all-done.x_ref = bf16[16,16,2048]{2,1,0:T(8,128)(2,1)S(1)} async-done(((bf16[16,16,2048]{2,1,0:T(8,128)(2,1)}), bf16[16,16,2048]{2,1,0:T(8,128)(2,1)S(1)}, u32[]{:S(2)}, u32[]{:S(2)}) %all-to-all-start) | async-done | bytes 1048608 | tf_op jit(solution)/shard_map/all_to_all | solution.py:417
  34.7 1.9 pick.1
  36.6 6.8 %all-to-all-start.1 = ((bf16[16,16,1024]{2,1,0:T(8,128)(2,1)}), bf16[16,16,1024]{2,1,0:T(8,128)(2,1)S(1)}, u32[]{:S(2)}, u32[]{:S(2)}) async-start(bf16[16,16,1024]{2,1,0:T(8,128)(2,1)} %get-tuple-element.31), calls=%async_computation.1 | async-start | bytes 1048576 | tf_op jit(solution)/shard_map/all_to_all | solution.py:417
  43.4 18.5 %diagonal.1 = (bf16[256,8192]{1,0:T(8,128)(2,1)}, f32[64,256]{1,0:T(8,128)}, bf16[256,8192]{1,0:T(8,128)(2,1)}, f32[256,2048]{1,0:T(8,128)}) custom-call(bf16[256,8192]{1,0:T(8,128)(2,1)} %q_ref.1, bf16[256,8192]{1,0:T(8,128)(2,1)} %do_ref.13, bf16[256,8192]{1,0:T(8,128)(2,1)} %out_ref.1, f32[64,256]{1,0:T(8,128)} %lse_ref.13, ...), custom_call_target="tpu_custom_call" | custom-call | flops 10737418240 | bytes 25165824 | tf_op jit(solution)/shard_map/diagonal/pallas_call | solution.py:186
  61.9 1.6 collective-permute-start.2
  64.5 6.1 %cross.8 = (bf16[256,8192]{1,0:T(8,128)(2,1)}, bf16[256,1024]{1,0:T(8,128)(2,1)}) custom-call(s32[2]{0:T(128)} %pad_add_fusion.info_ref, s32[16]{0:T(128)} %place_ref.15, s32[16]{0:T(128)} %bitcast.10, bf16[256,8192]{1,0:T(8,128)(2,1)} %get-tuple-element.27.rq_ref, bf16[256,8192]{1,0:T(8,128)(2,1)} %do_ref.13, f32[64,256]{1,0:T(8,128)} %lse_ref.13, ...), custom_call_target="tpu_custom_call" | custom-call | flops 5368709120 | bytes 12582912 | tf_op jit(solution)/shard_map/cross/pallas_call | solution.py:320
  70.6 6.0 %all-to-all-start.2 = ((bf16[16,16,1024]{2,1,0:T(8,128)(2,1)}), bf16[16,16,1024]{2,1,0:T(8,128)(2,1)S(1)}, u32[]{:S(2)}, u32[]{:S(2)}) async-start(bf16[16,16,1024]{2,1,0:T(8,128)(2,1)} %get-tuple-element.32), calls=%async_computation.2 | async-start | bytes 1048576 | tf_op jit(solution)/shard_map/all_to_all | solution.py:417
  76.6 9.7 %cross.9 = (bf16[256,8192]{1,0:T(8,128)(2,1)}, bf16[256,1024]{1,0:T(8,128)(2,1)}) custom-call(s32[2]{0:T(128)} %pad_add_fusion.info_ref, s32[16]{0:T(128)} %place_ref.15, s32[16]{0:T(128)} %bitcast.11, bf16[256,8192]{1,0:T(8,128)(2,1)} %get-tuple-element.27.rq_ref, bf16[256,8192]{1,0:T(8,128)(2,1)} %do_ref.13, f32[64,256]{1,0:T(8,128)} %lse_ref.13, ...), custom_call_target="tpu_custom_call" | custom-call | flops 5368709120 | bytes 12582912 | tf_op jit(solution)/shard_map/cross/pallas_call | solution.py:320
  87.1 10.2 %cross.10 = (bf16[256,8192]{1,0:T(8,128)(2,1)}, bf16[256,1024]{1,0:T(8,128)(2,1)}) custom-call(s32[2]{0:T(128)} %pad_add_fusion.info_ref, s32[16]{0:T(128)} %place_ref.15, s32[16]{0:T(128)} %bitcast.12, bf16[256,8192]{1,0:T(8,128)(2,1)} %get-tuple-element.27.rq_ref, bf16[256,8192]{1,0:T(8,128)(2,1)} %do_ref.13, f32[64,256]{1,0:T(8,128)} %lse_ref.13, ...), custom_call_target="tpu_custom_call" | custom-call | flops 5368709120 | bytes 12582912 | tf_op jit(solution)/shard_map/cross/pallas_call | solution.py:320
  97.3 4.4 %collective-permute-start.6 = (bf16[256,1024]{1,0:T(8,128)(2,1)}, bf16[256,1024]{1,0:T(8,128)(2,1)S(1)}, u32[]{:S(2)}, u32[]{:S(2)}) collective-permute-start(bf16[256,1024]{1,0:T(8,128)(2,1)} %get-tuple-element.46), channel_id=1, source_target_pairs={{0,16},{16,0},{1,17},{17,1},{2,18},{18,2},{3,19},{19,3},{4,20},{20... | collective-permute-start | bytes 1572872 | tf_op jit(solution)/shard_map/ppermute | solution.py:423
  101.8 12.9 %collective-permute-done.6 = bf16[256,1024]{1,0:T(8,128)(2,1)S(1)} collective-permute-done((bf16[256,1024]{1,0:T(8,128)(2,1)}, bf16[256,1024]{1,0:T(8,128)(2,1)S(1)}, u32[]{:S(2)}, u32[]{:S(2)}) %collective-permute-start.6) | collective-permute-done | bytes 524320 | tf_op jit(solution)/shard_map/ppermute | solution.py:423
  115.7 5.1 %all-to-all-start.3 = ((bf16[16,16,1024]{2,1,0:T(8,128)(2,1)}), bf16[16,16,1024]{2,1,0:T(8,128)(2,1)S(1)}, u32[]{:S(2)}, u32[]{:S(2)}) async-start(bf16[16,16,1024]{2,1,0:T(8,128)(2,1)} %bitcast.6), calls=%async_computation.3 | async-start | bytes 1048576 | tf_op jit(solution)/shard_map/all_to_all | solution.py:417
  120.8 4.8 %collective-permute-done.refs_0_ = bf16[256,1024]{1,0:T(8,128)(2,1)S(1)} collective-permute-done((bf16[256,1024]{1,0:T(8,128)(2,1)S(1)}, bf16[256,1024]{1,0:T(8,128)(2,1)S(1)}, u32[]{:S(2)}, u32[]{:S(2)}) %collective-permute-start) | collective-permute-done | bytes 524320 | tf_op jit(solution)/shard_map/ppermute | solution.py:423
  126.4 9.7 %cross.6 = (bf16[256,8192]{1,0:T(8,128)(2,1)}, bf16[256,1024]{1,0:T(8,128)(2,1)}) custom-call(s32[2]{0:T(128)} %pad_add_fusion.info_ref, s32[16]{0:T(128)} %place_ref.15, s32[16]{0:T(128)} %bitcast.13, bf16[256,8192]{1,0:T(8,128)(2,1)} %get-tuple-element.27.rq_ref, bf16[256,8192]{1,0:T(8,128)(2,1)} %do_ref.13, f32[64,256]{1,0:T(8,128)} %lse_ref.13, ...), custom_call_target="tpu_custom_call" | custom-call | flops 5368709120 | bytes 12582912 | tf_op jit(solution)/shard_map/cross/pallas_call | solution.py:320
  136.2 1.8 collective-permute-start.5
  138.0 9.9 %cross.7 = (bf16[256,8192]{1,0:T(8,128)(2,1)}, bf16[256,1024]{1,0:T(8,128)(2,1)}) custom-call(s32[2]{0:T(128)} %pad_add_fusion.info_ref, s32[16]{0:T(128)} %place_ref.15, s32[16]{0:T(128)} %bitcast.14, bf16[256,8192]{1,0:T(8,128)(2,1)} %get-tuple-element.27.rq_ref, bf16[256,8192]{1,0:T(8,128)(2,1)} %do_ref.13, f32[64,256]{1,0:T(8,128)} %lse_ref.13, ...), custom_call_target="tpu_custom_call" | custom-call | flops 5368709120 | bytes 12582912 | tf_op jit(solution)/shard_map/cross/pallas_call | solution.py:320
  147.8 2.3 %collective-permute-done.5 = bf16[256,1024]{1,0:T(8,128)(2,1)S(1)} collective-permute-done((bf16[256,1024]{1,0:T(8,128)(2,1)}, bf16[256,1024]{1,0:T(8,128)(2,1)S(1)}, u32[]{:S(2)}, u32[]{:S(2)}) %collective-permute-start.5) | collective-permute-done | bytes 524320 | tf_op jit(solution)/shard_map/ppermute | solution.py:423
  150.1 1.2 add_convert_fusion.1
  151.3 18.6 %all_to_all.30.refs_1_ = bf16[16,16,1024]{2,1,0:T(8,128)(2,1)S(1)} all-to-all(bf16[16,16,1024]{2,1,0:T(8,128)(2,1)S(1)} %bitcast.18), channel_id=1, replica_groups=mesh['head'=2,'ctx'=16] {'ctx'}, dimensions={0} | all-to-all | bytes 1048576 | tf_op jit(solution)/shard_map/all_to_all | solution.py:417
  170.0 2.4 %merge.1 = bf16[16,16,2048]{2,1,0:T(8,128)(2,1)} custom-call(s32[16]{0:T(128)S(1)} %copy-done.6, s32[16]{0:T(128)S(1)} %bitcast.17, f32[16,16,128]{2,1,0:T(8,128)S(1)} %get-tuple-element.69.c_ref, f32[16,16,128]{2,1,0:T(8,128)S(1)} %get-tuple-element.70.s_ref, bf16[16,16,1024]{2,1,0:T(8,128)(2,1)S(1)} %all-to-all-done.3.refs_0_, ...), custom_call_target="tpu_custom_call" | custom-call | tf_op jit(solution)/shard_map/merge/pallas_call | solution.py:115
  172.4 4.2 %all-to-all-start.5 = ((bf16[16,16,2048]{2,1,0:T(8,128)(2,1)}), bf16[16,16,2048]{2,1,0:T(8,128)(2,1)S(1)}, u32[]{:S(2)}, u32[]{:S(2)}) async-start(bf16[16,16,2048]{2,1,0:T(8,128)(2,1)} %merge.1), calls=%async_computation.5 | async-start | bytes 2097152 | tf_op jit(solution)/shard_map/all_to_all | solution.py:417
  176.6 1.3 collective-permute-start.3
  177.9 6.8 %cross.11 = (bf16[256,8192]{1,0:T(8,128)(2,1)}, bf16[256,1024]{1,0:T(8,128)(2,1)}) custom-call(s32[2]{0:T(128)} %pad_add_fusion.info_ref, s32[16]{0:T(128)} %place_ref.15, s32[16]{0:T(128)} %bitcast.15, bf16[256,8192]{1,0:T(8,128)(2,1)} %get-tuple-element.27.rq_ref, bf16[256,8192]{1,0:T(8,128)(2,1)} %do_ref.13, ...), custom_call_target="tpu_custom_call", output_to_operand_aliasing={{0}: (14, {})} | custom-call | flops 5368709120 | bytes 12582912 | tf_op jit(solution)/shard_map/cross/pallas_call | solution.py:320
  184.7 1.3 collective-permute-start.4
  186.0 6.7 %collective-permute-done.3.refs_0_ = bf16[256,1024]{1,0:T(8,128)(2,1)S(1)} collective-permute-done((bf16[256,1024]{1,0:T(8,128)(2,1)S(1)}, bf16[256,1024]{1,0:T(8,128)(2,1)S(1)}, u32[]{:S(2)}, u32[]{:S(2)}) %collective-permute-start.3) | collective-permute-done | bytes 524320 | tf_op jit(solution)/shard_map/ppermute | solution.py:423
  193.5 11.4 %collective-permute-done.4.refs_1_ = bf16[256,1024]{1,0:T(8,128)(2,1)S(1)} collective-permute-done((bf16[256,1024]{1,0:T(8,128)(2,1)}, bf16[256,1024]{1,0:T(8,128)(2,1)S(1)}, u32[]{:S(2)}, u32[]{:S(2)}) %collective-permute-start.4) | collective-permute-done | bytes 524320 | tf_op jit(solution)/shard_map/ppermute | solution.py:423
  204.9 1.6 copy-done
  207.9 1.3 finish.1
  (53 shorter events, 10.1 us)
Async XLA Ops:
  0.6 14.7 %copy-start.12 = (s32[256]{0:T(256)S(1)}, s32[256]{0:T(256)}, u32[]{:S(2)}) copy-start(s32[256]{0:T(256)} %param.17) | copy-start | bytes 3076
  0.6 17.4 %copy-start.5 = (s32[16]{0:T(128)S(1)}, s32[16]{0:T(128)}, u32[]{:S(2)}) copy-start(s32[16]{0:T(128)} %place_ref.15) | copy-start | bytes 196
  0.7 34.1 %copy-start.7 = (s32[16,1]{0,1:T(1,128)S(1)}, s32[16,1]{0,1:T(1,128)}, u32[]{:S(2)}) copy-start(s32[16,1]{0,1:T(1,128)} %param.15) | copy-start | bytes 196
  4.4 30.3 %all-to-all-start = ((bf16[16,16,2048]{2,1,0:T(8,128)(2,1)}), bf16[16,16,2048]{2,1,0:T(8,128)(2,1)S(1)}, u32[]{:S(2)}, u32[]{:S(2)}) async-start(bf16[16,16,2048]{2,1,0:T(8,128)(2,1)} %bitcast.3), calls=%async_computation | async-start | bytes 2097152 | tf_op jit(solution)/shard_map/all_to_all | solution.py:417
  11.8 51.6 %collective-permute-start.1 = (bf16[256,2048]{1,0:T(8,128)(2,1)}, bf16[256,2048]{1,0:T(8,128)(2,1)S(1)}, u32[]{:S(2)}, u32[]{:S(2)}) collective-permute-start(bf16[256,2048]{1,0:T(8,128)(2,1)} %constant_dynamic-update-slice_fusion), channel_id=1, source_target_pairs={{0,16},{1,17},{2,18},{3,19},{4,20},{5,21},{6,22},{7,23},{8,24},{9,... | collective-permute-start | bytes 3145736 | tf_op jit(solution)/shard_map/ppermute | solution.py:423
  36.6 25.3 %all-to-all-start.1 = ((bf16[16,16,1024]{2,1,0:T(8,128)(2,1)}), bf16[16,16,1024]{2,1,0:T(8,128)(2,1)S(1)}, u32[]{:S(2)}, u32[]{:S(2)}) async-start(bf16[16,16,1024]{2,1,0:T(8,128)(2,1)} %get-tuple-element.31), calls=%async_computation.1 | async-start | bytes 1048576 | tf_op jit(solution)/shard_map/all_to_all | solution.py:417
  61.9 8.7 %copy-start.11 = (bf16[16,16,1024]{2,1,0:T(8,128)(2,1)}, bf16[16,16,1024]{2,1,0:T(8,128)(2,1)S(1)}, u32[]{:S(2)}) copy-start(bf16[16,16,1024]{2,1,0:T(8,128)(2,1)S(1)} %all-to-all-done.1) | copy-start | bytes 1572868
  61.9 24.3 %collective-permute-start.2 = (bf16[256,1024]{1,0:T(8,128)(2,1)S(1)}, bf16[256,1024]{1,0:T(8,128)(2,1)S(1)}, u32[]{:S(2)}, u32[]{:S(2)}) collective-permute-start(bf16[256,1024]{1,0:T(8,128)(2,1)S(1)} %bitcast.21), channel_id=1, source_target_pairs={{0,16},{16,0},{1,17},{17,1},{2,18},{18,2},{3,19},{19,3},{4,20},{20... | collective-permute-start | bytes 1572872 | tf_op jit(solution)/shard_map/ppermute | solution.py:423
  63.5 1.0 copy-start.13
  70.6 31.2 %all-to-all-start.2 = ((bf16[16,16,1024]{2,1,0:T(8,128)(2,1)}), bf16[16,16,1024]{2,1,0:T(8,128)(2,1)S(1)}, u32[]{:S(2)}, u32[]{:S(2)}) async-start(bf16[16,16,1024]{2,1,0:T(8,128)(2,1)} %get-tuple-element.32), calls=%async_computation.2 | async-start | bytes 1048576 | tf_op jit(solution)/shard_map/all_to_all | solution.py:417
  86.3 0.8 copy-start.15
  87.1 27.6 %copy-start.9 = (bf16[256,1024]{1,0:T(8,128)(2,1)S(1)}, bf16[256,1024]{1,0:T(8,128)(2,1)}, u32[]{:S(2)}) copy-start(bf16[256,1024]{1,0:T(8,128)(2,1)} %get-tuple-element.45) | copy-start | bytes 1572868
  97.3 17.4 %collective-permute-start.6 = (bf16[256,1024]{1,0:T(8,128)(2,1)}, bf16[256,1024]{1,0:T(8,128)(2,1)S(1)}, u32[]{:S(2)}, u32[]{:S(2)}) collective-permute-start(bf16[256,1024]{1,0:T(8,128)(2,1)} %get-tuple-element.46), channel_id=1, source_target_pairs={{0,16},{16,0},{1,17},{17,1},{2,18},{18,2},{3,19},{19,3},{4,20},{20... | collective-permute-start | bytes 1572872 | tf_op jit(solution)/shard_map/ppermute | solution.py:423
  101.7 34.4 %copy-start.10 = (bf16[16,16,1024]{2,1,0:T(8,128)(2,1)}, bf16[16,16,1024]{2,1,0:T(8,128)(2,1)S(1)}, u32[]{:S(2)}) copy-start(bf16[16,16,1024]{2,1,0:T(8,128)(2,1)S(1)} %all-to-all-done.2) | copy-start | bytes 1572868
  101.7 23.9 %collective-permute-start = (bf16[256,1024]{1,0:T(8,128)(2,1)S(1)}, bf16[256,1024]{1,0:T(8,128)(2,1)S(1)}, u32[]{:S(2)}, u32[]{:S(2)}) collective-permute-start(bf16[256,1024]{1,0:T(8,128)(2,1)S(1)} %bitcast.19), channel_id=1, source_target_pairs={{0,16},{16,0},{1,17},{17,1},{2,18},{18,2},{3,19},{19,3},{4,20},{20... | collective-permute-start | bytes 1572872 | tf_op jit(solution)/shard_map/ppermute | solution.py:423
  115.7 35.6 %all-to-all-start.3 = ((bf16[16,16,1024]{2,1,0:T(8,128)(2,1)}), bf16[16,16,1024]{2,1,0:T(8,128)(2,1)S(1)}, u32[]{:S(2)}, u32[]{:S(2)}) async-start(bf16[16,16,1024]{2,1,0:T(8,128)(2,1)} %bitcast.6), calls=%async_computation.3 | async-start | bytes 1048576 | tf_op jit(solution)/shard_map/all_to_all | solution.py:417
  125.6 0.8 copy-start.16
  136.2 13.9 %collective-permute-start.5 = (bf16[256,1024]{1,0:T(8,128)(2,1)}, bf16[256,1024]{1,0:T(8,128)(2,1)S(1)}, u32[]{:S(2)}, u32[]{:S(2)}) collective-permute-start(bf16[256,1024]{1,0:T(8,128)(2,1)} %get-tuple-element.44), channel_id=1, source_target_pairs={{0,16},{16,0},{1,17},{17,1},{2,18},{18,2},{3,19},{19,3},{4,20},{20... | collective-permute-start | bytes 1572872 | tf_op jit(solution)/shard_map/ppermute | solution.py:423
  138.0 32.0 %copy-start.6 = (s32[16]{0:T(128)S(1)}, s32[16]{0:T(128)}, u32[]{:S(2)}) copy-start(s32[16]{0:T(128)} %place_ref.15) | copy-start | bytes 196
  138.0 32.0 %copy-start.8 = (s32[16,1]{0,1:T(1,128)S(1)}, s32[16,1]{0,1:T(1,128)}, u32[]{:S(2)}) copy-start(s32[16,1]{0,1:T(1,128)} %param.15) | copy-start | bytes 196
  147.8 28.7 %copy-start.14 = (bf16[256,1024]{1,0:T(8,128)(2,1)S(1)}, bf16[256,1024]{1,0:T(8,128)(2,1)}, u32[]{:S(2)}) copy-start(bf16[256,1024]{1,0:T(8,128)(2,1)} %get-tuple-element.41) | copy-start | bytes 1572868
  172.4 35.5 %all-to-all-start.5 = ((bf16[16,16,2048]{2,1,0:T(8,128)(2,1)}), bf16[16,16,2048]{2,1,0:T(8,128)(2,1)S(1)}, u32[]{:S(2)}, u32[]{:S(2)}) async-start(bf16[16,16,2048]{2,1,0:T(8,128)(2,1)} %merge.1), calls=%async_computation.5 | async-start | bytes 2097152 | tf_op jit(solution)/shard_map/all_to_all | solution.py:417
  176.6 16.1 %collective-permute-start.3 = (bf16[256,1024]{1,0:T(8,128)(2,1)S(1)}, bf16[256,1024]{1,0:T(8,128)(2,1)S(1)}, u32[]{:S(2)}, u32[]{:S(2)}) collective-permute-start(bf16[256,1024]{1,0:T(8,128)(2,1)S(1)} %copy-done.14), channel_id=1, source_target_pairs={{16,0},{17,1},{18,2},{19,3},{20,4},{21,5},{22,6},{23,7},{24,8},{25... | collective-permute-start | bytes 1572872 | tf_op jit(solution)/shard_map/ppermute | solution.py:423
  177.9 27.0 %copy-start.1 = (f32[256,128]{1,0:T(8,128)S(1)}, f32[256,128]{1,0:T(8,128)}, u32[]{:S(2)}) copy-start(f32[256,128]{1,0:T(8,128)} %get-tuple-element.65.c_ref) | copy-start | bytes 393220
  177.9 27.0 %copy-start.2 = (f32[256,128]{1,0:T(8,128)S(1)}, f32[256,128]{1,0:T(8,128)}, u32[]{:S(2)}) copy-start(f32[256,128]{1,0:T(8,128)} %get-tuple-element.66.s_ref) | copy-start | bytes 393220
  184.7 20.2 %collective-permute-start.4 = (bf16[256,1024]{1,0:T(8,128)(2,1)}, bf16[256,1024]{1,0:T(8,128)(2,1)S(1)}, u32[]{:S(2)}, u32[]{:S(2)}) collective-permute-start(bf16[256,1024]{1,0:T(8,128)(2,1)} %get-tuple-element.42), channel_id=1, source_target_pairs={{16,0},{17,1},{18,2},{19,3},{20,4},{21,5},{22,6},{23,7},{24,8},{25... | collective-permute-start | bytes 1572872 | tf_op jit(solution)/shard_map/ppermute | solution.py:423
  192.7 0.8 copy-start.3
  204.9 1.6 copy-start
  206.5 1.0 copy-start.4

commit v5 on v4

--- a/solution.py
+++ b/solution.py
@@ -22,12 +22,13 @@
 
 
 def rope_tables(positions):
+    lane = jnp.arange(HEAD_SIZE, dtype=jnp.int32)
     half_dim = HEAD_SIZE // 2
-    freq_index = jnp.arange(half_dim, dtype=jnp.float32)
+    freq_index = (lane % half_dim).astype(jnp.float32)
     inverse = rope_base ** (-(2.0 * freq_index / HEAD_SIZE))
     angles = positions.astype(jnp.float32)[:, None] * inverse[None, :]
-    c, s = jnp.cos(angles), jnp.sin(angles)
-    return jnp.concatenate([c, c], -1), jnp.concatenate([-s, s], -1)
+    sign = jnp.where(lane < half_dim, -1.0, 1.0)
+    return jnp.cos(angles), jnp.sin(angles) * sign[None, :]
 
 
 def dot(a, b, dims):
@@ -48,12 +49,49 @@
     )
 
 
+def side_kernel(pieces, k_ref, v_ref, o_ref, buf, sem_in, sem_out):
+    rows, width = k_ref.shape
+    step = rows // pieces
+    ins, outs = [], []
+    for i in range(2 * pieces):
+        part, x_ref = i // pieces, (k_ref, v_ref)[i // pieces]
+        at = pl.ds((i % pieces) * step, step)
+        to = o_ref.at[at, pl.ds(part * width, width)]
+        ins.append(pltpu.make_async_copy(x_ref.at[at], buf.at[i], sem_in.at[i]))
+        outs.append(pltpu.make_async_copy(buf.at[i], to, sem_out.at[i]))
+    for copy in ins:
+        copy.start()
+    for before, after in zip(ins, outs):
+        before.wait()
+        after.start()
+    for copy in outs:
+        copy.wait()
+
+
+def side(keys, values):
+    rows, width = keys.shape
+    pieces = 2
+    return pl.pallas_call(
+        functools.partial(side_kernel, pieces),
+        out_shape=jax.ShapeDtypeStruct((rows, 2 * width), keys.dtype),
+        in_specs=[pl.BlockSpec(memory_space=pl.ANY)] * 2,
+        out_specs=pl.BlockSpec(memory_space=pl.ANY),
+        scratch_shapes=[
+            pltpu.VMEM((2 * pieces, rows // pieces, width), keys.dtype),
+            pltpu.SemaphoreType.DMA((2 * pieces,)),
+            pltpu.SemaphoreType.DMA((2 * pieces,)),
+        ],
+        compiler_params=params(0, 60),
+        name="side",
+    )(keys, values)
+
+
 def find_slots(place_ref, slot_ref):
     for b in range(place_ref.shape[0]):
         slot_ref[place_ref[b]] = b
 
 
-def pick_kernel(place_ref, anc_ref, x_ref, c_ref, s_ref, *refs):
+def pick_kernel(copies, place_ref, anc_ref, x_ref, c_ref, s_ref, *refs):
     *o_refs, slot_ref = refs
     find_slots(place_ref, slot_ref)
     half = x_ref.shape[2] // 2
@@ -61,21 +99,23 @@
         at = slot_ref[jnp.maximum(anc_ref[place_ref[d]], 0)]
         c, s = c_ref[at], s_ref[at]
         a = 0
-        for o_ref in o_refs:
+        for o_ref, times in zip(o_refs, copies):
             for b in range(0, o_ref.shape[2], 2 * HEAD_SIZE):
                 x = x_ref[at, :, a : a + HEAD_SIZE].astype(jnp.float32)
-                o_ref[d, :, b : b + HEAD_SIZE] = turn(x, c, s).astype(jnp.bfloat16)
-                o_ref[d, :, b + HEAD_SIZE : b + 2 * HEAD_SIZE] = x_ref[
-                    at, :, half + a : half + a + HEAD_SIZE
-                ]
+                k = turn(x, c, s).astype(jnp.bfloat16)
+                v = x_ref[at, :, half + a : half + a + HEAD_SIZE]
+                for n in range(d * times, (d + 1) * times):
+                    o_ref[n, :, b : b + HEAD_SIZE] = k
+                    o_ref[n, :, b + HEAD_SIZE : b + 2 * HEAD_SIZE] = v
                 a += HEAD_SIZE
 
 
-def pick(sizes, places, ancestors, x, c, s):
-    return pl.pallas_call(
-        pick_kernel,
+def pick(sizes, copies, places, ancestors, x, c, s):
+    return pl.pallas_call(
+        functools.partial(pick_kernel, copies),
         out_shape=[
-            jax.ShapeDtypeStruct(x.shape[:2] + (size * 2 * HEAD_SIZE,), x.dtype) for size in sizes
+            jax.ShapeDtypeStruct((x.shape[0] * n, x.shape[1], size * 2 * HEAD_SIZE), x.dtype)
+            for size, n in zip(sizes, copies)
         ],
         in_specs=[pl.BlockSpec(memory_space=pltpu.SMEM)] * 2
         + [pl.BlockSpec(memory_space=pltpu.VMEM)] * 3,
@@ -205,6 +245,14 @@
     )(q, do, out, lse, c, s, keys, values)
 
 
+def part_of(shape, n):
+    places, hops, piece, _ = shape
+    return pl.BlockSpec(
+        (places, None, piece, 2 * HEAD_SIZE),
+        lambda g, info, *_: (0, lax.rem(info[0] + hops - n, hops), 0, g),
+    )
+
+
 def cross_kernel(group, joint, final, ours, info_ref, place_ref, anc_ref, rq_ref, do_ref, lse_ref, delta_ref, c_ref, s_ref, dq_in_ref, *refs):
     sets = len(joint)
     refs = list(refs)
@@ -236,8 +284,9 @@
                 k_ref[at] = turn(raw, kc_ref[...], ks_ref[...]).astype(jnp.bfloat16)
                 v_ref[at] = values_ref[...]
             else:
-                k_ref[at] = kv_refs[m][0][:, :HEAD_SIZE]
-                v_ref[at] = kv_refs[m][0][:, HEAD_SIZE:]
+                both = kv_refs[m][0][...].reshape(rows, 2 * HEAD_SIZE)
+                k_ref[at] = both[:, :HEAD_SIZE]
+                v_ref[at] = both[:, HEAD_SIZE:]
         k = k_ref[here]
         for h in range(group):
             lanes = slice(h * rows, (h + 1) * rows)
@@ -295,14 +344,14 @@
     table = pl.BlockSpec((rows, HEAD_SIZE), lambda g, *_: (0, 0))
     pair = pl.BlockSpec((rows, 2 * HEAD_SIZE), lambda g, *_: (0, g))
     args = [*tree, rq, do, lse, delta, c, s, dq]
-    args += [x for x in kvs] if not ours else [y for x, kc, ks in kvs for y in (x, x, kc, ks)]
+    args += [x for x, _ in kvs] if not ours else [y for x, kc, ks in kvs for y in (x, x, kc, ks)]
     in_specs = [big, big, row, row, table, table, big]
     if ours:
         keys_at = pl.BlockSpec((rows, HEAD_SIZE), lambda g, *_: (0, g + first))
         values_at = pl.BlockSpec((rows, HEAD_SIZE), lambda g, *_: (0, g + first + kv_count))
         in_specs += [keys_at, values_at, table, table] * len(kvs)
     else:
-        in_specs += [pair] * len(kvs)
+        in_specs += [pair if n is None else part_of(x.shape, n) for x, n in kvs]
     mode = 0
     aliases = {}
     if final:
@@ -422,7 +471,7 @@
         route = [(i, (i + n) % hops) for i in range(hops) if wrap or 0 <= i + n < hops]
         return lax.ppermute(x, "head", route)
 
-    raw = jnp.concatenate([unrotated_keys, value_rows], 1)
+    raw = side(unrotated_keys, value_rows)
 
     piece_rows = rows // places
     offset = me * rows + here * piece_rows + jnp.arange(piece_rows, dtype=jnp.int32)
@@ -436,18 +485,28 @@
     rq, delta, dq, local = diagonal(
         queries, output_gradient, outputs, saved_logsumexp, c, s, unrotated_keys, value_rows
     )
-    picked = pick(sizes, placement, parents, middle, middle_c, middle_s)
+    copies = [hops if hops == 2 and g else 1 for g in chunks]
+    picked = pick(sizes, copies, placement, parents, middle, middle_c, middle_s)
     near = []
     for g in chunks:
         send = picked[g]
         if g:
             send, near[-1] = lax.optimization_barrier((send, near[-1]))
-        near.append(exchange(send))
-    near = [x.reshape(rows, -1) for x in near]
+        if copies[g] == 1:
+            near.append(exchange(send))
+        else:
+            near.append(lax.all_to_all(send, ("ctx", "head"), 0, 0, tiled=True))
 
     far = []
     for g in chunks:
-        far.append([shift(near[g], n, True) for n in range(1, hops)])
+        if copies[g] == 1:
+            at_hand = near[g].reshape(rows, -1)
+            far.append([(shift(at_hand, n, True), None) for n in range(1, hops)])
+            near[g] = (at_hand, None)
+        else:
+            both = near[g].reshape(places, hops, piece_rows, -1)
+            far.append([(both, n) for n in range(1, hops)])
+            near[g] = (both, 0)
 
     def tiles(g, dq, kvs, ours, joint, whole=None, final=False):
         return cross(

time: 211 us -> 203 us (0.962)
  local copies, waits for them, and re-layouts: 9.81 us -> 5.28 us
  waiting for transfers between devices: 53.3 us -> 49.9 us
    all_to_all x5 -> x4, starting transfers between devices: 29.5 us -> 23.1 us  [exchange(): lax.all_to_all(x.reshape(places, rows // places, width), 'ctx', 0, 0, til...]
    all_to_all x0 -> x1, starting transfers between devices: none -> 4.97 us  [body(): near.append(lax.all_to_all(send, ('ctx', 'head'), 0, 0, tiled=True))]
    ppermute x7 -> x6, waiting for transfers between devices: 38.1 us -> 33.5 us  [shift(): return lax.ppermute(x, 'head', route)]
    unnamed x35 -> x32, local copies, waits for them, and re-layouts: 7.94 us -> 5.28 us
    mul x0 -> x2, other arithmetic: none -> 2.35 us  [rope_tables(): return (jnp.cos(angles), jnp.sin(angles) * sign[None, :])]
    pallas_call x1 -> x2, Pallas kernels: 1.85 us -> 4.06 us  [the longest x1 2.07 us: pick(): pl.pallas_call(functools.partial(pick_kernel, copies), out_shape=[jax.Sha...]
    all_to_all x5 -> x4, waiting for transfers between devices: 15.2 us -> 16.4 us  [exchange(): lax.all_to_all(x.reshape(places, rows // places, width), 'ctx', 0, 0, til...]
    ppermute x7 -> x6, starting transfers between devices: 13.9 us -> 15 us  [shift(): return lax.ppermute(x, 'head', route)]
  transfers between devices with their start and end apart: 12 -> 11, of which waited for: 6 -> 5; matrix products, arithmetic and copies ran while one was open for 3% -> 3% of each run, Pallas kernels for 35% -> 36%
where the time goes in v5:
time: 203 us; the launch traced here: 202 us
  Pallas kernels  78.6 us (39%)
  waiting for transfers between devices  49.9 us (25%)
  starting transfers between devices  43.1 us (21%)
  blocking collectives  18.9 us (9%)
  local copies, waits for them, and re-layouts  5.28 us (3%)
  other arithmetic  5.24 us (3%)
    pallas_call x6, Pallas kernels, cross(): pl.pallas_call(functools.partial(cross_kernel, group, joint, mode, ours),...  52 us
    ppermute x6, waiting for transfers between devices, shift(): return lax.ppermute(x, 'head', route)  33.5 us
    all_to_all x4, starting transfers between devices, exchange(): lax.all_to_all(x.reshape(places, rows // places, width), 'ctx', 0, 0, til...  23.1 us
    all_to_all x1, blocking collectives, exchange(): lax.all_to_all(x.reshape(places, rows // places, width), 'ctx', 0, 0, til...  18.9 us
    pallas_call x1, Pallas kernels, diagonal(): pl.pallas_call(functools.partial(diagonal_kernel, group), out_shape=[jax....  18.5 us
    all_to_all x4, waiting for transfers between devices, exchange(): lax.all_to_all(x.reshape(places, rows // places, width), 'ctx', 0, 0, til...  16.4 us
    ppermute x6, starting transfers between devices, shift(): return lax.ppermute(x, 'head', route)  15 us
    unnamed x32, local copies, waits for them, and re-layouts  5.28 us
  transfers between devices with their start and end apart: 11, of which 5 were waited for; matrix products, arithmetic and copies ran while one was open for 3% of the time, Pallas kernels for 36%

profile of v5, /device:TPU:0, one launch (start us, length us, event | category | flops | bytes accessed | tf_op | source)
XLA Modules:
  0.0 201.9 jit_solution(15954772321974760877)
XLA Ops:
  0.7 2.0 side.1
  2.7 7.4 %all-to-all-start = ((bf16[16,16,2048]{2,1,0:T(8,128)(2,1)}), bf16[16,16,2048]{2,1,0:T(8,128)(2,1)S(1)}, u32[]{:S(2)}, u32[]{:S(2)}) async-start(bf16[16,16,2048]{2,1,0:T(8,128)(2,1)} %bitcast.18), calls=%async_computation | async-start | bytes 2097152 | tf_op jit(solution)/shard_map/all_to_all | solution.py:466
  10.1 3.5 %collective-permute-start = (bf16[256,2048]{1,0:T(8,128)(2,1)}, bf16[256,2048]{1,0:T(8,128)(2,1)S(1)}, u32[]{:S(2)}, u32[]{:S(2)}) collective-permute-start(bf16[256,2048]{1,0:T(8,128)(2,1)} %side.1), channel_id=1, source_target_pairs={{0,16},{1,17},{2,18},{3,19},{4,20},{5,21},{6,22},{7,23},{8,24},{9,... | collective-permute-start | bytes 3145736 | tf_op jit(solution)/shard_map/ppermute | solution.py:472
  14.3 1.8 fusion.2
  16.6 16.4 %all-to-all-done.x_ref = bf16[16,16,2048]{2,1,0:T(8,128)(2,1)S(1)} async-done(((bf16[16,16,2048]{2,1,0:T(8,128)(2,1)}), bf16[16,16,2048]{2,1,0:T(8,128)(2,1)S(1)}, u32[]{:S(2)}, u32[]{:S(2)}) %all-to-all-start) | async-done | bytes 1048608 | tf_op jit(solution)/shard_map/all_to_all | solution.py:466
  33.0 2.1 %pick.1 = (bf16[16,16,1024]{2,1,0:T(8,128)(2,1)}, bf16[32,16,1024]{2,1,0:T(8,128)(2,1)}) custom-call(s32[16]{0:T(128)S(1)} %copy-done.5, s32[16]{0:T(128)S(1)} %bitcast.16, bf16[16,16,2048]{2,1,0:T(8,128)(2,1)S(1)} %all-to-all-done.x_ref, f32[16,16,128]{2,1,0:T(8,128)S(1)} %get-tuple-element.52.c_ref, f32[16,16,128]{2,1,0:T(8,128)S(1)} %get-tuple-element.51.s_ref), custom_call_target="tpu_custom_call" | custom-call | tf_op jit(solution)/shard_map/pick/pallas_call | solution.py:114
  35.1 6.8 %all-to-all-start.1 = ((bf16[16,16,1024]{2,1,0:T(8,128)(2,1)}), bf16[16,16,1024]{2,1,0:T(8,128)(2,1)S(1)}, u32[]{:S(2)}, u32[]{:S(2)}) async-start(bf16[16,16,1024]{2,1,0:T(8,128)(2,1)} %get-tuple-element.31), calls=%async_computation.1 | async-start | bytes 1048576 | tf_op jit(solution)/shard_map/all_to_all | solution.py:466
  41.9 18.5 %diagonal.1 = (bf16[256,8192]{1,0:T(8,128)(2,1)}, f32[64,256]{1,0:T(8,128)}, bf16[256,8192]{1,0:T(8,128)(2,1)}, f32[256,2048]{1,0:T(8,128)}) custom-call(bf16[256,8192]{1,0:T(8,128)(2,1)} %q_ref.1, bf16[256,8192]{1,0:T(8,128)(2,1)} %do_ref.13, bf16[256,8192]{1,0:T(8,128)(2,1)} %out_ref.1, f32[64,256]{1,0:T(8,128)} %lse_ref.13, ...), custom_call_target="tpu_custom_call" | custom-call | flops 10737418240 | bytes 25165824 | tf_op jit(solution)/shard_map/diagonal/pallas_call | solution.py:226
  60.4 1.6 collective-permute-start.1
  61.9 5.0 %all-to-all-start.2 = ((bf16[32,16,1024]{2,1,0:T(8,128)(2,1)}), bf16[32,16,1024]{2,1,0:T(8,128)(2,1)S(1)}, u32[]{:S(2)}, u32[]{:S(2)}) async-start(bf16[32,16,1024]{2,1,0:T(8,128)(2,1)} %get-tuple-element.32), calls=%async_computation.2 | async-start | bytes 2097152 | tf_op jit(solution)/shard_map/all_to_all | solution.py:498
  68.0 6.0 %cross.8 = (bf16[256,8192]{1,0:T(8,128)(2,1)}, bf16[256,1024]{1,0:T(8,128)(2,1)}) custom-call(s32[2]{0:T(128)} %pad_add_fusion.info_ref, s32[16]{0:T(128)} %place_ref.15, s32[16]{0:T(128)} %bitcast.10, bf16[256,8192]{1,0:T(8,128)(2,1)} %get-tuple-element.27.rq_ref, bf16[256,8192]{1,0:T(8,128)(2,1)} %do_ref.13, f32[64,256]{1,0:T(8,128)} %lse_ref.13, ...), custom_call_target="tpu_custom_call" | custom-call | flops 5368709120 | bytes 12582912 | tf_op jit(solution)/shard_map/cross/pallas_call | solution.py:369
  74.0 9.7 %cross.9 = (bf16[256,8192]{1,0:T(8,128)(2,1)}, bf16[256,1024]{1,0:T(8,128)(2,1)}) custom-call(s32[2]{0:T(128)} %pad_add_fusion.info_ref, s32[16]{0:T(128)} %place_ref.15, s32[16]{0:T(128)} %bitcast.11, bf16[256,8192]{1,0:T(8,128)(2,1)} %get-tuple-element.27.rq_ref, bf16[256,8192]{1,0:T(8,128)(2,1)} %do_ref.13, f32[64,256]{1,0:T(8,128)} %lse_ref.13, ...), custom_call_target="tpu_custom_call" | custom-call | flops 5368709120 | bytes 12582912 | tf_op jit(solution)/shard_map/cross/pallas_call | solution.py:369
  84.4 10.2 %cross.10 = (bf16[256,8192]{1,0:T(8,128)(2,1)}, bf16[256,1024]{1,0:T(8,128)(2,1)}) custom-call(s32[2]{0:T(128)} %pad_add_fusion.info_ref, s32[16]{0:T(128)} %place_ref.15, s32[16]{0:T(128)} %bitcast.12, bf16[256,8192]{1,0:T(8,128)(2,1)} %get-tuple-element.27.rq_ref, bf16[256,8192]{1,0:T(8,128)(2,1)} %do_ref.13, f32[64,256]{1,0:T(8,128)} %lse_ref.13, ...), custom_call_target="tpu_custom_call" | custom-call | flops 5368709120 | bytes 12582912 | tf_op jit(solution)/shard_map/cross/pallas_call | solution.py:369
  94.7 5.7 %collective-permute-start.5 = (bf16[256,1024]{1,0:T(8,128)(2,1)}, bf16[256,1024]{1,0:T(8,128)(2,1)S(1)}, u32[]{:S(2)}, u32[]{:S(2)}) collective-permute-start(bf16[256,1024]{1,0:T(8,128)(2,1)} %get-tuple-element.46), channel_id=1, source_target_pairs={{0,16},{16,0},{1,17},{17,1},{2,18},{18,2},{3,19},{19,3},{4,20},{20... | collective-permute-start | bytes 1572872 | tf_op jit(solution)/shard_map/ppermute | solution.py:472
  100.3 12.4 %collective-permute-done.5 = bf16[256,1024]{1,0:T(8,128)(2,1)S(1)} collective-permute-done((bf16[256,1024]{1,0:T(8,128)(2,1)}, bf16[256,1024]{1,0:T(8,128)(2,1)S(1)}, u32[]{:S(2)}, u32[]{:S(2)}) %collective-permute-start.5) | collective-permute-done | bytes 524320 | tf_op jit(solution)/shard_map/ppermute | solution.py:472
  113.8 4.7 %all-to-all-start.3 = ((bf16[16,16,1024]{2,1,0:T(8,128)(2,1)}), bf16[16,16,1024]{2,1,0:T(8,128)(2,1)S(1)}, u32[]{:S(2)}, u32[]{:S(2)}) async-start(bf16[16,16,1024]{2,1,0:T(8,128)(2,1)} %bitcast.6), calls=%async_computation.3 | async-start | bytes 1048576 | tf_op jit(solution)/shard_map/all_to_all | solution.py:466
  118.5 9.5 %cross.6 = (bf16[256,8192]{1,0:T(8,128)(2,1)}, bf16[256,1024]{1,0:T(8,128)(2,1)}) custom-call(s32[2]{0:T(128)} %pad_add_fusion.info_ref, s32[16]{0:T(128)} %place_ref.15, s32[16]{0:T(128)} %bitcast.13, bf16[256,8192]{1,0:T(8,128)(2,1)} %get-tuple-element.27.rq_ref, bf16[256,8192]{1,0:T(8,128)(2,1)} %do_ref.13, f32[64,256]{1,0:T(8,128)} %lse_ref.13, ...), custom_call_target="tpu_custom_call" | custom-call | flops 5368709120 | bytes 12582912 | tf_op jit(solution)/shard_map/cross/pallas_call | solution.py:369
  128.1 1.8 collective-permute-start.4
  129.9 9.7 %cross.7 = (bf16[256,8192]{1,0:T(8,128)(2,1)}, bf16[256,1024]{1,0:T(8,128)(2,1)}) custom-call(s32[2]{0:T(128)} %pad_add_fusion.info_ref, s32[16]{0:T(128)} %place_ref.15, s32[16]{0:T(128)} %bitcast.14, bf16[256,8192]{1,0:T(8,128)(2,1)} %get-tuple-element.27.rq_ref, bf16[256,8192]{1,0:T(8,128)(2,1)} %do_ref.13, f32[64,256]{1,0:T(8,128)} %lse_ref.13, ...), custom_call_target="tpu_custom_call" | custom-call | flops 5368709120 | bytes 12582912 | tf_op jit(solution)/shard_map/cross/pallas_call | solution.py:369
  139.6 3.0 %collective-permute-done.4 = bf16[256,1024]{1,0:T(8,128)(2,1)S(1)} collective-permute-done((bf16[256,1024]{1,0:T(8,128)(2,1)}, bf16[256,1024]{1,0:T(8,128)(2,1)S(1)}, u32[]{:S(2)}, u32[]{:S(2)}) %collective-permute-start.4) | collective-permute-done | bytes 524320 | tf_op jit(solution)/shard_map/ppermute | solution.py:472
  142.6 1.2 add_convert_fusion.1
  143.8 18.9 %all_to_all.30.refs_1_ = bf16[16,16,1024]{2,1,0:T(8,128)(2,1)S(1)} all-to-all(bf16[16,16,1024]{2,1,0:T(8,128)(2,1)S(1)} %bitcast.19), channel_id=1, replica_groups=mesh['head'=2,'ctx'=16] {'ctx'}, dimensions={0} | all-to-all | bytes 1048576 | tf_op jit(solution)/shard_map/all_to_all | solution.py:466
  162.7 2.4 %merge.1 = bf16[16,16,2048]{2,1,0:T(8,128)(2,1)} custom-call(s32[16]{0:T(128)S(1)} %copy-done.6, s32[16]{0:T(128)S(1)} %bitcast.17, f32[16,16,128]{2,1,0:T(8,128)S(1)} %get-tuple-element.52.c_ref, f32[16,16,128]{2,1,0:T(8,128)S(1)} %get-tuple-element.51.s_ref, bf16[16,16,1024]{2,1,0:T(8,128)(2,1)S(1)} %all-to-all-done.3.refs_0_, ...), custom_call_target="tpu_custom_call" | custom-call | tf_op jit(solution)/shard_map/merge/pallas_call | solution.py:155
  165.1 4.2 %all-to-all-start.5 = ((bf16[16,16,2048]{2,1,0:T(8,128)(2,1)}), bf16[16,16,2048]{2,1,0:T(8,128)(2,1)S(1)}, u32[]{:S(2)}, u32[]{:S(2)}) async-start(bf16[16,16,2048]{2,1,0:T(8,128)(2,1)} %merge.1), calls=%async_computation.5 | async-start | bytes 2097152 | tf_op jit(solution)/shard_map/all_to_all | solution.py:466
  169.3 1.3 collective-permute-start.2
  170.6 6.8 %cross.11 = (bf16[256,8192]{1,0:T(8,128)(2,1)}, bf16[256,1024]{1,0:T(8,128)(2,1)}) custom-call(s32[2]{0:T(128)} %pad_add_fusion.info_ref, s32[16]{0:T(128)} %place_ref.15, s32[16]{0:T(128)} %bitcast.15, bf16[256,8192]{1,0:T(8,128)(2,1)} %get-tuple-element.27.rq_ref, bf16[256,8192]{1,0:T(8,128)(2,1)} %do_ref.13, ...), custom_call_target="tpu_custom_call", output_to_operand_aliasing={{0}: (14, {})} | custom-call | flops 5368709120 | bytes 12582912 | tf_op jit(solution)/shard_map/cross/pallas_call | solution.py:369
  177.4 1.3 collective-permute-start.3
  178.7 6.7 %collective-permute-done.2.refs_0_ = bf16[256,1024]{1,0:T(8,128)(2,1)S(1)} collective-permute-done((bf16[256,1024]{1,0:T(8,128)(2,1)S(1)}, bf16[256,1024]{1,0:T(8,128)(2,1)S(1)}, u32[]{:S(2)}, u32[]{:S(2)}) %collective-permute-start.2) | collective-permute-done | bytes 524320 | tf_op jit(solution)/shard_map/ppermute | solution.py:472
  186.2 11.4 %collective-permute-done.3.refs_1_ = bf16[256,1024]{1,0:T(8,128)(2,1)S(1)} collective-permute-done((bf16[256,1024]{1,0:T(8,128)(2,1)}, bf16[256,1024]{1,0:T(8,128)(2,1)S(1)}, u32[]{:S(2)}, u32[]{:S(2)}) %collective-permute-start.3) | collective-permute-done | bytes 524320 | tf_op jit(solution)/shard_map/ppermute | solution.py:472
  197.6 1.6 copy-done
  199.2 1.0 copy-done.4
  200.7 1.3 finish.1
  (45 shorter events, 5.3 us)
Async XLA Ops:
  0.6 13.0 %copy-start.5 = (s32[16]{0:T(128)S(1)}, s32[16]{0:T(128)}, u32[]{:S(2)}) copy-start(s32[16]{0:T(128)} %place_ref.15) | copy-start | bytes 196
  0.6 13.0 %copy-start.12 = (s32[256]{0:T(256)S(1)}, s32[256]{0:T(256)}, u32[]{:S(2)}) copy-start(s32[256]{0:T(256)} %param.17) | copy-start | bytes 3076
  0.7 32.3 %copy-start.7 = (s32[16,1]{0,1:T(1,128)S(1)}, s32[16,1]{0,1:T(1,128)}, u32[]{:S(2)}) copy-start(s32[16,1]{0,1:T(1,128)} %param.15) | copy-start | bytes 196
  2.7 30.3 %all-to-all-start = ((bf16[16,16,2048]{2,1,0:T(8,128)(2,1)}), bf16[16,16,2048]{2,1,0:T(8,128)(2,1)S(1)}, u32[]{:S(2)}, u32[]{:S(2)}) async-start(bf16[16,16,2048]{2,1,0:T(8,128)(2,1)} %bitcast.18), calls=%async_computation | async-start | bytes 2097152 | tf_op jit(solution)/shard_map/all_to_all | solution.py:466
  10.1 56.8 %collective-permute-start = (bf16[256,2048]{1,0:T(8,128)(2,1)}, bf16[256,2048]{1,0:T(8,128)(2,1)S(1)}, u32[]{:S(2)}, u32[]{:S(2)}) collective-permute-start(bf16[256,2048]{1,0:T(8,128)(2,1)} %side.1), channel_id=1, source_target_pairs={{0,16},{1,17},{2,18},{3,19},{4,20},{5,21},{6,22},{7,23},{8,24},{9,... | collective-permute-start | bytes 3145736 | tf_op jit(solution)/shard_map/ppermute | solution.py:472
  35.1 25.3 %all-to-all-start.1 = ((bf16[16,16,1024]{2,1,0:T(8,128)(2,1)}), bf16[16,16,1024]{2,1,0:T(8,128)(2,1)S(1)}, u32[]{:S(2)}, u32[]{:S(2)}) async-start(bf16[16,16,1024]{2,1,0:T(8,128)(2,1)} %get-tuple-element.31), calls=%async_computation.1 | async-start | bytes 1048576 | tf_op jit(solution)/shard_map/all_to_all | solution.py:466
  60.4 13.6 %copy-start.11 = (bf16[16,16,1024]{2,1,0:T(8,128)(2,1)}, bf16[16,16,1024]{2,1,0:T(8,128)(2,1)S(1)}, u32[]{:S(2)}) copy-start(bf16[16,16,1024]{2,1,0:T(8,128)(2,1)S(1)} %all-to-all-done.1) | copy-start | bytes 1572868
  60.4 23.3 %collective-permute-start.1 = (bf16[256,1024]{1,0:T(8,128)(2,1)S(1)}, bf16[256,1024]{1,0:T(8,128)(2,1)S(1)}, u32[]{:S(2)}, u32[]{:S(2)}) collective-permute-start(bf16[256,1024]{1,0:T(8,128)(2,1)S(1)} %bitcast.22), channel_id=1, source_target_pairs={{0,16},{16,0},{1,17},{17,1},{2,18},{18,2},{3,19},{19,3},{4,20},{20... | collective-permute-start | bytes 1572872 | tf_op jit(solution)/shard_map/ppermute | solution.py:472
  61.9 51.8 %all-to-all-start.2 = ((bf16[32,16,1024]{2,1,0:T(8,128)(2,1)}), bf16[32,16,1024]{2,1,0:T(8,128)(2,1)S(1)}, u32[]{:S(2)}, u32[]{:S(2)}) async-start(bf16[32,16,1024]{2,1,0:T(8,128)(2,1)} %get-tuple-element.32), calls=%async_computation.2 | async-start | bytes 2097152 | tf_op jit(solution)/shard_map/all_to_all | solution.py:498
  66.9 1.0 copy-start.13
  83.7 0.8 copy-start.15
  84.4 28.3 %copy-start.10 = (bf16[256,1024]{1,0:T(8,128)(2,1)S(1)}, bf16[256,1024]{1,0:T(8,128)(2,1)}, u32[]{:S(2)}) copy-start(bf16[256,1024]{1,0:T(8,128)(2,1)} %get-tuple-element.45) | copy-start | bytes 1572868
  94.7 18.1 %collective-permute-start.5 = (bf16[256,1024]{1,0:T(8,128)(2,1)}, bf16[256,1024]{1,0:T(8,128)(2,1)S(1)}, u32[]{:S(2)}, u32[]{:S(2)}) collective-permute-start(bf16[256,1024]{1,0:T(8,128)(2,1)} %get-tuple-element.46), channel_id=1, source_target_pairs={{0,16},{16,0},{1,17},{17,1},{2,18},{18,2},{3,19},{19,3},{4,20},{20... | collective-permute-start | bytes 1572872 | tf_op jit(solution)/shard_map/ppermute | solution.py:472
  113.8 4.7 %copy-start.9 = (bf16[32,16,1024]{2,1,0:T(8,128)(2,1)}, bf16[32,16,1024]{2,1,0:T(8,128)(2,1)S(1)}, u32[]{:S(2)}) copy-start(bf16[32,16,1024]{2,1,0:T(8,128)(2,1)S(1)} %all-to-all-done.2) | copy-start | bytes 3145732
  113.8 30.0 %all-to-all-start.3 = ((bf16[16,16,1024]{2,1,0:T(8,128)(2,1)}), bf16[16,16,1024]{2,1,0:T(8,128)(2,1)S(1)}, u32[]{:S(2)}, u32[]{:S(2)}) async-start(bf16[16,16,1024]{2,1,0:T(8,128)(2,1)} %bitcast.6), calls=%async_computation.3 | async-start | bytes 1048576 | tf_op jit(solution)/shard_map/all_to_all | solution.py:466
  128.1 14.5 %collective-permute-start.4 = (bf16[256,1024]{1,0:T(8,128)(2,1)}, bf16[256,1024]{1,0:T(8,128)(2,1)S(1)}, u32[]{:S(2)}, u32[]{:S(2)}) collective-permute-start(bf16[256,1024]{1,0:T(8,128)(2,1)} %get-tuple-element.44), channel_id=1, source_target_pairs={{0,16},{16,0},{1,17},{17,1},{2,18},{18,2},{3,19},{19,3},{4,20},{20... | collective-permute-start | bytes 1572872 | tf_op jit(solution)/shard_map/ppermute | solution.py:472
  129.9 32.8 %copy-start.6 = (s32[16]{0:T(128)S(1)}, s32[16]{0:T(128)}, u32[]{:S(2)}) copy-start(s32[16]{0:T(128)} %place_ref.15) | copy-start | bytes 196
  129.9 32.8 %copy-start.8 = (s32[16,1]{0,1:T(1,128)S(1)}, s32[16,1]{0,1:T(1,128)}, u32[]{:S(2)}) copy-start(s32[16,1]{0,1:T(1,128)} %param.15) | copy-start | bytes 196
  139.6 29.7 %copy-start.14 = (bf16[256,1024]{1,0:T(8,128)(2,1)S(1)}, bf16[256,1024]{1,0:T(8,128)(2,1)}, u32[]{:S(2)}) copy-start(bf16[256,1024]{1,0:T(8,128)(2,1)} %get-tuple-element.41) | copy-start | bytes 1572868
  165.1 35.5 %all-to-all-start.5 = ((bf16[16,16,2048]{2,1,0:T(8,128)(2,1)}), bf16[16,16,2048]{2,1,0:T(8,128)(2,1)S(1)}, u32[]{:S(2)}, u32[]{:S(2)}) async-start(bf16[16,16,2048]{2,1,0:T(8,128)(2,1)} %merge.1), calls=%async_computation.5 | async-start | bytes 2097152 | tf_op jit(solution)/shard_map/all_to_all | solution.py:466
  169.3 16.1 %collective-permute-start.2 = (bf16[256,1024]{1,0:T(8,128)(2,1)S(1)}, bf16[256,1024]{1,0:T(8,128)(2,1)S(1)}, u32[]{:S(2)}, u32[]{:S(2)}) collective-permute-start(bf16[256,1024]{1,0:T(8,128)(2,1)S(1)} %copy-done.14), channel_id=1, source_target_pairs={{16,0},{17,1},{18,2},{19,3},{20,4},{21,5},{22,6},{23,7},{24,8},{25... | collective-permute-start | bytes 1572872 | tf_op jit(solution)/shard_map/ppermute | solution.py:472
  170.6 27.0 %copy-start.1 = (f32[256,128]{1,0:T(8,128)S(1)}, f32[256,128]{1,0:T(8,128)}, u32[]{:S(2)}) copy-start(f32[256,128]{1,0:T(8,128)} %get-tuple-element.57.c_ref) | copy-start | bytes 393220
  170.6 27.0 %copy-start.2 = (f32[256,128]{1,0:T(8,128)S(1)}, f32[256,128]{1,0:T(8,128)}, u32[]{:S(2)}) copy-start(f32[256,128]{1,0:T(8,128)} %get-tuple-element.58.s_ref) | copy-start | bytes 393220
  177.4 20.2 %collective-permute-start.3 = (bf16[256,1024]{1,0:T(8,128)(2,1)}, bf16[256,1024]{1,0:T(8,128)(2,1)S(1)}, u32[]{:S(2)}, u32[]{:S(2)}) collective-permute-start(bf16[256,1024]{1,0:T(8,128)(2,1)} %get-tuple-element.42), channel_id=1, source_target_pairs={{16,0},{17,1},{18,2},{19,3},{20,4},{21,5},{22,6},{23,7},{24,8},{25... | collective-permute-start | bytes 1572872 | tf_op jit(solution)/shard_map/ppermute | solution.py:472
  185.4 0.8 copy-start.3
  197.6 1.6 copy-start
  199.2 1.0 copy-start.4
